TPU v7x, 512 devices: a whole 4x4x16 slice. The times are simulated.
512 devices in a mesh: section: 8 (over z_hi, x), expert: 64 (over z_lo, y, core).
Axes of the slice: x: 4, y: 4, z: 16 (z_hi: 2, z_lo: 8; z = z_hi * 8 + z_lo), core: 2. Of those that a mesh axis runs over, the one named last changes fastest.
Arguments:
- inputs: bfloat16 [4, 2048, 1536], P(None, 'expert', 'section'), may hold values from -36 to 36
- cotangent: bfloat16 [4, 2048, 1536], P(None, 'expert', 'section'), may hold values from -1.25 to 1.25
- expert_out: bfloat16 [8, 4, 128, 64, 2, 1536], P('section', None, 'expert'), may hold values from -6 to 6
- route_ids: int32 [8, 4, 2048, 4], P('section', None, 'expert'), may hold values from 0 to 127, all different within a row; in each aligned block of 32 rows (0 to 31, 32 to 63, ..., all dimensions but the last counted through in order) at most 2 rows name the same one
- router_w: bfloat16 [8, 1536, 128], P('section'), may hold values from -0.15625 to 0.15625
- norm_gain: float32 [8, 1536], P('section'), may hold values from 0.1 to 1.9
- final_gain: float32 [1536], replicated, may hold values from 0.1 to 1.9
Outputs:
- router_grad: float32 [8, 1536, 128], P('section', 'expert')
- gain_grad: float32 [8, 1536], P('section', 'expert')
Inputs may be any that keep to these rules, and one draw needn't show every extreme that they name: `route_ids`: no expert is named by more than 2 of the 32 tokens that one device of the expert axis holds, in one layer and microbatch; some expert reaches it.
All inputs are finite; a program needn't handle non-finite values.
Results may differ from a plain program's by a relative error of at most 0.012.
Values may be sent and summed in bfloat16 or wider, within the bound.
No kernel may reach another device: no remote copies, remote signals or barrier semaphores. Data moves between devices by JAX's collectives and lax.ppermute only.
A program may use at most 64 MiB of HBM per device.

v0:
```python
import jax
import jax.numpy as jnp
from jax import lax
from jax.sharding import PartitionSpec as P

EPSILON = 1e-05


def shifted(value, axis, steps):
    count = lax.axis_size(axis)
    pairs = [(source, (source + steps) % count) for source in range(count)]
    return lax.ppermute(value, axis, pairs)


def rms_scale(values):
    return lax.rsqrt(jnp.mean(values * values, axis=-1, keepdims=True) + EPSILON)


def slot_numbers(route_block):
    flattened = route_block.reshape(route_block.shape[0], -1)
    pair_count = flattened.shape[1]
    matches = flattened[:, :, None] == flattened[:, None, :]
    earlier = lax.broadcasted_iota(jnp.int32, (pair_count, pair_count), 1) < lax.broadcasted_iota(
        jnp.int32, (pair_count, pair_count), 0
    )
    return jnp.sum(jnp.where(matches & earlier[None], 1, 0), axis=-1).astype(jnp.int32)


def route_weights(normed, router_weight, route_rows):
    logits = jnp.dot(normed, router_weight, preferred_element_type=jnp.float32)
    onehot = (
        route_rows[:, :, None] == lax.broadcasted_iota(jnp.int32, (1, 1, logits.shape[-1]), 2)
    ).astype(jnp.float32)
    chosen = jnp.sum(onehot * logits[:, None, :], axis=-1)
    raised = jnp.exp(chosen)
    return (raised / jnp.sum(raised, axis=-1, keepdims=True), onehot)


def layer_forward(state_rows, picked_rows, route_rows, router_weight, gain_row):
    state_float = state_rows.astype(jnp.float32)
    rscale = rms_scale(state_float)
    normed = (state_float * rscale * gain_row).astype(jnp.bfloat16)
    weights, onehot = route_weights(normed, router_weight, route_rows)
    mixture = jnp.sum(weights[:, :, None] * picked_rows.astype(jnp.float32), axis=1)
    return (state_float + mixture).astype(jnp.bfloat16)


def layer_backward(back_rows, state_rows, picked_rows, route_rows, router_weight, gain_row):
    state_float = state_rows.astype(jnp.float32)
    rscale = rms_scale(state_float)
    normal_part = state_float * rscale
    normed = (normal_part * gain_row).astype(jnp.bfloat16)
    weights, onehot = route_weights(normed, router_weight, route_rows)
    back_float = back_rows.astype(jnp.float32)
    dweights = jnp.sum(back_float[:, None, :] * picked_rows.astype(jnp.float32), axis=-1)
    dselect = weights * (dweights - jnp.sum(weights * dweights, axis=-1, keepdims=True))
    dlogits = jnp.sum(dselect[:, :, None] * onehot, axis=1).astype(jnp.bfloat16)
    router_term = lax.dot_general(
        normed, dlogits, (((0,), (0,)), ((), ())), preferred_element_type=jnp.float32
    )
    dnormed = lax.dot_general(
        dlogits, router_weight, (((1,), (1,)), ((), ())), preferred_element_type=jnp.float32
    )
    gain_term = jnp.sum(dnormed * normal_part, axis=0)
    varied = dnormed * gain_row
    new_back = back_float + rscale * (
        varied - normal_part * jnp.mean(varied * normal_part, axis=-1, keepdims=True)
    )
    return (new_back.astype(jnp.bfloat16), router_term, gain_term)


def final_back(last_states, cot_rows, final_gain):
    state_float = last_states.astype(jnp.float32)
    rscale = rms_scale(state_float)
    normal_part = state_float * rscale
    varied = cot_rows.astype(jnp.float32) * final_gain
    return (
        rscale * (varied - normal_part * jnp.mean(varied * normal_part, axis=-1, keepdims=True))
    ).astype(jnp.bfloat16)


def per_device(inputs, cotangent, expert_out, route_ids, router_w, norm_gain, final_gain):
    section_count = lax.axis_size("section")
    section_pos = lax.axis_index("section")
    micro_count = inputs.shape[0]
    tok_rows = inputs.shape[1]
    step_count = micro_count + section_count - 1
    full_inputs, full_cot = (
        lax.all_gather(inputs, "section", axis=2, tiled=True),
        lax.all_gather(cotangent, "section", axis=2, tiled=True),
    )
    width = full_inputs.shape[2]
    routes = route_ids[0]
    choice_count = routes.shape[2]
    capacity = expert_out.shape[4]
    router_weight = router_w[0]
    gain_row = norm_gain[0]
    row_index = routes.reshape(micro_count, -1) * capacity + slot_numbers(routes)
    picked_store = jnp.zeros((micro_count, tok_rows, choice_count, width), jnp.bfloat16)
    returned = lax.all_to_all(expert_out, "expert", split_axis=3, concat_axis=2, tiled=True)
    row_table = returned.reshape(micro_count, -1, width)
    picked_store = jax.vmap(
        lambda block_table, block_rows: jnp.take(block_table, block_rows, axis=0)
    )(row_table, row_index)
    picked_store = picked_store.reshape(micro_count, tok_rows, choice_count, width)

    def forward_step(step_at, carry):
        received, stashed, finals, picked_all = carry
        micro_at = step_at - section_pos
        is_valid = (micro_at >= 0) & (micro_at < micro_count)
        micro_clip = jnp.clip(micro_at, 0, micro_count - 1)
        inject = lax.dynamic_index_in_dim(
            full_inputs, jnp.minimum(step_at, micro_count - 1), 0, keepdims=False
        )
        current = jnp.where(section_pos == 0, inject, received)
        picked_now = lax.dynamic_index_in_dim(picked_all, micro_clip, 0, keepdims=False)
        routes_now = lax.dynamic_index_in_dim(routes, micro_clip, 0, keepdims=False)
        output = layer_forward(current, picked_now, routes_now, router_weight, gain_row)
        stashed = jnp.where(
            is_valid, lax.dynamic_update_index_in_dim(stashed, current, micro_clip, 0), stashed
        )
        arriving = shifted(output, "section", 1)
        final_at = step_at - (section_count - 1)
        keep_final = (section_pos == 0) & (final_at >= 0)
        final_clip = jnp.clip(final_at, 0, micro_count - 1)
        finals = jnp.where(
            keep_final, lax.dynamic_update_index_in_dim(finals, arriving, final_clip, 0), finals
        )
        return (arriving, stashed, finals, picked_all)

    empty_rows = jnp.zeros((tok_rows, width), jnp.bfloat16)
    empty_micro = jnp.zeros((micro_count, tok_rows, width), jnp.bfloat16)
    received, stashed, finals, picked_store = lax.fori_loop(
        0, step_count, forward_step, (empty_rows, empty_micro, empty_micro, picked_store)
    )
    back_top = final_back(finals, full_cot, final_gain)

    def backward_step(step_at, carry):
        pending, router_sum, gain_sum = carry
        micro_at = step_at - (section_count - 1 - section_pos)
        is_valid = (micro_at >= 0) & (micro_at < micro_count)
        micro_clip = jnp.clip(micro_at, 0, micro_count - 1)
        top_now = lax.dynamic_index_in_dim(
            back_top, jnp.minimum(step_at, micro_count - 1), 0, keepdims=False
        )
        sending = jnp.where(section_pos == 0, top_now, pending)
        current = shifted(sending, "section", -1)
        state_now = lax.dynamic_index_in_dim(stashed, micro_clip, 0, keepdims=False)
        picked_now = lax.dynamic_index_in_dim(picked_store, micro_clip, 0, keepdims=False)
        routes_now = lax.dynamic_index_in_dim(routes, micro_clip, 0, keepdims=False)
        new_back, router_term, gain_term = layer_backward(
            current, state_now, picked_now, routes_now, router_weight, gain_row
        )
        router_sum = router_sum + jnp.where(is_valid, router_term, 0.0)
        gain_sum = gain_sum + jnp.where(is_valid, gain_term, 0.0)
        pending = new_back
        return (pending, router_sum, gain_sum)

    router_start = jnp.zeros((width, router_weight.shape[1]), jnp.float32)
    gain_start = jnp.zeros((width,), jnp.float32)
    pending, router_sum, gain_sum = lax.fori_loop(
        0, step_count, backward_step, (empty_rows, router_start, gain_start)
    )
    router_part, gain_part = (
        lax.psum_scatter(router_sum, "expert", scatter_dimension=0, tiled=True),
        lax.psum_scatter(gain_sum, "expert", scatter_dimension=0, tiled=True),
    )
    return (router_part[None], gain_part[None])


def solution(mesh):
    placed = (
        P(None, "expert", "section"),
        P(None, "expert", "section"),
        P("section", None, "expert", None, None, None),
        P("section", None, "expert", None),
        P("section", None, None),
        P("section", None),
        P(),
    )
    return jax.shard_map(
        per_device,
        mesh=mesh,
        in_specs=placed,
        out_specs=(P("section", "expert", None), P("section", "expert")),
        check_vma=False,
    )
```

profile of v0, /device:TPU:6, one launch (start us, length us, event | category | flops | bytes accessed | tf_op | source)
XLA Modules:
  0.0 1308.6 jit_solution(3175136076809237665)
XLA Ops:
  7.2 7.0 copy.70
  14.2 16.3 %all-to-all-start = ((bf16[1,4,2,64,2,1536]{5,4,2,1,0,3:T(2,128)(2,1)}), bf16[1,4,2,64,2,1536]{5,4,2,1,0,3:T(2,128)(2,1)S(1)}, u32[]{:S(2)}, u32[]{:S(2)}) async-start(bf16[1,4,2,64,2,1536]{5,4,2,1,0,3:T(2,128)(2,1)} %copy.70), calls=%async_computation | async-start | bytes 6291456 | tf_op jit(solution)/shard_map/all_to_all | solution.py:100
  32.7 132.7 %all_gather.6 = bf16[4,32,1536]{1,0,2:T(4,128)(2,1)} all-gather(bf16[4,32,192]{1,0,2:T(4,128)(2,1)S(1)} %copy.66), channel_id=1, replica_groups=mesh['section'=8,'expert'=64] {'section'}, dimensions={2}, use_global_device_ids=true | all-gather | bytes 442368 | tf_op jit(solution)/shard_map/all_gather | solution.py:89
  165.4 3.3 copy.73
  169.7 70.5 %all_gather.7 = bf16[4,32,1536]{1,0,2:T(4,128)(2,1)} all-gather(bf16[4,32,192]{1,0,2:T(4,128)(2,1)S(1)} %copy.75), channel_id=1, replica_groups=mesh['section'=8,'expert'=64] {'section'}, dimensions={2}, use_global_device_ids=true | all-gather | bytes 442368 | tf_op jit(solution)/shard_map/all_gather | solution.py:90
  240.2 9.5 all-to-all-done
  249.7 3.8 copy.71
  253.5 6.3 reshape.178
  259.8 9.7 gather_fusion
  269.5 2.9 gather.7
  272.5 2.0 broadcast_select_fusion
  274.5 231.2 %while.39 = (s32[]{:T(128)}, bf16[32,1536]{1,0:T(8,128)(2,1)S(1)}, bf16[4,32,1536]{2,1,0:T(8,128)(2,1)S(1)}, bf16[4,32,1536]{2,1,0:T(8,128)(2,1)S(1)}, pred[]{:T...) while((s32[]{:T(128)}, bf16[32,1536]{1,0:T(8,128)(2,1)S(1)}, ...), condition=%wide.region_6.7_spmd, body=%wide.region_1.6_spmd.sunk | while | flops 13811857 | bytes 2809975 | solution.py:133
  276.2 1.6 fusion.74
  277.9 8.1 collective-permute-start
  286.0 8.8 collective-permute-done
  298.2 15.2 %collective-permute-start = (bf16[32,1536]{1,0:T(8,128)(2,1)S(1)}, bf16[32,1536]{1,0:T(8,128)(2,1)S(1)}, u32[]{:S(2)}, u32[]{:S(2)}) collective-permute-start(bf16[32,1536]{1,0:T(8,128)(2,1)S(1)} %fusion.75), channel_id=1, source_target_pairs={{0,64},{64,128},{128,192},{192,256},{256,320},{320,384},{384,448},... | collective-permute-start | bytes 294920 | tf_op jit(solution)/shard_map/while/body/eval_jaxpr/ppermute | solution.py:12
  313.4 4.2 collective-permute-done
  321.0 15.4 %collective-permute-start = (bf16[32,1536]{1,0:T(8,128)(2,1)S(1)}, bf16[32,1536]{1,0:T(8,128)(2,1)S(1)}, u32[]{:S(2)}, u32[]{:S(2)}) collective-permute-start(bf16[32,1536]{1,0:T(8,128)(2,1)S(1)} %fusion.75), channel_id=1, source_target_pairs={{0,64},{64,128},{128,192},{192,256},{256,320},{320,384},{384,448},... | collective-permute-start | bytes 294920 | tf_op jit(solution)/shard_map/while/body/eval_jaxpr/ppermute | solution.py:12
  336.4 3.7 collective-permute-done
  343.4 15.2 %collective-permute-start = (bf16[32,1536]{1,0:T(8,128)(2,1)S(1)}, bf16[32,1536]{1,0:T(8,128)(2,1)S(1)}, u32[]{:S(2)}, u32[]{:S(2)}) collective-permute-start(bf16[32,1536]{1,0:T(8,128)(2,1)S(1)} %fusion.75), channel_id=1, source_target_pairs={{0,64},{64,128},{128,192},{192,256},{256,320},{320,384},{384,448},... | collective-permute-start | bytes 294920 | tf_op jit(solution)/shard_map/while/body/eval_jaxpr/ppermute | solution.py:12
  358.6 2.2 collective-permute-done
  364.2 15.1 %collective-permute-start = (bf16[32,1536]{1,0:T(8,128)(2,1)S(1)}, bf16[32,1536]{1,0:T(8,128)(2,1)S(1)}, u32[]{:S(2)}, u32[]{:S(2)}) collective-permute-start(bf16[32,1536]{1,0:T(8,128)(2,1)S(1)} %fusion.75), channel_id=1, source_target_pairs={{0,64},{64,128},{128,192},{192,256},{256,320},{320,384},{384,448},... | collective-permute-start | bytes 294920 | tf_op jit(solution)/shard_map/while/body/eval_jaxpr/ppermute | solution.py:12
  379.3 2.2 collective-permute-done
  384.9 15.1 %collective-permute-start = (bf16[32,1536]{1,0:T(8,128)(2,1)S(1)}, bf16[32,1536]{1,0:T(8,128)(2,1)S(1)}, u32[]{:S(2)}, u32[]{:S(2)}) collective-permute-start(bf16[32,1536]{1,0:T(8,128)(2,1)S(1)} %fusion.75), channel_id=1, source_target_pairs={{0,64},{64,128},{128,192},{192,256},{256,320},{320,384},{384,448},... | collective-permute-start | bytes 294920 | tf_op jit(solution)/shard_map/while/body/eval_jaxpr/ppermute | solution.py:12
  400.0 2.2 collective-permute-done
  405.6 15.1 %collective-permute-start = (bf16[32,1536]{1,0:T(8,128)(2,1)S(1)}, bf16[32,1536]{1,0:T(8,128)(2,1)S(1)}, u32[]{:S(2)}, u32[]{:S(2)}) collective-permute-start(bf16[32,1536]{1,0:T(8,128)(2,1)S(1)} %fusion.75), channel_id=1, source_target_pairs={{0,64},{64,128},{128,192},{192,256},{256,320},{320,384},{384,448},... | collective-permute-start | bytes 294920 | tf_op jit(solution)/shard_map/while/body/eval_jaxpr/ppermute | solution.py:12
  420.8 2.2 collective-permute-done
  426.3 15.1 %collective-permute-start = (bf16[32,1536]{1,0:T(8,128)(2,1)S(1)}, bf16[32,1536]{1,0:T(8,128)(2,1)S(1)}, u32[]{:S(2)}, u32[]{:S(2)}) collective-permute-start(bf16[32,1536]{1,0:T(8,128)(2,1)S(1)} %fusion.75), channel_id=1, source_target_pairs={{0,64},{64,128},{128,192},{192,256},{256,320},{320,384},{384,448},... | collective-permute-start | bytes 294920 | tf_op jit(solution)/shard_map/while/body/eval_jaxpr/ppermute | solution.py:12
  441.5 2.2 collective-permute-done
  447.0 15.1 %collective-permute-start = (bf16[32,1536]{1,0:T(8,128)(2,1)S(1)}, bf16[32,1536]{1,0:T(8,128)(2,1)S(1)}, u32[]{:S(2)}, u32[]{:S(2)}) collective-permute-start(bf16[32,1536]{1,0:T(8,128)(2,1)S(1)} %fusion.75), channel_id=1, source_target_pairs={{0,64},{64,128},{128,192},{192,256},{256,320},{320,384},{384,448},... | collective-permute-start | bytes 294920 | tf_op jit(solution)/shard_map/while/body/eval_jaxpr/ppermute | solution.py:12
  462.2 2.2 collective-permute-done
  467.7 15.1 %collective-permute-start = (bf16[32,1536]{1,0:T(8,128)(2,1)S(1)}, bf16[32,1536]{1,0:T(8,128)(2,1)S(1)}, u32[]{:S(2)}, u32[]{:S(2)}) collective-permute-start(bf16[32,1536]{1,0:T(8,128)(2,1)S(1)} %fusion.75), channel_id=1, source_target_pairs={{0,64},{64,128},{128,192},{192,256},{256,320},{320,384},{384,448},... | collective-permute-start | bytes 294920 | tf_op jit(solution)/shard_map/while/body/eval_jaxpr/ppermute | solution.py:12
  482.9 2.2 collective-permute-done
  488.4 15.1 %collective-permute-start = (bf16[32,1536]{1,0:T(8,128)(2,1)S(1)}, bf16[32,1536]{1,0:T(8,128)(2,1)S(1)}, u32[]{:S(2)}, u32[]{:S(2)}) collective-permute-start(bf16[32,1536]{1,0:T(8,128)(2,1)S(1)} %fusion.75), channel_id=1, source_target_pairs={{0,64},{64,128},{128,192},{192,256},{256,320},{320,384},{384,448},... | collective-permute-start | bytes 294920 | tf_op jit(solution)/shard_map/while/body/eval_jaxpr/ppermute | solution.py:12
  503.6 2.2 collective-permute-done
  506.8 1.7 fusion.39
  508.5 5.4 fusion.35
  513.9 5.2 fusion.38
  519.2 2.6 copy.76
  521.7 220.0 %while.40 = (s32[]{:T(128)}, bf16[32,1536]{1,0:T(8,128)(2,1)S(1)}, f32[1536,128]{1,0:T(8,128)S(1)}, f32[1536]{0:T(1024)S(1)}, pred[]{:T(512)}, /*index=5*/bf16[4...) while((s32[]{:T(128)}, bf16[32,1536]{1,0:T(8,128)(2,1)S(1)}, ...), condition=%wide.region_18.19_spmd.clone, body=%wide.region_9.18_spmd.clone.sunk | while | flops 40500840 | bytes 5147231 | solution.py:161
  521.8 1.9 collective-permute-start.1
  524.4 15.1 %collective-permute-done.1 = bf16[32,1536]{1,0:T(8,128)(2,1)S(1)} collective-permute-done((bf16[32,1536]{1,0:T(8,128)(2,1)S(1)}, bf16[32,1536]{1,0:T(8,128)(2,1)S(1)}, u32[]{:S(2)}, u32[]{:S(2)}) %collective-permute-start.1) | collective-permute-done | bytes 98336 | tf_op jit(solution)/shard_map/while/body/eval_jaxpr/ppermute | solution.py:12
  542.0 1.9 collective-permute-start.1
  544.6 14.8 %collective-permute-done.1 = bf16[32,1536]{1,0:T(8,128)(2,1)S(1)} collective-permute-done((bf16[32,1536]{1,0:T(8,128)(2,1)S(1)}, bf16[32,1536]{1,0:T(8,128)(2,1)S(1)}, u32[]{:S(2)}, u32[]{:S(2)}) %collective-permute-start.1) | collective-permute-done | bytes 98336 | tf_op jit(solution)/shard_map/while/body/eval_jaxpr/ppermute | solution.py:12
  561.9 1.9 collective-permute-start.1
  564.5 14.9 %collective-permute-done.1 = bf16[32,1536]{1,0:T(8,128)(2,1)S(1)} collective-permute-done((bf16[32,1536]{1,0:T(8,128)(2,1)S(1)}, bf16[32,1536]{1,0:T(8,128)(2,1)S(1)}, u32[]{:S(2)}, u32[]{:S(2)}) %collective-permute-start.1) | collective-permute-done | bytes 98336 | tf_op jit(solution)/shard_map/while/body/eval_jaxpr/ppermute | solution.py:12
  581.9 1.9 collective-permute-start.1
  584.4 14.9 %collective-permute-done.1 = bf16[32,1536]{1,0:T(8,128)(2,1)S(1)} collective-permute-done((bf16[32,1536]{1,0:T(8,128)(2,1)S(1)}, bf16[32,1536]{1,0:T(8,128)(2,1)S(1)}, u32[]{:S(2)}, u32[]{:S(2)}) %collective-permute-start.1) | collective-permute-done | bytes 98336 | tf_op jit(solution)/shard_map/while/body/eval_jaxpr/ppermute | solution.py:12
  601.9 1.9 collective-permute-start.1
  604.4 14.9 %collective-permute-done.1 = bf16[32,1536]{1,0:T(8,128)(2,1)S(1)} collective-permute-done((bf16[32,1536]{1,0:T(8,128)(2,1)S(1)}, bf16[32,1536]{1,0:T(8,128)(2,1)S(1)}, u32[]{:S(2)}, u32[]{:S(2)}) %collective-permute-start.1) | collective-permute-done | bytes 98336 | tf_op jit(solution)/shard_map/while/body/eval_jaxpr/ppermute | solution.py:12
  621.9 1.9 collective-permute-start.1
  624.4 14.9 %collective-permute-done.1 = bf16[32,1536]{1,0:T(8,128)(2,1)S(1)} collective-permute-done((bf16[32,1536]{1,0:T(8,128)(2,1)S(1)}, bf16[32,1536]{1,0:T(8,128)(2,1)S(1)}, u32[]{:S(2)}, u32[]{:S(2)}) %collective-permute-start.1) | collective-permute-done | bytes 98336 | tf_op jit(solution)/shard_map/while/body/eval_jaxpr/ppermute | solution.py:12
  641.9 1.9 collective-permute-start.1
  644.5 14.9 %collective-permute-done.1 = bf16[32,1536]{1,0:T(8,128)(2,1)S(1)} collective-permute-done((bf16[32,1536]{1,0:T(8,128)(2,1)S(1)}, bf16[32,1536]{1,0:T(8,128)(2,1)S(1)}, u32[]{:S(2)}, u32[]{:S(2)}) %collective-permute-start.1) | collective-permute-done | bytes 98336 | tf_op jit(solution)/shard_map/while/body/eval_jaxpr/ppermute | solution.py:12
  661.9 1.9 collective-permute-start.1
  664.5 15.0 %collective-permute-done.1 = bf16[32,1536]{1,0:T(8,128)(2,1)S(1)} collective-permute-done((bf16[32,1536]{1,0:T(8,128)(2,1)S(1)}, bf16[32,1536]{1,0:T(8,128)(2,1)S(1)}, u32[]{:S(2)}, u32[]{:S(2)}) %collective-permute-start.1) | collective-permute-done | bytes 98336 | tf_op jit(solution)/shard_map/while/body/eval_jaxpr/ppermute | solution.py:12
  682.0 1.9 collective-permute-start.1
  684.6 15.0 %collective-permute-done.1 = bf16[32,1536]{1,0:T(8,128)(2,1)S(1)} collective-permute-done((bf16[32,1536]{1,0:T(8,128)(2,1)S(1)}, bf16[32,1536]{1,0:T(8,128)(2,1)S(1)}, u32[]{:S(2)}, u32[]{:S(2)}) %collective-permute-start.1) | collective-permute-done | bytes 98336 | tf_op jit(solution)/shard_map/while/body/eval_jaxpr/ppermute | solution.py:12
  702.0 1.9 collective-permute-start.1
  704.6 14.8 %collective-permute-done.1 = bf16[32,1536]{1,0:T(8,128)(2,1)S(1)} collective-permute-done((bf16[32,1536]{1,0:T(8,128)(2,1)S(1)}, bf16[32,1536]{1,0:T(8,128)(2,1)S(1)}, u32[]{:S(2)}, u32[]{:S(2)}) %collective-permute-start.1) | collective-permute-done | bytes 98336 | tf_op jit(solution)/shard_map/while/body/eval_jaxpr/ppermute | solution.py:12
  722.0 1.9 collective-permute-start.1
  724.5 14.8 %collective-permute-done.1 = bf16[32,1536]{1,0:T(8,128)(2,1)S(1)} collective-permute-done((bf16[32,1536]{1,0:T(8,128)(2,1)S(1)}, bf16[32,1536]{1,0:T(8,128)(2,1)S(1)}, u32[]{:S(2)}, u32[]{:S(2)}) %collective-permute-start.1) | collective-permute-done | bytes 98336 | tf_op jit(solution)/shard_map/while/body/eval_jaxpr/ppermute | solution.py:12
  744.6 246.1 %all-reduce.1 = f32[1536]{0:T(1024)S(1)} all-reduce(f32[1536]{0:T(1024)S(1)} %get-tuple-element.514), channel_id=3, replica_groups=mesh['section'=8,'expert'=64] {'expert'}, use_global_device_ids=true, to_apply=%region_20.21.clone | all-reduce | flops 1536 | bytes 12288
  991.4 310.4 %reduce-scatter.5.cloned.1.call-done = f32[24,128]{1,0:T(8,128)} async-done(((f32[1536,128]{1,0:T(8,128)}), f32[24,128]{1,0:T(8,128)}) %reduce-scatter.5.cloned.1.call-update) | async-done | bytes 12304
  (392 shorter events, 75.2 us)
Async XLA Ops:
  14.2 16.4 %copy-start.5 = (s32[1,4,32,4]{2,3,1,0:T(4,128)S(1)}, s32[1,4,32,4]{2,3,1,0:T(4,128)}, u32[]{:S(2)}) copy-start(s32[1,4,32,4]{2,3,1,0:T(4,128)} %param.14) | copy-start | bytes 6148
  14.2 235.5 %all-to-all-start = ((bf16[1,4,2,64,2,1536]{5,4,2,1,0,3:T(2,128)(2,1)}), bf16[1,4,2,64,2,1536]{5,4,2,1,0,3:T(2,128)(2,1)S(1)}, u32[]{:S(2)}, u32[]{:S(2)}) async-start(bf16[1,4,2,64,2,1536]{5,4,2,1,0,3:T(2,128)(2,1)} %copy.70), calls=%async_computation | async-start | bytes 6291456 | tf_op jit(solution)/shard_map/all_to_all | solution.py:100
  30.5 1271.2 %reduce-scatter.5.cloned.1.call-start = ((), (), s32[]{:S(2)}) async-start(), calls=%async_computation.2 | async-start | bytes 798720
  269.5 5.0 copy-start
  269.5 5.0 copy-start.4
  277.9 17.0 %collective-permute-start = (bf16[32,1536]{1,0:T(8,128)(2,1)S(1)}, bf16[32,1536]{1,0:T(8,128)(2,1)S(1)}, u32[]{:S(2)}, u32[]{:S(2)}) collective-permute-start(bf16[32,1536]{1,0:T(8,128)(2,1)S(1)} %fusion.75), channel_id=1, source_target_pairs={{0,64},{64,128},{128,192},{192,256},{256,320},{320,384},{384,448},... | collective-permute-start | bytes 294920 | tf_op jit(solution)/shard_map/while/body/eval_jaxpr/ppermute | solution.py:12
  298.2 19.4 %collective-permute-start = (bf16[32,1536]{1,0:T(8,128)(2,1)S(1)}, bf16[32,1536]{1,0:T(8,128)(2,1)S(1)}, u32[]{:S(2)}, u32[]{:S(2)}) collective-permute-start(bf16[32,1536]{1,0:T(8,128)(2,1)S(1)} %fusion.75), channel_id=1, source_target_pairs={{0,64},{64,128},{128,192},{192,256},{256,320},{320,384},{384,448},... | collective-permute-start | bytes 294920 | tf_op jit(solution)/shard_map/while/body/eval_jaxpr/ppermute | solution.py:12
  321.0 19.1 %collective-permute-start = (bf16[32,1536]{1,0:T(8,128)(2,1)S(1)}, bf16[32,1536]{1,0:T(8,128)(2,1)S(1)}, u32[]{:S(2)}, u32[]{:S(2)}) collective-permute-start(bf16[32,1536]{1,0:T(8,128)(2,1)S(1)} %fusion.75), channel_id=1, source_target_pairs={{0,64},{64,128},{128,192},{192,256},{256,320},{320,384},{384,448},... | collective-permute-start | bytes 294920 | tf_op jit(solution)/shard_map/while/body/eval_jaxpr/ppermute | solution.py:12
  343.4 17.4 %collective-permute-start = (bf16[32,1536]{1,0:T(8,128)(2,1)S(1)}, bf16[32,1536]{1,0:T(8,128)(2,1)S(1)}, u32[]{:S(2)}, u32[]{:S(2)}) collective-permute-start(bf16[32,1536]{1,0:T(8,128)(2,1)S(1)} %fusion.75), channel_id=1, source_target_pairs={{0,64},{64,128},{128,192},{192,256},{256,320},{320,384},{384,448},... | collective-permute-start | bytes 294920 | tf_op jit(solution)/shard_map/while/body/eval_jaxpr/ppermute | solution.py:12
  364.2 17.3 %collective-permute-start = (bf16[32,1536]{1,0:T(8,128)(2,1)S(1)}, bf16[32,1536]{1,0:T(8,128)(2,1)S(1)}, u32[]{:S(2)}, u32[]{:S(2)}) collective-permute-start(bf16[32,1536]{1,0:T(8,128)(2,1)S(1)} %fusion.75), channel_id=1, source_target_pairs={{0,64},{64,128},{128,192},{192,256},{256,320},{320,384},{384,448},... | collective-permute-start | bytes 294920 | tf_op jit(solution)/shard_map/while/body/eval_jaxpr/ppermute | solution.py:12
  384.9 17.3 %collective-permute-start = (bf16[32,1536]{1,0:T(8,128)(2,1)S(1)}, bf16[32,1536]{1,0:T(8,128)(2,1)S(1)}, u32[]{:S(2)}, u32[]{:S(2)}) collective-permute-start(bf16[32,1536]{1,0:T(8,128)(2,1)S(1)} %fusion.75), channel_id=1, source_target_pairs={{0,64},{64,128},{128,192},{192,256},{256,320},{320,384},{384,448},... | collective-permute-start | bytes 294920 | tf_op jit(solution)/shard_map/while/body/eval_jaxpr/ppermute | solution.py:12
  405.6 17.3 %collective-permute-start = (bf16[32,1536]{1,0:T(8,128)(2,1)S(1)}, bf16[32,1536]{1,0:T(8,128)(2,1)S(1)}, u32[]{:S(2)}, u32[]{:S(2)}) collective-permute-start(bf16[32,1536]{1,0:T(8,128)(2,1)S(1)} %fusion.75), channel_id=1, source_target_pairs={{0,64},{64,128},{128,192},{192,256},{256,320},{320,384},{384,448},... | collective-permute-start | bytes 294920 | tf_op jit(solution)/shard_map/while/body/eval_jaxpr/ppermute | solution.py:12
  426.3 17.3 %collective-permute-start = (bf16[32,1536]{1,0:T(8,128)(2,1)S(1)}, bf16[32,1536]{1,0:T(8,128)(2,1)S(1)}, u32[]{:S(2)}, u32[]{:S(2)}) collective-permute-start(bf16[32,1536]{1,0:T(8,128)(2,1)S(1)} %fusion.75), channel_id=1, source_target_pairs={{0,64},{64,128},{128,192},{192,256},{256,320},{320,384},{384,448},... | collective-permute-start | bytes 294920 | tf_op jit(solution)/shard_map/while/body/eval_jaxpr/ppermute | solution.py:12
  447.0 17.3 %collective-permute-start = (bf16[32,1536]{1,0:T(8,128)(2,1)S(1)}, bf16[32,1536]{1,0:T(8,128)(2,1)S(1)}, u32[]{:S(2)}, u32[]{:S(2)}) collective-permute-start(bf16[32,1536]{1,0:T(8,128)(2,1)S(1)} %fusion.75), channel_id=1, source_target_pairs={{0,64},{64,128},{128,192},{192,256},{256,320},{320,384},{384,448},... | collective-permute-start | bytes 294920 | tf_op jit(solution)/shard_map/while/body/eval_jaxpr/ppermute | solution.py:12
  467.7 17.3 %collective-permute-start = (bf16[32,1536]{1,0:T(8,128)(2,1)S(1)}, bf16[32,1536]{1,0:T(8,128)(2,1)S(1)}, u32[]{:S(2)}, u32[]{:S(2)}) collective-permute-start(bf16[32,1536]{1,0:T(8,128)(2,1)S(1)} %fusion.75), channel_id=1, source_target_pairs={{0,64},{64,128},{128,192},{192,256},{256,320},{320,384},{384,448},... | collective-permute-start | bytes 294920 | tf_op jit(solution)/shard_map/while/body/eval_jaxpr/ppermute | solution.py:12
  488.4 17.3 %collective-permute-start = (bf16[32,1536]{1,0:T(8,128)(2,1)S(1)}, bf16[32,1536]{1,0:T(8,128)(2,1)S(1)}, u32[]{:S(2)}, u32[]{:S(2)}) collective-permute-start(bf16[32,1536]{1,0:T(8,128)(2,1)S(1)} %fusion.75), channel_id=1, source_target_pairs={{0,64},{64,128},{128,192},{192,256},{256,320},{320,384},{384,448},... | collective-permute-start | bytes 294920 | tf_op jit(solution)/shard_map/while/body/eval_jaxpr/ppermute | solution.py:12
  505.8 2.7 copy-start.6
  506.8 7.1 copy-start.3
  513.9 7.8 copy-start.1
  521.8 17.7 %collective-permute-start.1 = (bf16[32,1536]{1,0:T(8,128)(2,1)S(1)}, bf16[32,1536]{1,0:T(8,128)(2,1)S(1)}, u32[]{:S(2)}, u32[]{:S(2)}) collective-permute-start(bf16[32,1536]{1,0:T(8,128)(2,1)S(1)} %bitcast_select_fusion.6), channel_id=1, source_target_pairs={{0,448},{64,0},{128,64},{192,128},{256,192},{320,256},{384,320},{4... | collective-permute-start | bytes 294920 | tf_op jit(solution)/shard_map/while/body/eval_jaxpr/ppermute | solution.py:12
  542.0 17.3 %collective-permute-start.1 = (bf16[32,1536]{1,0:T(8,128)(2,1)S(1)}, bf16[32,1536]{1,0:T(8,128)(2,1)S(1)}, u32[]{:S(2)}, u32[]{:S(2)}) collective-permute-start(bf16[32,1536]{1,0:T(8,128)(2,1)S(1)} %bitcast_select_fusion.6), channel_id=1, source_target_pairs={{0,448},{64,0},{128,64},{192,128},{256,192},{320,256},{384,320},{4... | collective-permute-start | bytes 294920 | tf_op jit(solution)/shard_map/while/body/eval_jaxpr/ppermute | solution.py:12
  561.9 17.4 %collective-permute-start.1 = (bf16[32,1536]{1,0:T(8,128)(2,1)S(1)}, bf16[32,1536]{1,0:T(8,128)(2,1)S(1)}, u32[]{:S(2)}, u32[]{:S(2)}) collective-permute-start(bf16[32,1536]{1,0:T(8,128)(2,1)S(1)} %bitcast_select_fusion.6), channel_id=1, source_target_pairs={{0,448},{64,0},{128,64},{192,128},{256,192},{320,256},{384,320},{4... | collective-permute-start | bytes 294920 | tf_op jit(solution)/shard_map/while/body/eval_jaxpr/ppermute | solution.py:12
  581.9 17.5 %collective-permute-start.1 = (bf16[32,1536]{1,0:T(8,128)(2,1)S(1)}, bf16[32,1536]{1,0:T(8,128)(2,1)S(1)}, u32[]{:S(2)}, u32[]{:S(2)}) collective-permute-start(bf16[32,1536]{1,0:T(8,128)(2,1)S(1)} %bitcast_select_fusion.6), channel_id=1, source_target_pairs={{0,448},{64,0},{128,64},{192,128},{256,192},{320,256},{384,320},{4... | collective-permute-start | bytes 294920 | tf_op jit(solution)/shard_map/while/body/eval_jaxpr/ppermute | solution.py:12
  601.9 17.5 %collective-permute-start.1 = (bf16[32,1536]{1,0:T(8,128)(2,1)S(1)}, bf16[32,1536]{1,0:T(8,128)(2,1)S(1)}, u32[]{:S(2)}, u32[]{:S(2)}) collective-permute-start(bf16[32,1536]{1,0:T(8,128)(2,1)S(1)} %bitcast_select_fusion.6), channel_id=1, source_target_pairs={{0,448},{64,0},{128,64},{192,128},{256,192},{320,256},{384,320},{4... | collective-permute-start | bytes 294920 | tf_op jit(solution)/shard_map/while/body/eval_jaxpr/ppermute | solution.py:12
  621.9 17.5 %collective-permute-start.1 = (bf16[32,1536]{1,0:T(8,128)(2,1)S(1)}, bf16[32,1536]{1,0:T(8,128)(2,1)S(1)}, u32[]{:S(2)}, u32[]{:S(2)}) collective-permute-start(bf16[32,1536]{1,0:T(8,128)(2,1)S(1)} %bitcast_select_fusion.6), channel_id=1, source_target_pairs={{0,448},{64,0},{128,64},{192,128},{256,192},{320,256},{384,320},{4... | collective-permute-start | bytes 294920 | tf_op jit(solution)/shard_map/while/body/eval_jaxpr/ppermute | solution.py:12
  641.9 17.5 %collective-permute-start.1 = (bf16[32,1536]{1,0:T(8,128)(2,1)S(1)}, bf16[32,1536]{1,0:T(8,128)(2,1)S(1)}, u32[]{:S(2)}, u32[]{:S(2)}) collective-permute-start(bf16[32,1536]{1,0:T(8,128)(2,1)S(1)} %bitcast_select_fusion.6), channel_id=1, source_target_pairs={{0,448},{64,0},{128,64},{192,128},{256,192},{320,256},{384,320},{4... | collective-permute-start | bytes 294920 | tf_op jit(solution)/shard_map/while/body/eval_jaxpr/ppermute | solution.py:12
  661.9 17.5 %collective-permute-start.1 = (bf16[32,1536]{1,0:T(8,128)(2,1)S(1)}, bf16[32,1536]{1,0:T(8,128)(2,1)S(1)}, u32[]{:S(2)}, u32[]{:S(2)}) collective-permute-start(bf16[32,1536]{1,0:T(8,128)(2,1)S(1)} %bitcast_select_fusion.6), channel_id=1, source_target_pairs={{0,448},{64,0},{128,64},{192,128},{256,192},{320,256},{384,320},{4... | collective-permute-start | bytes 294920 | tf_op jit(solution)/shard_map/while/body/eval_jaxpr/ppermute | solution.py:12
  682.0 17.5 %collective-permute-start.1 = (bf16[32,1536]{1,0:T(8,128)(2,1)S(1)}, bf16[32,1536]{1,0:T(8,128)(2,1)S(1)}, u32[]{:S(2)}, u32[]{:S(2)}) collective-permute-start(bf16[32,1536]{1,0:T(8,128)(2,1)S(1)} %bitcast_select_fusion.6), channel_id=1, source_target_pairs={{0,448},{64,0},{128,64},{192,128},{256,192},{320,256},{384,320},{4... | collective-permute-start | bytes 294920 | tf_op jit(solution)/shard_map/while/body/eval_jaxpr/ppermute | solution.py:12
  702.0 17.4 %collective-permute-start.1 = (bf16[32,1536]{1,0:T(8,128)(2,1)S(1)}, bf16[32,1536]{1,0:T(8,128)(2,1)S(1)}, u32[]{:S(2)}, u32[]{:S(2)}) collective-permute-start(bf16[32,1536]{1,0:T(8,128)(2,1)S(1)} %bitcast_select_fusion.6), channel_id=1, source_target_pairs={{0,448},{64,0},{128,64},{192,128},{256,192},{320,256},{384,320},{4... | collective-permute-start | bytes 294920 | tf_op jit(solution)/shard_map/while/body/eval_jaxpr/ppermute | solution.py:12
  722.0 17.3 %collective-permute-start.1 = (bf16[32,1536]{1,0:T(8,128)(2,1)S(1)}, bf16[32,1536]{1,0:T(8,128)(2,1)S(1)}, u32[]{:S(2)}, u32[]{:S(2)}) collective-permute-start(bf16[32,1536]{1,0:T(8,128)(2,1)S(1)} %bitcast_select_fusion.6), channel_id=1, source_target_pairs={{0,448},{64,0},{128,64},{192,128},{256,192},{320,256},{384,320},{4... | collective-permute-start | bytes 294920 | tf_op jit(solution)/shard_map/while/body/eval_jaxpr/ppermute | solution.py:12
  741.8 0.9 copy-start.2
Sparse Core Ops, SparseCore 0:
  742.8 558.8 reduce-scatter.4
where the time goes:
time: 1310 us
  waiting for transfers between devices  518 us (40%)
  blocking collectives  449 us (34%)
  starting transfers between devices  197 us (15%)
  other arithmetic  68.7 us (5%)
  local copies, waits for them, and re-layouts  44.2 us (3%)
  between operations  14.9 us (1%)
  matrix products  13.7 us (1%)
    unnamed x2, waiting for transfers between devices  310 us
    unnamed x1, blocking collectives  246 us
    ppermute x22, waiting for transfers between devices, shifted(): return lax.ppermute(value, axis, pairs)  198 us
    ppermute x22, starting transfers between devices, shifted(): return lax.ppermute(value, axis, pairs)  181 us
    all_gather x1, blocking collectives, per_device(): lax.all_gather(inputs, 'section', axis=2, tiled=True)  133 us
    all_gather x1, blocking collectives, per_device(): lax.all_gather(cotangent, 'section', axis=2, tiled=True)  70.5 us
  transfers between devices with their start and end apart: 24, of which 24 were waited for; matrix products, arithmetic and copies ran while one was open for 1% of the time, Pallas kernels for 0%

commit v1 on v0

v1 whole, which is shorter than its diff:
```python
import functools

import jax
import jax.numpy as jnp
from jax import lax
from jax.experimental import pallas as pl
from jax.experimental.pallas import tpu as pltpu
from jax.sharding import Mesh, PartitionSpec as P

EPSILON = 1e-05
HALVES = 2
F32 = jnp.float32
BF16 = jnp.bfloat16


def onehots(routes_ref, layer, choices, experts):
    lanes = lax.broadcasted_iota(jnp.int32, (routes_ref.shape[1], experts), 1)
    rows = routes_ref[layer]
    return [rows[:, k : k + 1] == lanes for k in range(choices)]


def forward_layer(layer, state, refs, normed_ref, weights_ref, rscale_ref):
    picks_ref, routes_ref, w_ref, gain_ref = refs
    half = state[0].shape[1]
    experts = w_ref.shape[2]
    choices = routes_ref.shape[2]
    floats = [part.astype(F32) for part in state]
    total = sum(jnp.sum(part * part, axis=-1, keepdims=True) for part in floats)
    rscale = lax.rsqrt(total / (HALVES * half) + EPSILON)
    logits = jnp.zeros((state[0].shape[0], experts), F32)
    for h in range(HALVES):
        normed = (floats[h] * rscale * gain_ref[layer, h : h + 1, :]).astype(BF16)
        normed_ref[layer, h] = normed
        logits += jnp.dot(normed, w_ref[layer, h * half : (h + 1) * half, :], preferred_element_type=F32)
    hots = onehots(routes_ref, layer, choices, experts)
    raised = [jnp.exp(jnp.sum(jnp.where(hot, logits, 0.0), axis=-1, keepdims=True)) for hot in hots]
    bottom = sum(raised)
    weights = [value / bottom for value in raised]
    for k in range(choices):
        weights_ref[layer, k] = jnp.broadcast_to(weights[k], weights_ref.shape[2:])
    rscale_ref[layer] = jnp.broadcast_to(rscale, rscale_ref.shape[1:])
    fresh = []
    for h in range(HALVES):
        mixture = sum(weights[k] * picks_ref[layer, h, k].astype(F32) for k in range(choices))
        fresh.append((floats[h] + mixture).astype(BF16))
    return fresh


def backward_layer(layer, back, state, refs, weights_ref, rscale_ref, dlogits_ref):
    picks_ref, routes_ref, w_ref, gain_ref = refs
    half = state[0].shape[1]
    experts = w_ref.shape[2]
    choices = routes_ref.shape[2]
    back_float = [part.astype(F32) for part in back]
    weights = [weights_ref[layer, k][:, 0:1] for k in range(choices)]
    rscale = rscale_ref[layer][:, 0:1]
    dweights = [
        sum(
            jnp.sum(back_float[h] * picks_ref[layer, h, k].astype(F32), axis=-1, keepdims=True)
            for h in range(HALVES)
        )
        for k in range(choices)
    ]
    average = sum(w * d for w, d in zip(weights, dweights))
    dlogits = jnp.zeros((back[0].shape[0], experts), F32)
    for k, hot in enumerate(onehots(routes_ref, layer, choices, experts)):
        dlogits += jnp.where(hot, weights[k] * (dweights[k] - average), 0.0)
    dlogits = dlogits.astype(BF16)
    dlogits_ref[layer] = dlogits
    varied, normal = [], []
    for h in range(HALVES):
        dnormed = lax.dot_general(
            dlogits,
            w_ref[layer, h * half : (h + 1) * half, :],
            (((1,), (1,)), ((), ())),
            preferred_element_type=F32,
        )
        varied.append(dnormed * gain_ref[layer, h : h + 1, :])
        normal.append(state[h].astype(F32) * rscale)
    mean = sum(jnp.sum(v * s, axis=-1, keepdims=True) for v, s in zip(varied, normal)) / (HALVES * half)
    return [(b + rscale * (v - s * mean)).astype(BF16) for b, v, s in zip(back_float, varied, normal)]


def first_kernel(
    zh_ref, table_ref, select_ref, routes_ref, w_ref, gain_ref, acts_ref,
    picks_ref, states_ref, normed_ref, weights_ref, rscale_ref, out_ref,
):
    layers = table_ref.shape[0]
    choices = routes_ref.shape[2]
    tokens = routes_ref.shape[1]
    for layer in range(layers):
        rows = jnp.dot(select_ref[layer], table_ref[layer], preferred_element_type=F32).astype(BF16)
        for h in range(HALVES):
            for k in range(choices):
                at = (h * choices + k) * tokens
                picks_ref[layer, h, k] = rows[at : at + tokens]

    @pl.when(zh_ref[0] == 0)
    def _():
        refs = (picks_ref, routes_ref, w_ref, gain_ref)
        state = [acts_ref[h] for h in range(HALVES)]
        for layer in range(layers):
            for h in range(HALVES):
                states_ref[layer, h] = state[h]
            state = forward_layer(layer, state, refs, normed_ref, weights_ref, rscale_ref)
        for h in range(HALVES):
            out_ref[h] = state[h]


def middle_kernel(
    zh_ref, arrived_ref, acts_ref, final_ref, picks_ref, routes_ref, w_ref, gain_ref, given_ref,
    normed_ref, dlogits_ref, out_ref, states_ref, weights_ref, rscale_ref,
):
    layers = picks_ref.shape[0]
    half = acts_ref.shape[2]

    @pl.when(zh_ref[0] == 0)
    def _():
        normed_ref[...] = given_ref[...]

    @pl.when(zh_ref[0] != 0)
    def _():
        refs = (picks_ref, routes_ref, w_ref, gain_ref)
        state = [arrived_ref[h] for h in range(HALVES)]
        for layer in range(layers):
            for h in range(HALVES):
                states_ref[layer, h] = state[h]
            state = forward_layer(layer, state, refs, normed_ref, weights_ref, rscale_ref)
        floats = [part.astype(F32) for part in state]
        total = sum(jnp.sum(part * part, axis=-1, keepdims=True) for part in floats)
        rscale = lax.rsqrt(total / (HALVES * half) + EPSILON)
        normal = [part * rscale for part in floats]
        varied = [acts_ref[h].astype(F32) * final_ref[h : h + 1, :] for h in range(HALVES)]
        mean = sum(jnp.sum(v * s, axis=-1, keepdims=True) for v, s in zip(varied, normal)) / (HALVES * half)
        back = [(rscale * (v - s * mean)).astype(BF16) for v, s in zip(varied, normal)]
        for layer in reversed(range(layers)):
            state = [states_ref[layer, h] for h in range(HALVES)]
            back = backward_layer(layer, back, state, refs, weights_ref, rscale_ref, dlogits_ref)
        for h in range(HALVES):
            out_ref[h] = back[h]


def last_kernel(
    zh_ref, arrived_ref, states_ref, weights_ref, rscale_ref, picks_ref, routes_ref, w_ref, gain_ref,
    given_ref, dlogits_ref,
):
    layers = picks_ref.shape[0]

    @pl.when(zh_ref[0] != 0)
    def _():
        dlogits_ref[...] = given_ref[...]

    @pl.when(zh_ref[0] == 0)
    def _():
        refs = (picks_ref, routes_ref, w_ref, gain_ref)
        back = [arrived_ref[h] for h in range(HALVES)]
        for layer in reversed(range(layers)):
            state = [states_ref[layer, h] for h in range(HALVES)]
            back = backward_layer(layer, back, state, refs, weights_ref, rscale_ref, dlogits_ref)


def grad_kernel(planes, normed_ref, dlogits_ref, out_ref):
    micros, _, tokens, half = normed_ref.shape
    experts = dlogits_ref.shape[2]
    groups, per_group = out_ref.shape[:2]
    piece = per_group // planes
    dlogits = dlogits_ref[...].reshape(micros * tokens, experts)
    for h in range(HALVES):
        rows = jnp.concatenate([normed_ref[m, h] for m in range(micros)], axis=0)
        term = lax.dot_general(rows, dlogits, (((0,), (0,)), ((), ())), preferred_element_type=F32)
        for at in range(0, half, piece):
            owner = (h * half + at) // piece
            plane, group = owner // groups, owner % groups
            out_ref[group, plane * piece : (plane + 1) * piece, :] = term[at : at + piece]


def call(kernel, outs, args, scratch=(), scalars=1):
    smem = [pl.BlockSpec(memory_space=pltpu.SMEM)] * scalars
    vmem = pl.BlockSpec(memory_space=pltpu.VMEM)
    return pl.pallas_call(
        kernel,
        out_shape=outs,
        in_specs=smem + [vmem] * (len(args) - scalars),
        out_specs=jax.tree.map(lambda _: vmem, outs),
        scratch_shapes=list(scratch),
    )(*args)


def slot_numbers(routes):
    flattened = routes.reshape(routes.shape[0], -1)
    pair_count = flattened.shape[1]
    matches = flattened[:, :, None] == flattened[:, None, :]
    earlier = lax.broadcasted_iota(jnp.int32, (pair_count, pair_count), 1) < lax.broadcasted_iota(
        jnp.int32, (pair_count, pair_count), 0
    )
    return jnp.sum(jnp.where(matches & earlier[None], 1, 0), axis=-1).astype(jnp.int32).reshape(routes.shape)


def thirds(values):
    high = values.astype(BF16)
    rest = values - high.astype(F32)
    middle = rest.astype(BF16)
    return jnp.stack([high, middle, (rest - middle.astype(F32)).astype(BF16)])


def per_device(expert_axes, plane_axis, flat_axes, inputs, cotangent, expert_out, route_ids, router_w, norm_gain, final_gain):
    zh = lax.axis_index("zh")
    micros, tokens, piece = inputs.shape
    layers = lax.axis_size("x")
    owners = lax.axis_size(expert_axes)
    local_experts, capacity, width = expert_out.shape[2], expert_out.shape[4], expert_out.shape[5]
    half = width // HALVES
    experts = router_w.shape[2]
    choices = route_ids.shape[3]
    zh_word = jnp.reshape(zh, (1,)).astype(jnp.int32)

    kept = jnp.where(zh == 0, inputs, cotangent)
    crossing = jnp.where(zh == 0, cotangent, inputs)
    crossed = lax.ppermute(crossing, "zh", [(0, 1), (1, 0)])

    rows = expert_out[0].reshape(micros, local_experts, owners, capacity, HALVES, half)
    rows = rows.transpose(0, 2, 1, 4, 3, 5).reshape(micros * owners, local_experts * HALVES * capacity, half)
    with jax.named_scope("rows_exchange"):
        table = lax.all_to_all(rows, ("x",) + expert_axes, split_axis=0, concat_axis=0, tiled=True)
    table = table.reshape(layers, experts * HALVES * capacity, half)

    lower = jnp.where(zh == 0, kept, crossed)
    upper = jnp.where(zh == 0, crossed, kept)
    acts_part = jnp.stack([lower, upper], axis=2).reshape(micros, tokens * HALVES * piece // 128, 128)
    act_rows = acts_part.shape[1]
    route_part = route_ids[0].astype(BF16).reshape(micros, tokens * choices // 128, 128)
    route_rows = route_part.shape[1]
    route_part = jnp.pad(route_part, ((0, 0), (0, 8 - route_rows), (0, 0)))
    gain_part = thirds(norm_gain[0]).reshape(3 * width // 128, 128)
    gain_rows = gain_part.shape[0]
    gain_part = jnp.pad(gain_part, ((0, -gain_rows % 8), (0, 0)))
    shared = jnp.concatenate([router_w[0], gain_part], axis=0)
    shared = jnp.broadcast_to(shared[None], (layers,) + shared.shape)
    with jax.named_scope("small_exchange"):
        packed = lax.all_to_all(
            jnp.concatenate([shared, acts_part, route_part], axis=1), "x", split_axis=0, concat_axis=0, tiled=True
        )
    w_all = packed[:, :width]
    gain_all = packed[:, width : width + gain_rows].reshape(layers, 3, width).astype(F32)
    gain_all = (gain_all[:, 0] + gain_all[:, 1] + gain_all[:, 2]).reshape(layers, HALVES, half)
    at = shared.shape[1]
    acts = packed[:, at : at + act_rows].reshape(layers, tokens, HALVES, piece)
    acts = acts.transpose(2, 1, 0, 3).reshape(HALVES, tokens, half)
    at += act_rows
    routes = packed[:, at : at + route_rows].reshape(layers, tokens, choices).astype(F32).astype(jnp.int32)

    target = routes * (HALVES * capacity) + slot_numbers(routes)
    target = target.transpose(0, 2, 1)[:, None] + (jnp.arange(HALVES) * capacity)[None, :, None, None]
    target = target.reshape(layers, HALVES * choices * tokens, 1)
    select = (target == jnp.arange(experts * HALVES * capacity)[None, None, :]).astype(BF16)

    shape = jax.ShapeDtypeStruct
    rows_shape = (HALVES, tokens, half)
    picks, states, normed, weights, rscale, sent = call(
        first_kernel,
        (
            shape((layers, HALVES, choices, tokens, half), BF16),
            shape((layers,) + rows_shape, BF16),
            shape((layers,) + rows_shape, BF16),
            shape((layers, choices, tokens, 128), F32),
            shape((layers, tokens, 128), F32),
            shape(rows_shape, BF16),
        ),
        (zh_word, table, select, routes, w_all, gain_all, acts),
    )
    arrived = lax.ppermute(sent, "zh", [(0, 1)])
    normed, dlogits, sent = call(
        middle_kernel,
        (
            shape((layers,) + rows_shape, BF16),
            shape((layers, tokens, experts), BF16),
            shape(rows_shape, BF16),
        ),
        (zh_word, arrived, acts, final_gain.reshape(HALVES, half), picks, routes, w_all, gain_all, normed),
        scratch=(
            pltpu.VMEM((layers,) + rows_shape, BF16),
            pltpu.VMEM((layers, choices, tokens, 128), F32),
            pltpu.VMEM((layers, tokens, 128), F32),
        ),
    )
    arrived = lax.ppermute(sent, "zh", [(1, 0)])
    with jax.named_scope("normed_exchange"):
        normed = lax.all_to_all(normed, "x", split_axis=0, concat_axis=0, tiled=True)
    dlogits = call(
        last_kernel,
        shape((layers, tokens, experts), BF16),
        (zh_word, arrived, states, weights, rscale, picks, routes, w_all, gain_all, dlogits),
    )
    dlogits = lax.all_to_all(dlogits, "x", split_axis=0, concat_axis=0, tiled=True)

    planes = lax.axis_size(plane_axis)
    groups = owners // planes
    term = call(
        functools.partial(grad_kernel, planes),
        shape((groups, width // groups, experts), F32),
        (normed, dlogits),
        scalars=0,
    )
    term = lax.all_to_all(term, flat_axes, split_axis=0, concat_axis=0, tiled=True)
    term = jnp.sum(term, axis=0).reshape(planes, width // owners, experts)
    term = lax.all_to_all(term, plane_axis, split_axis=0, concat_axis=0, tiled=True)
    router_part = jnp.sum(term, axis=0)
    at = lax.axis_index(expert_axes) * (width // owners)
    w_slab = lax.dynamic_slice_in_dim(router_w[0], at, width // owners, 0).astype(F32)
    gain_slab = lax.dynamic_slice_in_dim(norm_gain[0], at, width // owners, 0)
    gain_part = jnp.sum(w_slab * router_part, axis=-1) / gain_slab
    return (router_part[None], gain_part[None])


def solution(mesh):
    sections, owners = mesh.shape["section"], mesh.shape["expert"]
    planes = 8 if owners % 8 == 0 and owners > 8 else owners // 2
    groups = owners // planes
    wide = Mesh(mesh.devices.reshape(HALVES, sections // HALVES, planes, groups), ("zh", "x", "z", "yc"))
    section, expert = ("zh", "x"), ("z", "yc")
    placed = (
        P(None, expert, section),
        P(None, expert, section),
        P(section, None, expert, None, None, None),
        P(section, None, expert, None),
        P(section, None, None),
        P(section, None),
        P(),
    )
    return jax.shard_map(
        functools.partial(per_device, expert, "z", "yc"),
        mesh=wide,
        in_specs=placed,
        out_specs=(P(section, expert, None), P(section, expert)),
        check_vma=False,
    )
```

time: 1310 us -> 318 us (0.24)
  blocking collectives: 449 us -> 37.5 us
  waiting for transfers between devices: 518 us -> 171 us
  starting transfers between devices: 197 us -> 57.3 us
  other arithmetic: 68.7 us -> 12.2 us
  local copies, waits for them, and re-layouts: 44.2 us -> 21.2 us
  Pallas kernels: 0 us -> 17 us
  between operations: 14.9 us -> 0.83 us
  matrix products: 13.7 us -> 0 us
    unnamed x2 -> x0, waiting for transfers between devices: 310 us -> none
    unnamed x1 -> x0, blocking collectives: 246 us -> none
    all_gather x2 -> x0, blocking collectives: 203 us -> none  [the longest x1 133 us: per_device(): lax.all_gather(inputs, 'section', axis=2, tiled=True)]
    ppermute x22 -> x3, waiting for transfers between devices: 198 us -> 21.3 us  [the longest x1 18 us: per_device(): arrived = lax.ppermute(sent, 'zh', [(1, 0)])]
    ppermute x22 -> x3, starting transfers between devices: 181 us -> 22.6 us  [the longest x1 15.7 us: per_device(): crossed = lax.ppermute(crossing, 'zh', [(0, 1), (1, 0)])]
    all_to_all x1 -> x3, waiting for transfers between devices: 9.49 us -> 149 us  [the longest x1 131 us: per_device(): lax.all_to_all(rows, ('x',) + expert_axes, split_axis=0, concat_axis=0, t...]
    reduce_sum x112 -> x3, other arithmetic: 47.5 us -> 1.49 us  [the longest x1 0.81 us: per_device(): gain_part = jnp.sum(w_slab * router_part, axis=-1) / gain_slab]
    all_to_all x0 -> x3, blocking collectives: none -> 37.5 us  [the longest x1 17 us: per_device(): lax.all_to_all(term, flat_axes, split_axis=0, concat_axis=0, tiled=True)]
  transfers between devices with their start and end apart: 24 -> 6, of which waited for: 24 -> 6; matrix products, arithmetic and copies ran while one was open for 1% -> 8% of each run, Pallas kernels for 0% -> 0%
where the time goes in v1:
time: 318 us; the launch traced here: 317 us
  waiting for transfers between devices  171 us (54%)
  starting transfers between devices  57.3 us (18%)
  blocking collectives  37.5 us (12%)
  local copies, waits for them, and re-layouts  21.2 us (7%)
  Pallas kernels  17 us (5%)
  other arithmetic  12.2 us (4%)
    all_to_all x1, waiting for transfers between devices, per_device(): lax.all_to_all(rows, ('x',) + expert_axes, split_axis=0, concat_axis=0, t...  131 us
    all_to_all x1, starting transfers between devices, per_device(): lax.all_to_all(rows, ('x',) + expert_axes, split_axis=0, concat_axis=0, t...  20.1 us
    ppermute x1, waiting for transfers between devices, per_device(): arrived = lax.ppermute(sent, 'zh', [(1, 0)])  18 us
    all_to_all x1, blocking collectives, per_device(): lax.all_to_all(term, flat_axes, split_axis=0, concat_axis=0, tiled=True)  17 us
    pallas_call x4, Pallas kernels, call(): pl.pallas_call(kernel, out_shape=outs, in_specs=smem + [vmem] * (len(args...  17 us
    ppermute x1, starting transfers between devices, per_device(): crossed = lax.ppermute(crossing, 'zh', [(0, 1), (1, 0)])  15.7 us
    all_to_all x1, waiting for transfers between devices, per_device(): lax.all_to_all(term, plane_axis, split_axis=0, concat_axis=0, tiled=True)  11.2 us
    all_to_all x1, blocking collectives, per_device(): lax.all_to_all(normed, 'x', split_axis=0, concat_axis=0, tiled=True)  10.4 us
  transfers between devices with their start and end apart: 6, of which 6 were waited for; matrix products, arithmetic and copies ran while one was open for 8% of the time, Pallas kernels for 0%

profile of v1, /device:TPU:6, one launch (start us, length us, event | category | flops | bytes accessed | tf_op | source)
XLA Modules:
  0.0 316.6 jit_solution(16743028628657522751)
XLA Ops:
  0.6 0.9 broadcast_select_fusion
  1.5 15.7 %collective-permute-start = (bf16[4,32,192]{2,1,0:T(8,128)(2,1)S(1)}, bf16[4,32,192]{2,1,0:T(8,128)(2,1)S(1)}, u32[]{:S(2)}, u32[]{:S(2)}) collective-permute-start(bf16[4,32,192]{2,1,0:T(8,128)(2,1)S(1)} %broadcast_select_fusion), channel_id=1, source_target_pairs={{0,256},{256,0},{1,257},{257,1},{2,258},{258,2},{3,259},{259,3},{4... | collective-permute-start | bytes 147464 | tf_op jit(solution)/shard_map/ppermute | solution.py:219
  17.2 0.8 fusion.10
  18.1 1.0 fusion.4
  19.1 0.7 convert_element_type.78
  19.8 0.1 copy.25
  19.9 0.1 convert_element_type.91
  20.1 1.4 collective-permute-done
  21.4 0.9 select_bitcast_fusion.1
  22.3 0.1 copy.24
  22.5 0.2 reshape.103
  22.7 0.2 broadcast_in_dim.12
  22.9 1.4 fusion.2
  24.2 5.5 %all-to-all-start.1 = ((bf16[4,1680,128]{2,1,0:T(8,128)(2,1)}), bf16[4,1680,128]{2,1,0:T(8,128)(2,1)}, u32[]{:S(2)}, u32[]{:S(2)}) async-start(bf16[4,1680,128]{2,1,0:T(8,128)(2,1)} %fusion.2), calls=%async_computation.1 | async-start | bytes 3440640 | tf_op jit(solution)/shard_map/small_exchange/all_to_all | solution.py:240
  29.7 0.0 copy-done.1
  29.7 3.3 %reshape_squeeze.3 = bf16[4,2,64,2,2,768]{5,4,3,2,1,0:T(2,128)(2,1)} reshape(bf16[1,4,2,64,2,1536]{5,4,3,2,1,0:T(2,128)(2,1)S(1)} %copy-done.1) | data formatting | bytes 6291456 | tf_op jit(solution)/shard_map/reshape;squeeze | solution.py:221
  33.0 5.1 %copy.23 = bf16[4,64,2,2,2,768]{5,4,3,2,1,0:T(2,128)(2,1)S(1)} copy(bf16[4,64,2,2,2,768]{5,3,4,1,2,0:T(2,128)(2,1)} %bitcast.22) | data formatting | bytes 6291456 | tf_op jit(solution)/shard_map/transpose | solution.py:222
  38.1 2.7 reshape.100
  40.8 7.5 %all-to-all-done.1 = bf16[4,1680,128]{2,1,0:T(8,128)(2,1)} async-done(((bf16[4,1680,128]{2,1,0:T(8,128)(2,1)}), bf16[4,1680,128]{2,1,0:T(8,128)(2,1)}, u32[]{:S(2)}, u32[]{:S(2)}) %all-to-all-start.1) | async-done | bytes 1720352 | tf_op jit(solution)/shard_map/small_exchange/all_to_all | solution.py:240
  48.3 20.1 %all-to-all-start = ((bf16[256,8,768]{2,1,0:T(8,128)(2,1)}), bf16[256,8,768]{2,1,0:T(8,128)(2,1)S(1)}, u32[]{:S(2)}, u32[]{:S(2)}) async-start(bf16[256,8,768]{2,1,0:T(8,128)(2,1)} %reshape.100), calls=%async_computation | async-start | bytes 6291456 | tf_op jit(solution)/shard_map/rows_exchange/all_to_all | solution.py:224
  68.4 0.1 add.52
  68.5 0.1 add.53
  68.6 0.7 fusion.7
  69.3 0.2 select_reduce_fusion
  69.6 0.1 reshape.104
  69.7 0.7 fusion.9
  70.4 0.1 convert_element_type.82.routes_ref
  70.5 0.0 copy-start.2
  70.5 0.1 copy.27
  70.6 0.1 add.51
  70.7 0.8 slice_convert_fusion
  71.6 0.1 fusion.5
  71.7 0.6 add.58.gain_ref
  72.3 0.9 slice.34
  73.2 0.1 reshape.105
  73.3 0.1 copy.28
  73.4 0.8 reshape.106.acts_ref
  74.2 2.7 slice.29.w_ref
  76.9 0.0 copy-done.2
  76.9 1.2 fusion.1.select_ref
  78.1 130.6 %all-to-all-done = bf16[256,8,768]{2,1,0:T(8,128)(2,1)S(1)} async-done(((bf16[256,8,768]{2,1,0:T(8,128)(2,1)}), bf16[256,8,768]{2,1,0:T(8,128)(2,1)S(1)}, u32[]{:S(2)}, u32[]{:S(2)}) %all-to-all-start) | async-done | bytes 3145760 | tf_op jit(solution)/shard_map/rows_exchange/all_to_all | solution.py:224
  208.8 1.6 copy-done
  210.4 7.2 %shard_map.86 = (bf16[4,2,4,32,768]{4,3,2,1,0:T(8,128)(2,1)}, bf16[4,2,32,768]{3,2,1,0:T(8,128)(2,1)}, bf16[4,2,32,768]{3,2,1,0:T(8,128)(2,1)}, f32[4,4,32,128]{...) custom-call(s32[1]{0:T(128)} %bitcast.zh_ref, bf16[4,512,768]{2,1,0:T(8,128)(2,1)} %bitcast.21, ...), custom_call_target="tpu_custom_call" | custom-call | tf_op jit(solution)/shard_map/pallas_call | solution.py:180
  217.6 5.6 %collective-permute-start.1 = (bf16[2,32,768]{2,1,0:T(8,128)(2,1)}, bf16[2,32,768]{2,1,0:T(8,128)(2,1)S(1)}, u32[]{:S(2)}, u32[]{:S(2)}) collective-permute-start(bf16[2,32,768]{2,1,0:T(8,128)(2,1)} %get-tuple-element.11), channel_id=1, source_target_pairs={{0,256},{1,257},{2,258},{3,259},{4,260},{5,261},{6,262},{7,263},{8... | collective-permute-start | bytes 294920 | tf_op jit(solution)/shard_map/ppermute | solution.py:271
  223.3 0.0 copy-done.7
  223.3 0.6 reshape.107.final_ref
  223.9 1.9 collective-permute-done.1.arrived_ref
  225.8 0.6 copy-done.5
  226.4 2.9 shard_map.87
  229.3 1.3 collective-permute-start.2
  230.6 18.0 %collective-permute-done.2.arrived_ref = bf16[2,32,768]{2,1,0:T(8,128)(2,1)S(1)} collective-permute-done((bf16[2,32,768]{2,1,0:T(8,128)(2,1)}, bf16[2,32,768]{2,1,0:T(8,128)(2,1)S(1)}, u32[]{:S(2)}, u32[]{:S(2)}) %collective-permute-start.2) | collective-permute-done | bytes 98336 | tf_op jit(solution)/shard_map/ppermute | solution.py:286
  248.6 0.6 copy-done.4
  249.3 4.7 %shard_map.88 = bf16[4,32,128]{2,1,0:T(8,128)(2,1)} custom-call(s32[1]{0:T(128)} %bitcast.zh_ref, bf16[2,32,768]{2,1,0:T(8,128)(2,1)} %copy-done.4, bf16[4,2,32,768]{3,2,1,0:T(8,128)(2,1)} %get-tuple-element.16.states_ref, f32[4,4,32,128]{3,2,1,0:T(8,128)} %get-tuple-element.17.weights_ref, f32[4,32,128]{2,1,0:T(8,128)} %get-tuple-element.18.rscale_ref, ...), custom_call_target="tpu_custom_call" | custom-call | tf_op jit(solution)/shard_map/pallas_call | solution.py:180
  253.9 10.0 %all_to_all.30.dlogits_ref = bf16[4,32,128]{2,1,0:T(8,128)(2,1)} all-to-all(bf16[4,32,128]{2,1,0:T(8,128)(2,1)} %shard_map.88), channel_id=1, replica_groups=mesh['zh'=2,'x'=4,'z'=8,'yc'=8] {'x'}, dimensions={0} | all-to-all | bytes 65536 | tf_op jit(solution)/shard_map/all_to_all | solution.py:294
  264.0 0.0 copy-done.3
  264.0 10.4 %all_to_all.31.normed_ref = bf16[4,2,32,768]{3,2,1,0:T(8,128)(2,1)} all-to-all(bf16[4,2,32,768]{3,2,1,0:T(8,128)(2,1)S(1)} %copy-done.3), channel_id=1, replica_groups=mesh['zh'=2,'x'=4,'z'=8,'yc'=8] {'x'}, dimensions={0} | all-to-all | bytes 786432 | tf_op jit(solution)/shard_map/normed_exchange/all_to_all | solution.py:288
  274.4 2.2 shard_map.89
  276.6 17.0 %all_to_all.32 = f32[8,192,128]{2,1,0:T(8,128)S(1)} all-to-all(f32[8,192,128]{2,1,0:T(8,128)} %shard_map.89), channel_id=1, replica_groups=mesh['zh'=2,'x'=4,'z'=8,'yc'=8] {'yc'}, dimensions={0} | all-to-all | bytes 1572864 | tf_op jit(solution)/shard_map/all_to_all | solution.py:304
  293.6 0.7 reduce_sum.39
  294.3 9.0 %all-to-all-start.5 = ((f32[8,24,128]{2,1,0:T(8,128)}), f32[8,24,128]{2,1,0:T(8,128)S(1)}, u32[]{:S(2)}, u32[]{:S(2)}) async-start(f32[8,24,128]{2,1,0:T(8,128)} %bitcast.9), calls=%async_computation.5 | async-start | bytes 196608 | tf_op jit(solution)/shard_map/all_to_all | solution.py:306
  303.3 11.2 %all-to-all-done.5 = f32[8,24,128]{2,1,0:T(8,128)S(1)} async-done(((f32[8,24,128]{2,1,0:T(8,128)}), f32[8,24,128]{2,1,0:T(8,128)S(1)}, u32[]{:S(2)}, u32[]{:S(2)}) %all-to-all-start.5) | async-done | bytes 98336 | tf_op jit(solution)/shard_map/all_to_all | solution.py:306
  314.5 0.0 copy-start.6
  314.5 0.8 fusion.6
  315.3 1.3 bitcast_divide_fusion
  (17 shorter events, 0.2 us)
Async XLA Ops:
  1.5 19.9 %collective-permute-start = (bf16[4,32,192]{2,1,0:T(8,128)(2,1)S(1)}, bf16[4,32,192]{2,1,0:T(8,128)(2,1)S(1)}, u32[]{:S(2)}, u32[]{:S(2)}) collective-permute-start(bf16[4,32,192]{2,1,0:T(8,128)(2,1)S(1)} %broadcast_select_fusion), channel_id=1, source_target_pairs={{0,256},{256,0},{1,257},{257,1},{2,258},{258,2},{3,259},{259,3},{4... | collective-permute-start | bytes 147464 | tf_op jit(solution)/shard_map/ppermute | solution.py:219
  24.2 5.5 %copy-start.1 = (bf16[1,4,2,64,2,1536]{5,4,3,2,1,0:T(2,128)(2,1)S(1)}, bf16[1,4,2,64,2,1536]{5,4,3,2,1,0:T(2,128)(2,1)}, u32[]{:S(2)}) copy-start(bf16[1,4,2,64,2,1536]{5,4,3,2,1,0:T(2,128)(2,1)} %param.9) | copy-start | bytes 9437188
  24.2 24.0 %all-to-all-start.1 = ((bf16[4,1680,128]{2,1,0:T(8,128)(2,1)}), bf16[4,1680,128]{2,1,0:T(8,128)(2,1)}, u32[]{:S(2)}, u32[]{:S(2)}) async-start(bf16[4,1680,128]{2,1,0:T(8,128)(2,1)} %fusion.2), calls=%async_computation.1 | async-start | bytes 3440640 | tf_op jit(solution)/shard_map/small_exchange/all_to_all | solution.py:240
  48.3 160.5 %all-to-all-start = ((bf16[256,8,768]{2,1,0:T(8,128)(2,1)}), bf16[256,8,768]{2,1,0:T(8,128)(2,1)S(1)}, u32[]{:S(2)}, u32[]{:S(2)}) async-start(bf16[256,8,768]{2,1,0:T(8,128)(2,1)} %reshape.100), calls=%async_computation | async-start | bytes 6291456 | tf_op jit(solution)/shard_map/rows_exchange/all_to_all | solution.py:224
  70.5 6.4 %copy-start.2 = (s32[4,32,4]{2,1,0:T(8,128)}, s32[4,32,4]{2,1,0:T(8,128)S(1)}, u32[]{:S(2)}) copy-start(s32[4,32,4]{2,1,0:T(8,128)S(1)} %convert_element_type.82.routes_ref) | copy-start | bytes 6148
  208.8 1.6 copy-start
  210.4 12.9 %copy-start.7 = (f32[1536]{0:T(1024)S(1)}, f32[1536]{0:T(1024)}, u32[]{:S(2)}) copy-start(f32[1536]{0:T(1024)} %param.13) | copy-start | bytes 18436
  217.6 8.1 %collective-permute-start.1 = (bf16[2,32,768]{2,1,0:T(8,128)(2,1)}, bf16[2,32,768]{2,1,0:T(8,128)(2,1)S(1)}, u32[]{:S(2)}, u32[]{:S(2)}) collective-permute-start(bf16[2,32,768]{2,1,0:T(8,128)(2,1)} %get-tuple-element.11), channel_id=1, source_target_pairs={{0,256},{1,257},{2,258},{3,259},{4,260},{5,261},{6,262},{7,263},{8... | collective-permute-start | bytes 294920 | tf_op jit(solution)/shard_map/ppermute | solution.py:271
  225.8 0.6 copy-start.5
  229.3 19.3 %collective-permute-start.2 = (bf16[2,32,768]{2,1,0:T(8,128)(2,1)}, bf16[2,32,768]{2,1,0:T(8,128)(2,1)S(1)}, u32[]{:S(2)}, u32[]{:S(2)}) collective-permute-start(bf16[2,32,768]{2,1,0:T(8,128)(2,1)} %get-tuple-element.15), channel_id=1, source_target_pairs={{256,0},{257,1},{258,2},{259,3},{260,4},{261,5},{262,6},{263,7},{2... | collective-permute-start | bytes 294920 | tf_op jit(solution)/shard_map/ppermute | solution.py:286
  248.6 0.6 copy-start.4
  249.3 14.7 %copy-start.3 = (bf16[4,2,32,768]{3,2,1,0:T(8,128)(2,1)S(1)}, bf16[4,2,32,768]{3,2,1,0:T(8,128)(2,1)}, u32[]{:S(2)}) copy-start(bf16[4,2,32,768]{3,2,1,0:T(8,128)(2,1)} %get-tuple-element.14) | copy-start | bytes 1179652
  294.3 20.2 %all-to-all-start.5 = ((f32[8,24,128]{2,1,0:T(8,128)}), f32[8,24,128]{2,1,0:T(8,128)S(1)}, u32[]{:S(2)}, u32[]{:S(2)}) async-start(f32[8,24,128]{2,1,0:T(8,128)} %bitcast.9), calls=%async_computation.5 | async-start | bytes 196608 | tf_op jit(solution)/shard_map/all_to_all | solution.py:306
  314.5 2.1 copy-start.6

commit v2 on v1

--- a/solution.py
+++ b/solution.py
@@ -6,6 +6,7 @@
 from jax.experimental import pallas as pl
 from jax.experimental.pallas import tpu as pltpu
 from jax.sharding import Mesh, PartitionSpec as P
+
 
 EPSILON = 1e-05
 HALVES = 2
@@ -142,7 +143,7 @@
 
 def last_kernel(
     zh_ref, arrived_ref, states_ref, weights_ref, rscale_ref, picks_ref, routes_ref, w_ref, gain_ref,
-    given_ref, dlogits_ref,
+    given_ref, copies_ref, dlogits_ref,
 ):
     layers = picks_ref.shape[0]
 
@@ -158,20 +159,33 @@
             state = [states_ref[layer, h] for h in range(HALVES)]
             back = backward_layer(layer, back, state, refs, weights_ref, rscale_ref, dlogits_ref)
 
-
-def grad_kernel(planes, normed_ref, dlogits_ref, out_ref):
-    micros, _, tokens, half = normed_ref.shape
+    for layer in range(layers):
+        for group in range(copies_ref.shape[1]):
+            copies_ref[layer, group] = dlogits_ref[layer]
+
+
+def spread_kernel(normed_ref, order_ref, out_ref):
+    layers, halves, tokens, half = normed_ref.shape
+    rows = normed_ref[...].reshape(layers * halves * tokens, half)
+    moved = jnp.dot(rows, order_ref[...], preferred_element_type=F32).astype(BF16)
+    for layer in range(layers):
+        for h in range(halves):
+            at = (layer * halves + h) * tokens
+            for group in range(out_ref.shape[1]):
+                out_ref[layer, group, h] = moved[at : at + tokens, group * 128 : (group + 1) * 128]
+
+
+def grad_kernel(normed_ref, dlogits_ref, out_ref):
+    sources, halves, tokens, lanes = normed_ref.shape
     experts = dlogits_ref.shape[2]
-    groups, per_group = out_ref.shape[:2]
-    piece = per_group // planes
-    dlogits = dlogits_ref[...].reshape(micros * tokens, experts)
-    for h in range(HALVES):
-        rows = jnp.concatenate([normed_ref[m, h] for m in range(micros)], axis=0)
-        term = lax.dot_general(rows, dlogits, (((0,), (0,)), ((), ())), preferred_element_type=F32)
-        for at in range(0, half, piece):
-            owner = (h * half + at) // piece
-            plane, group = owner // groups, owner % groups
-            out_ref[group, plane * piece : (plane + 1) * piece, :] = term[at : at + piece]
+    planes, rows = out_ref.shape[:2]
+    dlogits = dlogits_ref[...].reshape(sources * tokens, experts)
+    per_half = planes // halves
+    for h in range(halves):
+        normed = normed_ref[:, h].reshape(sources * tokens, lanes)
+        term = lax.dot_general(normed, dlogits, (((0,), (0,)), ((), ())), preferred_element_type=F32)
+        for plane in range(per_half):
+            out_ref[h * per_half + plane] = term[plane * rows : (plane + 1) * rows]
 
 
 def call(kernel, outs, args, scratch=(), scalars=1):
@@ -197,15 +211,29 @@
 
 
 def thirds(values):
-    high = values.astype(BF16)
-    rest = values - high.astype(F32)
-    middle = rest.astype(BF16)
-    return jnp.stack([high, middle, (rest - middle.astype(F32)).astype(BF16)])
-
-
-def per_device(expert_axes, plane_axis, flat_axes, inputs, cotangent, expert_out, route_ids, router_w, norm_gain, final_gain):
+    high = lax.reduce_precision(values, 8, 7)
+    middle = lax.reduce_precision(values - high, 8, 7)
+    return jnp.stack([high, middle, values - high - middle]).astype(BF16)
+
+
+def from_all(shared, given, axis):
+    count, here = lax.axis_size(axis), lax.axis_index(axis)
+    slots = []
+    for shift in range(count):
+        mine = lax.dynamic_index_in_dim(given, (here + shift) % count, 0, keepdims=False)
+        block = jnp.concatenate([shared, mine], axis=0)
+        if shift:
+            block = lax.ppermute(block, axis, [(source, (source + shift) % count) for source in range(count)])
+        slots.append(block)
+    slots = jnp.stack(slots)
+    return jnp.concatenate(
+        [lax.dynamic_slice_in_dim(slots, (here - source) % count, 1, 0) for source in range(count)]
+    )
+
+
+def compute(expert_axes, plane_axis, flat_axes, inputs, cotangent, expert_out, route_ids, router_w, norm_gain, final_gain):
     zh = lax.axis_index("zh")
-    micros, tokens, piece = inputs.shape
+    micros, tokens, part = inputs.shape
     layers = lax.axis_size("x")
     owners = lax.axis_size(expert_axes)
     local_experts, capacity, width = expert_out.shape[2], expert_out.shape[4], expert_out.shape[5]
@@ -220,31 +248,29 @@
 
     rows = expert_out[0].reshape(micros, local_experts, owners, capacity, HALVES, half)
     rows = rows.transpose(0, 2, 1, 4, 3, 5).reshape(micros * owners, local_experts * HALVES * capacity, half)
-    with jax.named_scope("rows_exchange"):
-        table = lax.all_to_all(rows, ("x",) + expert_axes, split_axis=0, concat_axis=0, tiled=True)
+    rows, router_here, gain_here, routes_here = lax.optimization_barrier(
+        (rows, router_w[0], norm_gain[0], route_ids[0])
+    )
+    table = lax.all_to_all(rows, ("x",) + expert_axes, split_axis=0, concat_axis=0, tiled=True)
     table = table.reshape(layers, experts * HALVES * capacity, half)
 
     lower = jnp.where(zh == 0, kept, crossed)
     upper = jnp.where(zh == 0, crossed, kept)
-    acts_part = jnp.stack([lower, upper], axis=2).reshape(micros, tokens * HALVES * piece // 128, 128)
+    acts_part = jnp.stack([lower, upper], axis=2).reshape(micros, tokens * HALVES * part // 128, 128)
     act_rows = acts_part.shape[1]
-    route_part = route_ids[0].astype(BF16).reshape(micros, tokens * choices // 128, 128)
+    route_part = routes_here.astype(BF16).reshape(micros, tokens * choices // 128, 128)
     route_rows = route_part.shape[1]
     route_part = jnp.pad(route_part, ((0, 0), (0, 8 - route_rows), (0, 0)))
-    gain_part = thirds(norm_gain[0]).reshape(3 * width // 128, 128)
+    gain_part = thirds(gain_here).reshape(3 * width // 128, 128)
     gain_rows = gain_part.shape[0]
     gain_part = jnp.pad(gain_part, ((0, -gain_rows % 8), (0, 0)))
-    shared = jnp.concatenate([router_w[0], gain_part], axis=0)
-    shared = jnp.broadcast_to(shared[None], (layers,) + shared.shape)
-    with jax.named_scope("small_exchange"):
-        packed = lax.all_to_all(
-            jnp.concatenate([shared, acts_part, route_part], axis=1), "x", split_axis=0, concat_axis=0, tiled=True
-        )
+    shared = jnp.concatenate([router_here, gain_part], axis=0)
+    packed = from_all(shared, jnp.concatenate([acts_part, route_part], axis=1), "x")
     w_all = packed[:, :width]
     gain_all = packed[:, width : width + gain_rows].reshape(layers, 3, width).astype(F32)
     gain_all = (gain_all[:, 0] + gain_all[:, 1] + gain_all[:, 2]).reshape(layers, HALVES, half)
-    at = shared.shape[1]
-    acts = packed[:, at : at + act_rows].reshape(layers, tokens, HALVES, piece)
+    at = shared.shape[0]
+    acts = packed[:, at : at + act_rows].reshape(layers, tokens, HALVES, part)
     acts = acts.transpose(2, 1, 0, 3).reshape(HALVES, tokens, half)
     at += act_rows
     routes = packed[:, at : at + route_rows].reshape(layers, tokens, choices).astype(F32).astype(jnp.int32)
@@ -253,6 +279,13 @@
     target = target.transpose(0, 2, 1)[:, None] + (jnp.arange(HALVES) * capacity)[None, :, None, None]
     target = target.reshape(layers, HALVES * choices * tokens, 1)
     select = (target == jnp.arange(experts * HALVES * capacity)[None, None, :]).astype(BF16)
+
+    planes = lax.axis_size(plane_axis)
+    groups = owners // planes
+    piece = width // owners
+    feature = jnp.arange(half)
+    place = feature // piece % groups * 128 + feature // (piece * groups) * piece + feature % piece
+    order = (place[:, None] == jnp.arange(groups * 128)[None, :]).astype(BF16)
 
     shape = jax.ShapeDtypeStruct
     rows_shape = (HALVES, tokens, half)
@@ -284,25 +317,20 @@
         ),
     )
     arrived = lax.ppermute(sent, "zh", [(1, 0)])
-    with jax.named_scope("normed_exchange"):
-        normed = lax.all_to_all(normed, "x", split_axis=0, concat_axis=0, tiled=True)
-    dlogits = call(
+    normed = call(
+        spread_kernel, shape((layers, groups, HALVES, tokens, 128), BF16), (normed, order), scalars=0
+    )
+    normed = normed.reshape(layers * groups, HALVES, tokens, 128)
+    normed = lax.all_to_all(normed, ("x",) + flat_axes, split_axis=0, concat_axis=0, tiled=True)
+    arrived, normed = lax.optimization_barrier((arrived, normed))
+    dlogits, _ = call(
         last_kernel,
-        shape((layers, tokens, experts), BF16),
+        (shape((layers, groups, tokens, experts), BF16), shape((layers, tokens, experts), BF16)),
         (zh_word, arrived, states, weights, rscale, picks, routes, w_all, gain_all, dlogits),
     )
-    dlogits = lax.all_to_all(dlogits, "x", split_axis=0, concat_axis=0, tiled=True)
-
-    planes = lax.axis_size(plane_axis)
-    groups = owners // planes
-    term = call(
-        functools.partial(grad_kernel, planes),
-        shape((groups, width // groups, experts), F32),
-        (normed, dlogits),
-        scalars=0,
-    )
-    term = lax.all_to_all(term, flat_axes, split_axis=0, concat_axis=0, tiled=True)
-    term = jnp.sum(term, axis=0).reshape(planes, width // owners, experts)
+    dlogits = dlogits.reshape(layers * groups, tokens, experts)
+    dlogits = lax.all_to_all(dlogits, ("x",) + flat_axes, split_axis=0, concat_axis=0, tiled=True)
+    term = call(grad_kernel, shape((planes, piece, experts), F32), (normed, dlogits), scalars=0)
     term = lax.all_to_all(term, plane_axis, split_axis=0, concat_axis=0, tiled=True)
     router_part = jnp.sum(term, axis=0)
     at = lax.axis_index(expert_axes) * (width // owners)
@@ -314,8 +342,8 @@
 
 def solution(mesh):
     sections, owners = mesh.shape["section"], mesh.shape["expert"]
-    planes = 8 if owners % 8 == 0 and owners > 8 else owners // 2
-    groups = owners // planes
+    groups = 8
+    planes = owners // groups
     wide = Mesh(mesh.devices.reshape(HALVES, sections // HALVES, planes, groups), ("zh", "x", "z", "yc"))
     section, expert = ("zh", "x"), ("z", "yc")
     placed = (
@@ -328,7 +356,7 @@
         P(),
     )
     return jax.shard_map(
-        functools.partial(per_device, expert, "z", "yc"),
+        functools.partial(compute, expert, "z", ("yc",)),
         mesh=wide,
         in_specs=placed,
         out_specs=(P(section, expert, None), P(section, expert)),

time: 318 us -> 313 us (0.984)
  starting transfers between devices: 57.3 us -> 92.8 us
  waiting for transfers between devices: 171 us -> 144 us
  blocking collectives: 37.5 us -> 14.4 us
  local copies, waits for them, and re-layouts: 21.2 us -> 26.5 us
    all_to_all x3, waiting for transfers between devices: 149 us -> 45 us  [the longest x1 33.4 us: compute(): lax.all_to_all(rows, ('x',) + expert_axes, split_axis=0, concat_axis=0, t...]
    ppermute x3 -> x6, waiting for transfers between devices: 21.3 us -> 98.6 us  [the longest x1 58.7 us: compute(): crossed = lax.ppermute(crossing, 'zh', [(0, 1), (1, 0)])]
    all_to_all x3, starting transfers between devices: 34.6 us -> 68.4 us  [the longest x1 38.9 us: compute(): lax.all_to_all(term, plane_axis, split_axis=0, concat_axis=0, tiled=True)]
    all_to_all x3 -> x1, blocking collectives: 37.5 us -> 14.4 us  [compute(): lax.all_to_all(dlogits, ('x',) + flat_axes, split_axis=0, concat_axis=0,...]
    another operation x2 -> x5, local copies, waits for them, and re-layouts: 3.42 us -> 9.39 us  [the longest x1 9.23 us: compute(): expert_out[0].reshape(micros, local_experts, owners, capacity, HALVES, half)]
    another operation x3 -> x6, other arithmetic: 0.91 us -> 4.16 us  [the longest x2 4.08 us: from_all(): slots = jnp.stack(slots)]
    pallas_call x4 -> x5, Pallas kernels: 17 us -> 19.8 us  [call(): pl.pallas_call(kernel, out_shape=outs, in_specs=smem + [vmem] * (len(args...]
    ppermute x3 -> x6, starting transfers between devices: 22.6 us -> 24.4 us  [the longest x3 8.4 us: from_all(): lax.ppermute(block, axis, [(source, (source + shift) % count) for source...]
  transfers between devices with their start and end apart: 6 -> 9, of which waited for: 6 -> 8; matrix products, arithmetic and copies ran while one was open for 8% -> 5% of each run, Pallas kernels for 0% -> 0%
where the time goes in v2:
time: 313 us; the launch traced here: 311 us
  waiting for transfers between devices  144 us (46%)
  starting transfers between devices  92.8 us (30%)
  local copies, waits for them, and re-layouts  26.5 us (8%)
  Pallas kernels  19.8 us (6%)
  blocking collectives  14.4 us (5%)
  other arithmetic  12.5 us (4%)
    ppermute x1, waiting for transfers between devices, compute(): crossed = lax.ppermute(crossing, 'zh', [(0, 1), (1, 0)])  58.7 us
    all_to_all x1, starting transfers between devices, compute(): lax.all_to_all(term, plane_axis, split_axis=0, concat_axis=0, tiled=True)  38.9 us
    all_to_all x1, waiting for transfers between devices, compute(): lax.all_to_all(rows, ('x',) + expert_axes, split_axis=0, concat_axis=0, t...  33.4 us
    all_to_all x1, starting transfers between devices, compute(): lax.all_to_all(rows, ('x',) + expert_axes, split_axis=0, concat_axis=0, t...  22.3 us
    ppermute x3, waiting for transfers between devices, from_all(): lax.ppermute(block, axis, [(source, (source + shift) % count) for source...  21.3 us
    pallas_call x5, Pallas kernels, call(): pl.pallas_call(kernel, out_shape=outs, in_specs=smem + [vmem] * (len(args...  19.8 us
    ppermute x1, waiting for transfers between devices, compute(): arrived = lax.ppermute(sent, 'zh', [(1, 0)])  18.2 us
    all_to_all x1, blocking collectives, compute(): lax.all_to_all(dlogits, ('x',) + flat_axes, split_axis=0, concat_axis=0,...  14.4 us
  transfers between devices with their start and end apart: 9, of which 8 were waited for; matrix products, arithmetic and copies ran while one was open for 5% of the time, Pallas kernels for 0%

profile of v2, /device:TPU:6, one launch (start us, length us, event | category | flops | bytes accessed | tf_op | source)
XLA Modules:
  0.0 310.9 jit_solution(15055679122639377354)
XLA Ops:
  0.6 9.2 %reshape_squeeze.3 = bf16[4,2,64,2,2,768]{5,4,3,2,1,0:T(2,128)(2,1)} reshape(bf16[1,4,2,64,2,1536]{5,4,3,2,1,0:T(2,128)(2,1)} %param.9) | data formatting | bytes 6291456 | tf_op jit(solution)/shard_map/reshape;squeeze | solution.py:249
  9.9 5.1 %copy.21 = bf16[4,64,2,2,2,768]{5,4,3,2,1,0:T(2,128)(2,1)S(1)} copy(bf16[4,64,2,2,2,768]{5,3,4,1,2,0:T(2,128)(2,1)} %bitcast.35) | data formatting | bytes 6291456 | tf_op jit(solution)/shard_map/transpose | solution.py:250
  15.0 0.0 copy-start.14
  15.0 2.7 reshape.133
  17.8 0.0 copy-start.13
  17.8 22.3 %all-to-all-start = ((bf16[256,8,768]{2,1,0:T(8,128)(2,1)}), bf16[256,8,768]{2,1,0:T(8,128)(2,1)S(1)}, u32[]{:S(2)}, u32[]{:S(2)}) async-start(bf16[256,8,768]{2,1,0:T(8,128)(2,1)} %reshape.133), calls=%async_computation | async-start | bytes 6291456 | tf_op jit(solution)/shard_map/all_to_all | solution.py:254
  40.1 8.2 %collective-permute-start = (bf16[4,32,192]{2,1,0:T(8,128)(2,1)S(1)}, bf16[4,32,192]{2,1,0:T(8,128)(2,1)S(1)}, u32[]{:S(2)}, u32[]{:S(2)}) collective-permute-start(bf16[4,32,192]{2,1,0:T(8,128)(2,1)S(1)} %broadcast_select_fusion), channel_id=1, source_target_pairs={{0,256},{256,0},{1,257},{257,1},{2,258},{258,2},{3,259},{259,3},{4... | collective-permute-start | bytes 147464 | tf_op jit(solution)/shard_map/ppermute | solution.py:247
  48.5 0.1 copy.23
  48.6 0.1 reshape.145
  48.8 58.7 %collective-permute-done = bf16[4,32,192]{2,1,0:T(8,128)(2,1)S(1)} collective-permute-done((bf16[4,32,192]{2,1,0:T(8,128)(2,1)S(1)}, bf16[4,32,192]{2,1,0:T(8,128)(2,1)S(1)}, u32[]{:S(2)}, u32[]{:S(2)}) %collective-permute-start) | collective-permute-done | bytes 49184 | tf_op jit(solution)/shard_map/ppermute | solution.py:247
  107.6 0.1 copy.22
  107.7 0.2 reshape.135
  107.9 2.5 maximum_bitcast_fusion
  110.4 1.9 collective-permute-start.1
  112.3 4.4 %collective-permute-start.2 = (bf16[1680,128]{1,0:T(8,128)(2,1)}, bf16[1680,128]{1,0:T(8,128)(2,1)}, u32[]{:S(2)}, u32[]{:S(2)}) collective-permute-start(bf16[1680,128]{1,0:T(8,128)(2,1)} %get-tuple-element.42), channel_id=1, source_target_pairs={{0,128},{64,192},{128,0},{192,64},{1,129},{65,193},{129,1},{193,65... | collective-permute-start | bytes 1290248 | tf_op jit(solution)/shard_map/ppermute | solution.py:226
  116.7 2.1 collective-permute-start.3
  118.9 0.1 add.169
  119.0 0.1 add.170
  119.1 8.1 %collective-permute-done.1 = bf16[1680,128]{1,0:T(8,128)(2,1)} collective-permute-done((bf16[1680,128]{1,0:T(8,128)(2,1)}, bf16[1680,128]{1,0:T(8,128)(2,1)}, u32[]{:S(2)}, u32[]{:S(2)}) %collective-permute-start.1) | collective-permute-done | bytes 430112 | tf_op jit(solution)/shard_map/ppermute | solution.py:226
  127.2 4.4 %collective-permute-done.2 = bf16[1680,128]{1,0:T(8,128)(2,1)} collective-permute-done((bf16[1680,128]{1,0:T(8,128)(2,1)}, bf16[1680,128]{1,0:T(8,128)(2,1)}, u32[]{:S(2)}, u32[]{:S(2)}) %collective-permute-start.2) | collective-permute-done | bytes 430112 | tf_op jit(solution)/shard_map/ppermute | solution.py:226
  131.6 8.8 %collective-permute-done.3 = bf16[1680,128]{1,0:T(8,128)(2,1)} collective-permute-done((bf16[1680,128]{1,0:T(8,128)(2,1)}, bf16[1680,128]{1,0:T(8,128)(2,1)}, u32[]{:S(2)}, u32[]{:S(2)}) %collective-permute-start.3) | collective-permute-done | bytes 430112 | tf_op jit(solution)/shard_map/ppermute | solution.py:226
  140.4 1.6 pad_maximum_fusion
  142.0 0.1 constant_dynamic-slice_fusion.4
  142.2 0.7 copy-done.1
  143.0 0.1 copy-done.2
  143.1 0.2 copy-done.3
  143.2 0.2 copy-done.4
  143.4 0.1 reshape.138
  143.5 0.1 copy.26
  143.6 0.8 reshape.139.acts_ref
  144.4 0.8 maximum_convert_fusion
  145.2 0.1 fusion.7
  145.3 0.6 add.175.gain_ref
  145.9 1.6 pad_maximum_fusion.1
  147.5 1.3 slice.28.w_ref
  148.8 0.5 broadcast.152
  149.3 1.4 fusion.26
  150.7 0.2 select_reduce_fusion
  150.9 0.1 reshape.137
  151.0 0.1 convert_element_type.51.routes_ref
  151.2 0.1 copy.25
  151.3 0.1 add.168
  151.4 1.2 fusion.1.select_ref
  152.6 33.4 %all-to-all-done = bf16[256,8,768]{2,1,0:T(8,128)(2,1)S(1)} async-done(((bf16[256,8,768]{2,1,0:T(8,128)(2,1)}), bf16[256,8,768]{2,1,0:T(8,128)(2,1)S(1)}, u32[]{:S(2)}, u32[]{:S(2)}) %all-to-all-start) | async-done | bytes 3145760 | tf_op jit(solution)/shard_map/all_to_all | solution.py:254
  186.0 1.6 copy-done
  187.7 7.1 %shard_map.86 = (bf16[4,2,4,32,768]{4,3,2,1,0:T(8,128)(2,1)}, bf16[4,2,32,768]{3,2,1,0:T(8,128)(2,1)}, bf16[4,2,32,768]{3,2,1,0:T(8,128)(2,1)}, f32[4,4,32,128]{...) custom-call(s32[1]{0:T(128)} %bitcast.zh_ref, bf16[4,512,768]{2,1,0:T(8,128)(2,1)} %bitcast.34, ...), custom_call_target="tpu_custom_call" | custom-call | tf_op jit(solution)/shard_map/pallas_call | solution.py:194
  194.7 6.5 %collective-permute-start.4 = (bf16[2,32,768]{2,1,0:T(8,128)(2,1)}, bf16[2,32,768]{2,1,0:T(8,128)(2,1)S(1)}, u32[]{:S(2)}, u32[]{:S(2)}) collective-permute-start(bf16[2,32,768]{2,1,0:T(8,128)(2,1)} %get-tuple-element.22), channel_id=1, source_target_pairs={{0,256},{1,257},{2,258},{3,259},{4,260},{5,261},{6,262},{7,263},{8... | collective-permute-start | bytes 294920 | tf_op jit(solution)/shard_map/ppermute | solution.py:304
  201.2 1.5 fusion.order_ref
  202.7 0.6 reshape.140.final_ref
  203.3 0.4 collective-permute-done.4.arrived_ref
  203.7 0.6 copy-done.10
  204.3 2.9 shard_map.87
  207.3 3.0 shard_map.88
  210.2 7.3 %all-to-all-start.1 = ((bf16[32,2,32,128]{3,2,1,0:T(8,128)(2,1)}), bf16[32,2,32,128]{3,2,1,0:T(8,128)(2,1)S(1)}, u32[]{:S(2)}, u32[]{:S(2)}) async-start(bf16[32,2,32,128]{3,2,1,0:T(8,128)(2,1)} %bitcast.36), calls=%async_computation.1 | async-start | bytes 1048576 | tf_op jit(solution)/shard_map/all_to_all | solution.py:324
  217.6 1.3 collective-permute-start.5
  218.9 18.2 %collective-permute-done.5.arrived_ref = bf16[2,32,768]{2,1,0:T(8,128)(2,1)S(1)} collective-permute-done((bf16[2,32,768]{2,1,0:T(8,128)(2,1)S(1)}, bf16[2,32,768]{2,1,0:T(8,128)(2,1)S(1)}, u32[]{:S(2)}, u32[]{:S(2)}) %collective-permute-start.5) | collective-permute-done | bytes 98336 | tf_op jit(solution)/shard_map/ppermute | solution.py:319
  237.0 0.6 copy-done.9
  237.7 4.8 %shard_map.89 = (bf16[4,8,32,128]{3,2,1,0:T(8,128)(2,1)}, bf16[4,32,128]{2,1,0:T(8,128)(2,1)}) custom-call(s32[1]{0:T(128)} %bitcast.zh_ref, bf16[2,32,768]{2,1,0:T(8,128)(2,1)} %copy-done.9, bf16[4,2,32,768]{3,2,1,0:T(8,128)(2,1)} %get-tuple-element.29.states_ref, f32[4,4,32,128]{3,2,1,0:T(8,128)} %get-tuple-element.30.weights_ref, ...), custom_call_target="tpu_custom_call" | custom-call | tf_op jit(solution)/shard_map/pallas_call | solution.py:194
  242.4 14.4 %all_to_all.20.dlogits_ref = bf16[32,32,128]{2,1,0:T(8,128)(2,1)} all-to-all(bf16[32,32,128]{2,1,0:T(8,128)(2,1)} %bitcast.39), channel_id=1, replica_groups=mesh['zh'=2,'x'=4,'z'=8,'yc'=8] {'x','yc'}, dimensions={0} | all-to-all | bytes 524288 | tf_op jit(solution)/shard_map/all_to_all | solution.py:332
  256.9 2.1 shard_map.90
  259.0 38.9 %all-to-all-start.3 = ((f32[8,24,128]{2,1,0:T(8,128)}), f32[8,24,128]{2,1,0:T(8,128)S(1)}, u32[]{:S(2)}, u32[]{:S(2)}) async-start(f32[8,24,128]{2,1,0:T(8,128)} %shard_map.90), calls=%async_computation.3 | async-start | bytes 196608 | tf_op jit(solution)/shard_map/all_to_all | solution.py:334
  297.8 11.6 %all-to-all-done.3 = f32[8,24,128]{2,1,0:T(8,128)S(1)} async-done(((f32[8,24,128]{2,1,0:T(8,128)}), f32[8,24,128]{2,1,0:T(8,128)S(1)}, u32[]{:S(2)}, u32[]{:S(2)}) %all-to-all-start.3) | async-done | bytes 98336 | tf_op jit(solution)/shard_map/all_to_all | solution.py:334
  309.4 0.8 fusion.8
  310.3 0.6 fusion.25
  (46 shorter events, 0.4 us)
Async XLA Ops:
  15.0 2.7 copy-start.14
  17.7 22.3 %copy-start.7 = (bf16[4,32,192]{2,1,0:T(8,128)(2,1)S(1)}, bf16[4,32,192]{2,1,0:T(8,128)(2,1)}, u32[]{:S(2)}) copy-start(bf16[4,32,192]{2,1,0:T(8,128)(2,1)} %param.8) | copy-start | bytes 147460
  17.7 22.3 %copy-start.8 = (bf16[4,32,192]{2,1,0:T(8,128)(2,1)S(1)}, bf16[4,32,192]{2,1,0:T(8,128)(2,1)}, u32[]{:S(2)}) copy-start(bf16[4,32,192]{2,1,0:T(8,128)(2,1)} %param.7) | copy-start | bytes 147460
  17.8 30.7 %copy-start.13 = (s32[1,4,32,4]{2,3,1,0:T(4,128)S(1)}, s32[1,4,32,4]{2,3,1,0:T(4,128)}, u32[]{:S(2)}) copy-start(s32[1,4,32,4]{2,3,1,0:T(4,128)} %param.10) | copy-start | bytes 6148
  17.8 168.3 %all-to-all-start = ((bf16[256,8,768]{2,1,0:T(8,128)(2,1)}), bf16[256,8,768]{2,1,0:T(8,128)(2,1)S(1)}, u32[]{:S(2)}, u32[]{:S(2)}) async-start(bf16[256,8,768]{2,1,0:T(8,128)(2,1)} %reshape.133), calls=%async_computation | async-start | bytes 6291456 | tf_op jit(solution)/shard_map/all_to_all | solution.py:254
  40.1 67.4 %collective-permute-start = (bf16[4,32,192]{2,1,0:T(8,128)(2,1)S(1)}, bf16[4,32,192]{2,1,0:T(8,128)(2,1)S(1)}, u32[]{:S(2)}, u32[]{:S(2)}) collective-permute-start(bf16[4,32,192]{2,1,0:T(8,128)(2,1)S(1)} %broadcast_select_fusion), channel_id=1, source_target_pairs={{0,256},{256,0},{1,257},{257,1},{2,258},{258,2},{3,259},{259,3},{4... | collective-permute-start | bytes 147464 | tf_op jit(solution)/shard_map/ppermute | solution.py:247
  110.4 16.8 %collective-permute-start.1 = (bf16[1680,128]{1,0:T(8,128)(2,1)}, bf16[1680,128]{1,0:T(8,128)(2,1)}, u32[]{:S(2)}, u32[]{:S(2)}) collective-permute-start(bf16[1680,128]{1,0:T(8,128)(2,1)} %get-tuple-element.41), channel_id=1, source_target_pairs={{0,64},{64,128},{128,192},{192,0},{1,65},{65,129},{129,193},{193,1... | collective-permute-start | bytes 1290248 | tf_op jit(solution)/shard_map/ppermute | solution.py:226
  112.3 19.3 %collective-permute-start.2 = (bf16[1680,128]{1,0:T(8,128)(2,1)}, bf16[1680,128]{1,0:T(8,128)(2,1)}, u32[]{:S(2)}, u32[]{:S(2)}) collective-permute-start(bf16[1680,128]{1,0:T(8,128)(2,1)} %get-tuple-element.42), channel_id=1, source_target_pairs={{0,128},{64,192},{128,0},{192,64},{1,129},{65,193},{129,1},{193,65... | collective-permute-start | bytes 1290248 | tf_op jit(solution)/shard_map/ppermute | solution.py:226
  116.7 23.7 %collective-permute-start.3 = (bf16[1680,128]{1,0:T(8,128)(2,1)}, bf16[1680,128]{1,0:T(8,128)(2,1)}, u32[]{:S(2)}, u32[]{:S(2)}) collective-permute-start(bf16[1680,128]{1,0:T(8,128)(2,1)} %get-tuple-element.43), channel_id=1, source_target_pairs={{0,192},{64,0},{128,64},{192,128},{1,193},{65,1},{129,65},{193,129... | collective-permute-start | bytes 1290248 | tf_op jit(solution)/shard_map/ppermute | solution.py:226
  142.2 0.8 copy-start.1
  142.2 0.9 copy-start.2
  142.2 1.0 copy-start.3
  142.2 1.2 copy-start.4
  151.1 34.9 %copy-start.6 = (s32[4,32,4]{2,1,0:T(8,128)}, s32[4,32,4]{2,1,0:T(8,128)S(1)}, u32[]{:S(2)}) copy-start(s32[4,32,4]{2,1,0:T(8,128)S(1)} %convert_element_type.51.routes_ref) | copy-start | bytes 6148
  186.0 1.6 copy-start
  187.7 15.0 %copy-start.12 = (f32[1536]{0:T(1024)S(1)}, f32[1536]{0:T(1024)}, u32[]{:S(2)}) copy-start(f32[1536]{0:T(1024)} %param.13) | copy-start | bytes 18436
  194.7 9.0 %collective-permute-start.4 = (bf16[2,32,768]{2,1,0:T(8,128)(2,1)}, bf16[2,32,768]{2,1,0:T(8,128)(2,1)S(1)}, u32[]{:S(2)}, u32[]{:S(2)}) collective-permute-start(bf16[2,32,768]{2,1,0:T(8,128)(2,1)} %get-tuple-element.22), channel_id=1, source_target_pairs={{0,256},{1,257},{2,258},{3,259},{4,260},{5,261},{6,262},{7,263},{8... | collective-permute-start | bytes 294920 | tf_op jit(solution)/shard_map/ppermute | solution.py:304
  203.7 0.6 copy-start.10
  207.3 10.3 %copy-start.15 = (bf16[2,32,768]{2,1,0:T(8,128)(2,1)S(1)}, bf16[2,32,768]{2,1,0:T(8,128)(2,1)}, u32[]{:S(2)}) copy-start(bf16[2,32,768]{2,1,0:T(8,128)(2,1)} %get-tuple-element.25) | copy-start | bytes 294916
  210.2 26.8 %all-to-all-start.1 = ((bf16[32,2,32,128]{3,2,1,0:T(8,128)(2,1)}), bf16[32,2,32,128]{3,2,1,0:T(8,128)(2,1)S(1)}, u32[]{:S(2)}, u32[]{:S(2)}) async-start(bf16[32,2,32,128]{3,2,1,0:T(8,128)(2,1)} %bitcast.36), calls=%async_computation.1 | async-start | bytes 1048576 | tf_op jit(solution)/shard_map/all_to_all | solution.py:324
  217.6 19.5 %collective-permute-start.5 = (bf16[2,32,768]{2,1,0:T(8,128)(2,1)S(1)}, bf16[2,32,768]{2,1,0:T(8,128)(2,1)S(1)}, u32[]{:S(2)}, u32[]{:S(2)}) collective-permute-start(bf16[2,32,768]{2,1,0:T(8,128)(2,1)S(1)} %copy-done.15), channel_id=1, source_target_pairs={{256,0},{257,1},{258,2},{259,3},{260,4},{261,5},{262,6},{263,7},{2... | collective-permute-start | bytes 294920 | tf_op jit(solution)/shard_map/ppermute | solution.py:319
  237.0 0.6 copy-start.9
  237.0 5.4 %copy-start.5 = (bf16[32,2,32,128]{3,2,1,0:T(8,128)(2,1)}, bf16[32,2,32,128]{3,2,1,0:T(8,128)(2,1)S(1)}, u32[]{:S(2)}) copy-start(bf16[32,2,32,128]{3,2,1,0:T(8,128)(2,1)S(1)} %all-to-all-done.1.normed_ref) | copy-start | bytes 1572868
  259.0 50.4 %all-to-all-start.3 = ((f32[8,24,128]{2,1,0:T(8,128)}), f32[8,24,128]{2,1,0:T(8,128)S(1)}, u32[]{:S(2)}, u32[]{:S(2)}) async-start(f32[8,24,128]{2,1,0:T(8,128)} %shard_map.90), calls=%async_computation.3 | async-start | bytes 196608 | tf_op jit(solution)/shard_map/all_to_all | solution.py:334
  309.4 1.4 copy-start.11

commit v3 on v2

--- a/solution.py
+++ b/solution.py
@@ -20,26 +20,29 @@
     return [rows[:, k : k + 1] == lanes for k in range(choices)]
 
 
-def forward_layer(layer, state, refs, normed_ref, weights_ref, rscale_ref):
+def forward_layer(layer, state, refs, stats_ref, normed_ref=None):
     picks_ref, routes_ref, w_ref, gain_ref = refs
-    half = state[0].shape[1]
+    tokens, half = state[0].shape
     experts = w_ref.shape[2]
     choices = routes_ref.shape[2]
     floats = [part.astype(F32) for part in state]
     total = sum(jnp.sum(part * part, axis=-1, keepdims=True) for part in floats)
     rscale = lax.rsqrt(total / (HALVES * half) + EPSILON)
-    logits = jnp.zeros((state[0].shape[0], experts), F32)
+    logits = jnp.zeros((tokens, experts), F32)
     for h in range(HALVES):
         normed = (floats[h] * rscale * gain_ref[layer, h : h + 1, :]).astype(BF16)
-        normed_ref[layer, h] = normed
+        if normed_ref is not None:
+            normed_ref[layer, h] = normed
         logits += jnp.dot(normed, w_ref[layer, h * half : (h + 1) * half, :], preferred_element_type=F32)
     hots = onehots(routes_ref, layer, choices, experts)
     raised = [jnp.exp(jnp.sum(jnp.where(hot, logits, 0.0), axis=-1, keepdims=True)) for hot in hots]
     bottom = sum(raised)
     weights = [value / bottom for value in raised]
+    lanes = lax.broadcasted_iota(jnp.int32, stats_ref.shape[1:], 1)
+    stats = jnp.broadcast_to(rscale, lanes.shape)
     for k in range(choices):
-        weights_ref[layer, k] = jnp.broadcast_to(weights[k], weights_ref.shape[2:])
-    rscale_ref[layer] = jnp.broadcast_to(rscale, rscale_ref.shape[1:])
+        stats = jnp.where(lanes == k, weights[k], stats)
+    stats_ref[layer] = stats
     fresh = []
     for h in range(HALVES):
         mixture = sum(weights[k] * picks_ref[layer, h, k].astype(F32) for k in range(choices))
@@ -47,14 +50,15 @@
     return fresh
 
 
-def backward_layer(layer, back, state, refs, weights_ref, rscale_ref, dlogits_ref):
+def backward_layer(layer, back, state, refs, stats_ref, dlogits_ref):
     picks_ref, routes_ref, w_ref, gain_ref = refs
     half = state[0].shape[1]
     experts = w_ref.shape[2]
     choices = routes_ref.shape[2]
     back_float = [part.astype(F32) for part in back]
-    weights = [weights_ref[layer, k][:, 0:1] for k in range(choices)]
-    rscale = rscale_ref[layer][:, 0:1]
+    stats = stats_ref[layer]
+    weights = [stats[:, k : k + 1] for k in range(choices)]
+    rscale = stats[:, choices : choices + 1]
     dweights = [
         sum(
             jnp.sum(back_float[h] * picks_ref[layer, h, k].astype(F32), axis=-1, keepdims=True)
@@ -82,42 +86,96 @@
     return [(b + rscale * (v - s * mean)).astype(BF16) for b, v, s in zip(back_float, varied, normal)]
 
 
+def layout_kernel(rows_ref, out_ref, held_ref, stage_ref, in_sems, out_sems):
+    micros, local_experts, owners, capacity, width = rows_ref.shape
+    half = width // HALVES
+    arriving = [
+        [
+            pltpu.make_async_copy(
+                rows_ref.at[m, e], held_ref.at[m, e], in_sems.at[m * local_experts + e]
+            )
+            for e in range(local_experts)
+        ]
+        for m in range(micros)
+    ]
+    for copies in arriving:
+        for copy in copies:
+            copy.start()
+    leaving = []
+    for m in range(micros):
+        blocks = pl.ds(m * owners, owners)
+        for e in range(local_experts):
+            arriving[m][e].wait()
+            for h in range(HALVES):
+                at = (e * HALVES + h) * capacity
+                stage_ref[blocks, pl.ds(at, capacity), :] = held_ref[m, e, :, :, h * half : (h + 1) * half]
+        leaving.append(pltpu.make_async_copy(stage_ref.at[blocks], out_ref.at[blocks], out_sems.at[m]))
+        leaving[-1].start()
+    for copy in leaving:
+        copy.wait()
+
+
+def pick_layer(layer, copies, table_ref, select_ref, picks_ref):
+    tokens = picks_ref.shape[3]
+    choices = picks_ref.shape[2]
+    for copy in copies[layer]:
+        copy.wait()
+    rows = jnp.dot(select_ref[layer], table_ref[layer], preferred_element_type=F32).astype(BF16)
+    for h in range(HALVES):
+        for k in range(choices):
+            at = (h * choices + k) * tokens
+            picks_ref[layer, h, k] = rows[at : at + tokens]
+
+
 def first_kernel(
-    zh_ref, table_ref, select_ref, routes_ref, w_ref, gain_ref, acts_ref,
-    picks_ref, states_ref, normed_ref, weights_ref, rscale_ref, out_ref,
+    zh_ref, rows_ref, chosen_ref, routes_ref, w_ref, gain_ref, acts_ref,
+    picks_ref, states_ref, stats_ref, out_ref, table_ref, select_ref, sems,
 ):
     layers = table_ref.shape[0]
-    choices = routes_ref.shape[2]
-    tokens = routes_ref.shape[1]
-    for layer in range(layers):
-        rows = jnp.dot(select_ref[layer], table_ref[layer], preferred_element_type=F32).astype(BF16)
-        for h in range(HALVES):
-            for k in range(choices):
-                at = (h * choices + k) * tokens
-                picks_ref[layer, h, k] = rows[at : at + tokens]
+    copies = [
+        (
+            pltpu.make_async_copy(chosen_ref.at[layer], select_ref.at[layer], sems.at[0, layer]),
+            pltpu.make_async_copy(rows_ref.at[layer], table_ref.at[layer], sems.at[1, layer]),
+        )
+        for layer in range(layers)
+    ]
+    for pair in copies:
+        for copy in pair:
+            copy.start()
+
+    @pl.when(zh_ref[0] != 0)
+    def _():
+        for layer in range(layers):
+            pick_layer(layer, copies, table_ref, select_ref, picks_ref)
 
     @pl.when(zh_ref[0] == 0)
     def _():
         refs = (picks_ref, routes_ref, w_ref, gain_ref)
         state = [acts_ref[h] for h in range(HALVES)]
         for layer in range(layers):
+            pick_layer(layer, copies, table_ref, select_ref, picks_ref)
             for h in range(HALVES):
                 states_ref[layer, h] = state[h]
-            state = forward_layer(layer, state, refs, normed_ref, weights_ref, rscale_ref)
+            state = forward_layer(layer, state, refs, stats_ref)
         for h in range(HALVES):
             out_ref[h] = state[h]
 
 
 def middle_kernel(
-    zh_ref, arrived_ref, acts_ref, final_ref, picks_ref, routes_ref, w_ref, gain_ref, given_ref,
-    normed_ref, dlogits_ref, out_ref, states_ref, weights_ref, rscale_ref,
+    zh_ref, arrived_ref, acts_ref, final_ref, picks_ref, routes_ref, w_ref, gain_ref, given_states_ref, given_stats_ref,
+    normed_ref, dlogits_ref, out_ref, states_ref, stats_ref,
 ):
     layers = picks_ref.shape[0]
+    choices = routes_ref.shape[2]
     half = acts_ref.shape[2]
 
     @pl.when(zh_ref[0] == 0)
     def _():
-        normed_ref[...] = given_ref[...]
+        for layer in range(layers):
+            rscale = given_stats_ref[layer][:, choices : choices + 1]
+            for h in range(HALVES):
+                floats = given_states_ref[layer, h].astype(F32)
+                normed_ref[layer, h] = (floats * rscale * gain_ref[layer, h : h + 1, :]).astype(BF16)
 
     @pl.when(zh_ref[0] != 0)
     def _():
@@ -126,7 +184,7 @@
         for layer in range(layers):
             for h in range(HALVES):
                 states_ref[layer, h] = state[h]
-            state = forward_layer(layer, state, refs, normed_ref, weights_ref, rscale_ref)
+            state = forward_layer(layer, state, refs, stats_ref, normed_ref)
         floats = [part.astype(F32) for part in state]
         total = sum(jnp.sum(part * part, axis=-1, keepdims=True) for part in floats)
         rscale = lax.rsqrt(total / (HALVES * half) + EPSILON)
@@ -136,14 +194,14 @@
         back = [(rscale * (v - s * mean)).astype(BF16) for v, s in zip(varied, normal)]
         for layer in reversed(range(layers)):
             state = [states_ref[layer, h] for h in range(HALVES)]
-            back = backward_layer(layer, back, state, refs, weights_ref, rscale_ref, dlogits_ref)
+            back = backward_layer(layer, back, state, refs, stats_ref, dlogits_ref)
         for h in range(HALVES):
             out_ref[h] = back[h]
 
 
 def last_kernel(
-    zh_ref, arrived_ref, states_ref, weights_ref, rscale_ref, picks_ref, routes_ref, w_ref, gain_ref,
-    given_ref, copies_ref, dlogits_ref,
+    zh_ref, arrived_ref, states_ref, stats_ref, picks_ref, routes_ref, w_ref, gain_ref, given_ref,
+    copies_ref, dlogits_ref,
 ):
     layers = picks_ref.shape[0]
 
@@ -157,7 +215,7 @@
         back = [arrived_ref[h] for h in range(HALVES)]
         for layer in reversed(range(layers)):
             state = [states_ref[layer, h] for h in range(HALVES)]
-            back = backward_layer(layer, back, state, refs, weights_ref, rscale_ref, dlogits_ref)
+            back = backward_layer(layer, back, state, refs, stats_ref, dlogits_ref)
 
     for layer in range(layers):
         for group in range(copies_ref.shape[1]):
@@ -188,15 +246,19 @@
             out_ref[h * per_half + plane] = term[plane * rows : (plane + 1) * rows]
 
 
-def call(kernel, outs, args, scratch=(), scalars=1):
+def call(kernel, outs, args, scratch=(), scalars=1, apart=0, apart_out=False, limit=16):
     smem = [pl.BlockSpec(memory_space=pltpu.SMEM)] * scalars
+    free = pl.BlockSpec(memory_space=pltpu.HBM)
     vmem = pl.BlockSpec(memory_space=pltpu.VMEM)
+    far = [pltpu.with_memory_space_constraint(arg, pltpu.HBM) for arg in args[scalars : scalars + apart]]
+    args = (*args[:scalars], *far, *args[scalars + apart :])
     return pl.pallas_call(
         kernel,
         out_shape=outs,
-        in_specs=smem + [vmem] * (len(args) - scalars),
-        out_specs=jax.tree.map(lambda _: vmem, outs),
+        in_specs=smem + [free] * apart + [vmem] * (len(args) - scalars - apart),
+        out_specs=jax.tree.map(lambda _: free if apart_out else vmem, outs),
         scratch_shapes=list(scratch),
+        compiler_params=pltpu.CompilerParams(vmem_limit_bytes=limit * 2**20),
     )(*args)
 
 
@@ -246,8 +308,21 @@
     crossing = jnp.where(zh == 0, cotangent, inputs)
     crossed = lax.ppermute(crossing, "zh", [(0, 1), (1, 0)])
 
-    rows = expert_out[0].reshape(micros, local_experts, owners, capacity, HALVES, half)
-    rows = rows.transpose(0, 2, 1, 4, 3, 5).reshape(micros * owners, local_experts * HALVES * capacity, half)
+    row_blocks = (micros * owners, local_experts * HALVES * capacity, half)
+    rows = call(
+        layout_kernel,
+        jax.ShapeDtypeStruct(row_blocks, BF16),
+        (expert_out[0],),
+        scratch=(
+            pltpu.VMEM(expert_out.shape[1:3] + expert_out.shape[3:], BF16),
+            pltpu.VMEM(row_blocks, BF16),
+            pltpu.SemaphoreType.DMA((micros * local_experts,)),
+            pltpu.SemaphoreType.DMA((micros,)),
+        ),
+        scalars=0,
+        apart=1,
+        apart_out=True,
+    )
     rows, router_here, gain_here, routes_here = lax.optimization_barrier(
         (rows, router_w[0], norm_gain[0], route_ids[0])
     )
@@ -289,17 +364,21 @@
 
     shape = jax.ShapeDtypeStruct
     rows_shape = (HALVES, tokens, half)
-    picks, states, normed, weights, rscale, sent = call(
+    picks, states, stats, sent = call(
         first_kernel,
         (
             shape((layers, HALVES, choices, tokens, half), BF16),
             shape((layers,) + rows_shape, BF16),
-            shape((layers,) + rows_shape, BF16),
-            shape((layers, choices, tokens, 128), F32),
             shape((layers, tokens, 128), F32),
             shape(rows_shape, BF16),
         ),
         (zh_word, table, select, routes, w_all, gain_all, acts),
+        scratch=(
+            pltpu.VMEM(table.shape, BF16),
+            pltpu.VMEM(select.shape, BF16),
+            pltpu.SemaphoreType.DMA((2, layers)),
+        ),
+        apart=2,
     )
     arrived = lax.ppermute(sent, "zh", [(0, 1)])
     normed, dlogits, sent = call(
@@ -309,12 +388,10 @@
             shape((layers, tokens, experts), BF16),
             shape(rows_shape, BF16),
         ),
-        (zh_word, arrived, acts, final_gain.reshape(HALVES, half), picks, routes, w_all, gain_all, normed),
-        scratch=(
-            pltpu.VMEM((layers,) + rows_shape, BF16),
-            pltpu.VMEM((layers, choices, tokens, 128), F32),
-            pltpu.VMEM((layers, tokens, 128), F32),
+        (
+            zh_word, arrived, acts, final_gain.reshape(HALVES, half), picks, routes, w_all, gain_all, states, stats,
         ),
+        scratch=(pltpu.VMEM((layers,) + rows_shape, BF16), pltpu.VMEM((layers, tokens, 128), F32)),
     )
     arrived = lax.ppermute(sent, "zh", [(1, 0)])
     normed = call(
@@ -323,10 +400,11 @@
     normed = normed.reshape(layers * groups, HALVES, tokens, 128)
     normed = lax.all_to_all(normed, ("x",) + flat_axes, split_axis=0, concat_axis=0, tiled=True)
     arrived, normed = lax.optimization_barrier((arrived, normed))
-    dlogits, _ = call(
+    dlogits = call(
         last_kernel,
-        (shape((layers, groups, tokens, experts), BF16), shape((layers, tokens, experts), BF16)),
-        (zh_word, arrived, states, weights, rscale, picks, routes, w_all, gain_all, dlogits),
+        shape((layers, groups, tokens, experts), BF16),
+        (zh_word, arrived, states, stats, picks, routes, w_all, gain_all, dlogits),
+        scratch=(pltpu.VMEM((layers, tokens, experts), BF16),),
     )
     dlogits = dlogits.reshape(layers * groups, tokens, experts)
     dlogits = lax.all_to_all(dlogits, ("x",) + flat_axes, split_axis=0, concat_axis=0, tiled=True)

time: 313 us -> 281 us (0.90)
  local copies, waits for them, and re-layouts: 26.5 us -> 7.2 us
  waiting for transfers between devices: 144 us -> 155 us
  starting transfers between devices: 92.8 us -> 82.2 us
  Pallas kernels: 19.8 us -> 13.1 us
  other arithmetic: 12.5 us -> 6.03 us
    all_to_all x1, starting transfers between devices: 38.9 us -> 26.1 us  [compute(): lax.all_to_all(term, plane_axis, split_axis=0, concat_axis=0, tiled=True)]
    all_to_all x1, waiting for transfers between devices: 33.4 us -> 43.5 us  [compute(): lax.all_to_all(rows, ('x',) + expert_axes, split_axis=0, concat_axis=0, t...]
    another operation x1 -> x0, local copies, waits for them, and re-layouts: 9.23 us -> none  [compute(): expert_out[0].reshape(micros, local_experts, owners, capacity, HALVES, half)]
    pallas_call x5 -> x6, Pallas kernels: 19.8 us -> 13.1 us  [call(): pl.pallas_call(kernel, out_shape=outs, in_specs=smem + [free] * apart + [...]
    transpose x1 -> x0, local copies, waits for them, and re-layouts: 5.12 us -> none  [compute(): rows.transpose(0, 2, 1, 4, 3, 5)]
    another operation x2, other arithmetic: 4.08 us -> 0.43 us  [from_all(): slots = jnp.stack(slots)]
  transfers between devices with their start and end apart: 9 -> 9, of which waited for: 8 -> 8; matrix products, arithmetic and copies ran while one was open for 5% -> 2% of each run, Pallas kernels for 0% -> 0%
where the time goes in v3:
time: 281 us; the launch traced here: 279 us
  waiting for transfers between devices  155 us (55%)
  starting transfers between devices  82.2 us (29%)
  blocking collectives  14.1 us (5%)
  Pallas kernels  13.1 us (5%)
  local copies, waits for them, and re-layouts  7.2 us (3%)
  other arithmetic  6.03 us (2%)
    ppermute x1, waiting for transfers between devices, compute(): crossed = lax.ppermute(crossing, 'zh', [(0, 1), (1, 0)])  57.7 us
    all_to_all x1, waiting for transfers between devices, compute(): lax.all_to_all(rows, ('x',) + expert_axes, split_axis=0, concat_axis=0, t...  43.5 us
    all_to_all x1, starting transfers between devices, compute(): lax.all_to_all(term, plane_axis, split_axis=0, concat_axis=0, tiled=True)  26.1 us
    all_to_all x1, starting transfers between devices, compute(): lax.all_to_all(rows, ('x',) + expert_axes, split_axis=0, concat_axis=0, t...  23.2 us
    ppermute x3, waiting for transfers between devices, from_all(): lax.ppermute(block, axis, [(source, (source + shift) % count) for source...  21.5 us
    ppermute x1, waiting for transfers between devices, compute(): arrived = lax.ppermute(sent, 'zh', [(1, 0)])  20.2 us
    all_to_all x1, blocking collectives, compute(): lax.all_to_all(dlogits, ('x',) + flat_axes, split_axis=0, concat_axis=0,...  14.1 us
    pallas_call x6, Pallas kernels, call(): pl.pallas_call(kernel, out_shape=outs, in_specs=smem + [free] * apart + [...  13.1 us
  transfers between devices with their start and end apart: 9, of which 8 were waited for; matrix products, arithmetic and copies ran while one was open for 2% of the time, Pallas kernels for 0%

profile of v3, /device:TPU:6, one launch (start us, length us, event | category | flops | bytes accessed | tf_op | source)
XLA Modules:
  0.0 279.4 jit_solution(7782657970472705178)
XLA Ops:
  0.6 0.0 copy-start.13
  0.6 3.6 %shard_map.86 = bf16[256,8,768]{2,1,0:T(8,128)(2,1)} custom-call(bf16[4,2,64,2,1536]{4,3,2,1,0:T(2,128)(2,1)} %bitcast.36), custom_call_target="tpu_custom_call" | custom-call | tf_op jit(solution)/shard_map/pallas_call | solution.py:255
  4.3 0.0 copy-start.8
  4.3 0.0 copy-start.9
  4.4 0.0 copy-start.12
  4.4 23.2 %all-to-all-start = ((bf16[256,8,768]{2,1,0:T(8,128)(2,1)}), bf16[256,8,768]{2,1,0:T(8,128)(2,1)}, u32[]{:S(2)}, u32[]{:S(2)}) async-start(bf16[256,8,768]{2,1,0:T(8,128)(2,1)} %shard_map.86), calls=%async_computation | async-start | bytes 6291456 | tf_op jit(solution)/shard_map/all_to_all | solution.py:329
  27.5 0.0 copy-start.7
  27.6 8.4 %collective-permute-start = (bf16[4,32,192]{2,1,0:T(8,128)(2,1)S(1)}, bf16[4,32,192]{2,1,0:T(8,128)(2,1)S(1)}, u32[]{:S(2)}, u32[]{:S(2)}) collective-permute-start(bf16[4,32,192]{2,1,0:T(8,128)(2,1)S(1)} %broadcast_select_fusion), channel_id=1, source_target_pairs={{0,256},{256,0},{1,257},{257,1},{2,258},{258,2},{3,259},{259,3},{4... | collective-permute-start | bytes 147464 | tf_op jit(solution)/shard_map/ppermute | solution.py:309
  36.1 0.1 copy.20
  36.2 0.1 reshape.141
  36.4 57.7 %collective-permute-done = bf16[4,32,192]{2,1,0:T(8,128)(2,1)S(1)} collective-permute-done((bf16[4,32,192]{2,1,0:T(8,128)(2,1)S(1)}, bf16[4,32,192]{2,1,0:T(8,128)(2,1)S(1)}, u32[]{:S(2)}, u32[]{:S(2)}) %collective-permute-start) | collective-permute-done | bytes 49184 | tf_op jit(solution)/shard_map/ppermute | solution.py:309
  94.2 0.1 copy.19
  94.3 0.2 reshape.131
  94.6 0.2 maximum_bitcast_fusion
  94.8 1.9 collective-permute-start.1
  96.7 4.4 %collective-permute-start.2 = (bf16[1680,128]{1,0:T(8,128)(2,1)S(1)}, bf16[1680,128]{1,0:T(8,128)(2,1)S(1)}, u32[]{:S(2)}, u32[]{:S(2)}) collective-permute-start(bf16[1680,128]{1,0:T(8,128)(2,1)S(1)} %get-tuple-element.36), channel_id=1, source_target_pairs={{0,128},{64,192},{128,0},{192,64},{1,129},{65,193},{129,1},{193,65... | collective-permute-start | bytes 1290248 | tf_op jit(solution)/shard_map/ppermute | solution.py:288
  101.1 1.9 collective-permute-start.3
  103.1 0.1 add.169
  103.2 0.1 add.170
  103.3 7.9 %collective-permute-done.1 = bf16[1680,128]{1,0:T(8,128)(2,1)S(1)} collective-permute-done((bf16[1680,128]{1,0:T(8,128)(2,1)S(1)}, bf16[1680,128]{1,0:T(8,128)(2,1)S(1)}, u32[]{:S(2)}, u32[]{:S(2)}) %collective-permute-start.1) | collective-permute-done | bytes 430112 | tf_op jit(solution)/shard_map/ppermute | solution.py:288
  111.2 3.5 %collective-permute-done.2 = bf16[1680,128]{1,0:T(8,128)(2,1)S(1)} collective-permute-done((bf16[1680,128]{1,0:T(8,128)(2,1)S(1)}, bf16[1680,128]{1,0:T(8,128)(2,1)S(1)}, u32[]{:S(2)}, u32[]{:S(2)}) %collective-permute-start.2) | collective-permute-done | bytes 430112 | tf_op jit(solution)/shard_map/ppermute | solution.py:288
  114.7 10.1 %collective-permute-done.3 = bf16[1680,128]{1,0:T(8,128)(2,1)S(1)} collective-permute-done((bf16[1680,128]{1,0:T(8,128)(2,1)S(1)}, bf16[1680,128]{1,0:T(8,128)(2,1)S(1)}, u32[]{:S(2)}, u32[]{:S(2)}) %collective-permute-start.3) | collective-permute-done | bytes 430112 | tf_op jit(solution)/shard_map/ppermute | solution.py:288
  124.8 0.2 pad_maximum_fusion
  125.0 0.1 constant_dynamic-slice_fusion.4
  125.2 0.1 reshape.134
  125.3 0.1 copy.23
  125.4 0.1 reshape.135.acts_ref
  125.6 0.1 fusion.7
  125.8 0.2 pad_maximum_fusion.1
  126.0 0.1 slice.28.w_ref
  126.1 0.5 broadcast.152
  126.6 0.7 fusion.26
  127.3 0.2 select_reduce_fusion
  127.5 0.1 reshape.133
  127.6 0.1 convert_element_type.51.routes_ref
  127.8 0.1 copy.22
  127.9 0.1 add.168
  128.0 1.2 fusion.1.chosen_ref
  129.2 43.5 %all-to-all-done = bf16[256,8,768]{2,1,0:T(8,128)(2,1)} async-done(((bf16[256,8,768]{2,1,0:T(8,128)(2,1)}), bf16[256,8,768]{2,1,0:T(8,128)(2,1)}, u32[]{:S(2)}, u32[]{:S(2)}) %all-to-all-start) | async-done | bytes 3145760 | tf_op jit(solution)/shard_map/all_to_all | solution.py:329
  172.7 4.3 %shard_map.87 = (bf16[4,2,4,32,768]{4,3,2,1,0:T(8,128)(2,1)S(1)}, bf16[4,2,32,768]{3,2,1,0:T(8,128)(2,1)S(1)}, f32[4,32,128]{2,1,0:T(8,128)S(1)}, bf16[2,32,768]{2,1,0:T(8,128)(2,1)}) custom-call(s32[1]{0:T(128)} %bitcast.zh_ref, bf16[4,512,768]{2,1,0:T(8,128)(2,1)} %bitcast.4.rows_ref, bf16[4,256,512]{2,1,0:T(8,128)(2,1)} %fusion.1.chosen_ref, ...), custom_call_target="tpu_custom_call" | custom-call | tf_op jit(solution)/shard_map/pallas_call | solution.py:255
  177.1 0.0 copy-start.2
  177.1 0.7 copy-done.2
  177.8 7.7 %collective-permute-start.4 = (bf16[2,32,768]{2,1,0:T(8,128)(2,1)}, bf16[2,32,768]{2,1,0:T(8,128)(2,1)S(1)}, u32[]{:S(2)}, u32[]{:S(2)}) collective-permute-start(bf16[2,32,768]{2,1,0:T(8,128)(2,1)} %get-tuple-element.19), channel_id=1, source_target_pairs={{0,256},{1,257},{2,258},{3,259},{4,260},{5,261},{6,262},{7,263},{8... | collective-permute-start | bytes 294920 | tf_op jit(solution)/shard_map/ppermute | solution.py:383
  185.6 1.5 fusion.order_ref
  187.1 1.0 collective-permute-done.4.arrived_ref
  188.1 1.0 copy-done.3
  189.1 0.2 shard_map.88
  189.3 0.6 copy-done.5
  189.9 0.6 copy-done
  190.5 0.6 shard_map.89
  191.1 0.8 copy-done.1
  191.9 7.4 %all-to-all-start.1 = ((bf16[32,2,32,128]{3,2,1,0:T(8,128)(2,1)}), bf16[32,2,32,128]{3,2,1,0:T(8,128)(2,1)}, u32[]{:S(2)}, u32[]{:S(2)}) async-start(bf16[32,2,32,128]{3,2,1,0:T(8,128)(2,1)} %bitcast.34), calls=%async_computation.1 | async-start | bytes 1048576 | tf_op jit(solution)/shard_map/all_to_all | solution.py:401
  199.3 1.3 collective-permute-start.5
  200.6 20.2 %collective-permute-done.5.arrived_ref = bf16[2,32,768]{2,1,0:T(8,128)(2,1)S(1)} collective-permute-done((bf16[2,32,768]{2,1,0:T(8,128)(2,1)S(1)}, bf16[2,32,768]{2,1,0:T(8,128)(2,1)S(1)}, u32[]{:S(2)}, u32[]{:S(2)}) %collective-permute-start.5) | collective-permute-done | bytes 98336 | tf_op jit(solution)/shard_map/ppermute | solution.py:396
  220.8 0.0 all-to-all-done.1.normed_ref
  220.8 1.0 copy-done.4
  221.8 2.3 shard_map.90
  224.1 14.1 %all_to_all.20.dlogits_ref = bf16[32,32,128]{2,1,0:T(8,128)(2,1)S(1)} all-to-all(bf16[32,32,128]{2,1,0:T(8,128)(2,1)S(1)} %bitcast.35), channel_id=1, replica_groups=mesh['zh'=2,'x'=4,'z'=8,'yc'=8] {'x','yc'}, dimensions={0} | all-to-all | bytes 524288 | tf_op jit(solution)/shard_map/all_to_all | solution.py:410
  238.2 2.0 shard_map.91
  240.3 26.1 %all-to-all-start.3 = ((f32[8,24,128]{2,1,0:T(8,128)}), f32[8,24,128]{2,1,0:T(8,128)S(1)}, u32[]{:S(2)}, u32[]{:S(2)}) async-start(f32[8,24,128]{2,1,0:T(8,128)} %shard_map.91), calls=%async_computation.3 | async-start | bytes 196608 | tf_op jit(solution)/shard_map/all_to_all | solution.py:412
  266.4 11.6 %all-to-all-done.3 = f32[8,24,128]{2,1,0:T(8,128)S(1)} async-done(((f32[8,24,128]{2,1,0:T(8,128)}), f32[8,24,128]{2,1,0:T(8,128)S(1)}, u32[]{:S(2)}, u32[]{:S(2)}) %all-to-all-start.3) | async-done | bytes 98336 | tf_op jit(solution)/shard_map/all_to_all | solution.py:412
  278.0 0.0 copy-start.10
  278.0 0.8 fusion.8
  278.8 0.6 fusion.25
  (40 shorter events, 0.4 us)
Async XLA Ops:
  0.6 3.7 %copy-start.13 = (f32[1,1536]{1,0:T(1,128)S(1)}, f32[1,1536]{1,0:T(1,128)}, u32[]{:S(2)}) copy-start(f32[1,1536]{1,0:T(1,128)} %param.12) | copy-start | bytes 18436
  4.3 23.2 %copy-start.8 = (bf16[4,32,192]{2,1,0:T(8,128)(2,1)S(1)}, bf16[4,32,192]{2,1,0:T(8,128)(2,1)}, u32[]{:S(2)}) copy-start(bf16[4,32,192]{2,1,0:T(8,128)(2,1)} %param.8) | copy-start | bytes 147460
  4.3 23.2 %copy-start.9 = (bf16[4,32,192]{2,1,0:T(8,128)(2,1)S(1)}, bf16[4,32,192]{2,1,0:T(8,128)(2,1)}, u32[]{:S(2)}) copy-start(bf16[4,32,192]{2,1,0:T(8,128)(2,1)} %param.7) | copy-start | bytes 147460
  4.4 31.7 %copy-start.12 = (s32[1,4,32,4]{2,3,1,0:T(4,128)S(1)}, s32[1,4,32,4]{2,3,1,0:T(4,128)}, u32[]{:S(2)}) copy-start(s32[1,4,32,4]{2,3,1,0:T(4,128)} %param.10) | copy-start | bytes 6148
  4.4 168.4 %all-to-all-start = ((bf16[256,8,768]{2,1,0:T(8,128)(2,1)}), bf16[256,8,768]{2,1,0:T(8,128)(2,1)}, u32[]{:S(2)}, u32[]{:S(2)}) async-start(bf16[256,8,768]{2,1,0:T(8,128)(2,1)} %shard_map.86), calls=%async_computation | async-start | bytes 6291456 | tf_op jit(solution)/shard_map/all_to_all | solution.py:329
  27.5 67.0 %copy-start.7 = (bf16[1,1536,128]{2,1,0:T(8,128)(2,1)S(1)}, bf16[1,1536,128]{2,1,0:T(8,128)(2,1)}, u32[]{:S(2)}) copy-start(bf16[1,1536,128]{2,1,0:T(8,128)(2,1)} %param.11) | copy-start | bytes 1179652
  27.6 66.5 %collective-permute-start = (bf16[4,32,192]{2,1,0:T(8,128)(2,1)S(1)}, bf16[4,32,192]{2,1,0:T(8,128)(2,1)S(1)}, u32[]{:S(2)}, u32[]{:S(2)}) collective-permute-start(bf16[4,32,192]{2,1,0:T(8,128)(2,1)S(1)} %broadcast_select_fusion), channel_id=1, source_target_pairs={{0,256},{256,0},{1,257},{257,1},{2,258},{258,2},{3,259},{259,3},{4... | collective-permute-start | bytes 147464 | tf_op jit(solution)/shard_map/ppermute | solution.py:309
  94.8 16.5 %collective-permute-start.1 = (bf16[1680,128]{1,0:T(8,128)(2,1)S(1)}, bf16[1680,128]{1,0:T(8,128)(2,1)S(1)}, u32[]{:S(2)}, u32[]{:S(2)}) collective-permute-start(bf16[1680,128]{1,0:T(8,128)(2,1)S(1)} %get-tuple-element.35), channel_id=1, source_target_pairs={{0,64},{64,128},{128,192},{192,0},{1,65},{65,129},{129,193},{193,1... | collective-permute-start | bytes 1290248 | tf_op jit(solution)/shard_map/ppermute | solution.py:288
  96.7 18.0 %collective-permute-start.2 = (bf16[1680,128]{1,0:T(8,128)(2,1)S(1)}, bf16[1680,128]{1,0:T(8,128)(2,1)S(1)}, u32[]{:S(2)}, u32[]{:S(2)}) collective-permute-start(bf16[1680,128]{1,0:T(8,128)(2,1)S(1)} %get-tuple-element.36), channel_id=1, source_target_pairs={{0,128},{64,192},{128,0},{192,64},{1,129},{65,193},{129,1},{193,65... | collective-permute-start | bytes 1290248 | tf_op jit(solution)/shard_map/ppermute | solution.py:288
  101.1 23.7 %collective-permute-start.3 = (bf16[1680,128]{1,0:T(8,128)(2,1)S(1)}, bf16[1680,128]{1,0:T(8,128)(2,1)S(1)}, u32[]{:S(2)}, u32[]{:S(2)}) collective-permute-start(bf16[1680,128]{1,0:T(8,128)(2,1)S(1)} %get-tuple-element.37), channel_id=1, source_target_pairs={{0,192},{64,0},{128,64},{192,128},{1,193},{65,1},{129,65},{193,129... | collective-permute-start | bytes 1290248 | tf_op jit(solution)/shard_map/ppermute | solution.py:288
  172.7 14.4 %copy-start.11 = (f32[1536]{0:T(1024)S(1)}, f32[1536]{0:T(1024)}, u32[]{:S(2)}) copy-start(f32[1536]{0:T(1024)} %param.13) | copy-start | bytes 18436
  177.1 0.8 copy-start.2
  177.8 10.3 %collective-permute-start.4 = (bf16[2,32,768]{2,1,0:T(8,128)(2,1)}, bf16[2,32,768]{2,1,0:T(8,128)(2,1)S(1)}, u32[]{:S(2)}, u32[]{:S(2)}) collective-permute-start(bf16[2,32,768]{2,1,0:T(8,128)(2,1)} %get-tuple-element.19), channel_id=1, source_target_pairs={{0,256},{1,257},{2,258},{3,259},{4,260},{5,261},{6,262},{7,263},{8... | collective-permute-start | bytes 294920 | tf_op jit(solution)/shard_map/ppermute | solution.py:383
  188.1 1.0 copy-start.3
  189.1 1.4 copy-start
  189.3 0.6 copy-start.5
  190.5 8.8 %copy-start.6 = (bf16[2,32,768]{2,1,0:T(8,128)(2,1)S(1)}, bf16[2,32,768]{2,1,0:T(8,128)(2,1)}, u32[]{:S(2)}) copy-start(bf16[2,32,768]{2,1,0:T(8,128)(2,1)} %copy-done.5) | copy-start | bytes 294916
  191.1 0.8 copy-start.1
  191.9 28.8 %all-to-all-start.1 = ((bf16[32,2,32,128]{3,2,1,0:T(8,128)(2,1)}), bf16[32,2,32,128]{3,2,1,0:T(8,128)(2,1)}, u32[]{:S(2)}, u32[]{:S(2)}) async-start(bf16[32,2,32,128]{3,2,1,0:T(8,128)(2,1)} %bitcast.34), calls=%async_computation.1 | async-start | bytes 1048576 | tf_op jit(solution)/shard_map/all_to_all | solution.py:401
  199.3 21.5 %collective-permute-start.5 = (bf16[2,32,768]{2,1,0:T(8,128)(2,1)S(1)}, bf16[2,32,768]{2,1,0:T(8,128)(2,1)S(1)}, u32[]{:S(2)}, u32[]{:S(2)}) collective-permute-start(bf16[2,32,768]{2,1,0:T(8,128)(2,1)S(1)} %copy-done.6), channel_id=1, source_target_pairs={{256,0},{257,1},{258,2},{259,3},{260,4},{261,5},{262,6},{263,7},{2... | collective-permute-start | bytes 294920 | tf_op jit(solution)/shard_map/ppermute | solution.py:396
  220.8 1.0 copy-start.4
  240.3 37.7 %all-to-all-start.3 = ((f32[8,24,128]{2,1,0:T(8,128)}), f32[8,24,128]{2,1,0:T(8,128)S(1)}, u32[]{:S(2)}, u32[]{:S(2)}) async-start(f32[8,24,128]{2,1,0:T(8,128)} %shard_map.91), calls=%async_computation.3 | async-start | bytes 196608 | tf_op jit(solution)/shard_map/all_to_all | solution.py:412
  278.0 1.4 copy-start.10

commit v4 on v3

--- a/solution.py
+++ b/solution.py
@@ -86,9 +86,10 @@
     return [(b + rscale * (v - s * mean)).astype(BF16) for b, v, s in zip(back_float, varied, normal)]
 
 
-def layout_kernel(rows_ref, out_ref, held_ref, stage_ref, in_sems, out_sems):
+def layout_kernel(planes, zh_ref, rows_ref, out_ref, held_ref, stage_ref, in_sems, out_sems):
     micros, local_experts, owners, capacity, width = rows_ref.shape
     half = width // HALVES
+    group = owners // planes
     arriving = [
         [
             pltpu.make_async_copy(
@@ -103,14 +104,23 @@
             copy.start()
     leaving = []
     for m in range(micros):
-        blocks = pl.ds(m * owners, owners)
         for e in range(local_experts):
             arriving[m][e].wait()
             for h in range(HALVES):
                 at = (e * HALVES + h) * capacity
-                stage_ref[blocks, pl.ds(at, capacity), :] = held_ref[m, e, :, :, h * half : (h + 1) * half]
-        leaving.append(pltpu.make_async_copy(stage_ref.at[blocks], out_ref.at[blocks], out_sems.at[m]))
-        leaving[-1].start()
+                stage_ref[pl.ds(m * owners, owners), pl.ds(at, capacity), :] = held_ref[
+                    m, e, :, :, h * half : (h + 1) * half
+                ]
+        for plane in range(planes):
+            site = jnp.where(zh_ref[0] == 0, plane, plane ^ 1)
+            leaving.append(
+                pltpu.make_async_copy(
+                    stage_ref.at[pl.ds(m * owners + plane * group, group)],
+                    out_ref.at[pl.ds(m * owners + site * group, group)],
+                    out_sems.at[m * planes + plane],
+                )
+            )
+            leaving[-1].start()
     for copy in leaving:
         copy.wait()
 
@@ -243,7 +253,7 @@
         normed = normed_ref[:, h].reshape(sources * tokens, lanes)
         term = lax.dot_general(normed, dlogits, (((0,), (0,)), ((), ())), preferred_element_type=F32)
         for plane in range(per_half):
-            out_ref[h * per_half + plane] = term[plane * rows : (plane + 1) * rows]
+            out_ref[h * per_half + plane] = term[plane * rows : (plane + 1) * rows].astype(BF16)
 
 
 def call(kernel, outs, args, scratch=(), scalars=1, apart=0, apart_out=False, limit=16):
@@ -278,12 +288,11 @@
     return jnp.stack([high, middle, values - high - middle]).astype(BF16)
 
 
-def from_all(shared, given, axis):
+def from_all(rows, axis, addressed=False):
     count, here = lax.axis_size(axis), lax.axis_index(axis)
     slots = []
     for shift in range(count):
-        mine = lax.dynamic_index_in_dim(given, (here + shift) % count, 0, keepdims=False)
-        block = jnp.concatenate([shared, mine], axis=0)
+        block = lax.dynamic_index_in_dim(rows, (here + shift) % count, 0, keepdims=False) if addressed else rows
         if shift:
             block = lax.ppermute(block, axis, [(source, (source + shift) % count) for source in range(count)])
         slots.append(block)
@@ -306,20 +315,22 @@
 
     kept = jnp.where(zh == 0, inputs, cotangent)
     crossing = jnp.where(zh == 0, cotangent, inputs)
-    crossed = lax.ppermute(crossing, "zh", [(0, 1), (1, 0)])
+    planes = lax.axis_size(plane_axis)
+    lines = ("zh", plane_axis)
+    there = [(plane, planes + (plane ^ 1)) for plane in range(planes)]
+    crossed = lax.ppermute(crossing, lines, there + [(planes + plane, plane) for plane in range(planes)])
 
     row_blocks = (micros * owners, local_experts * HALVES * capacity, half)
     rows = call(
-        layout_kernel,
+        functools.partial(layout_kernel, planes),
         jax.ShapeDtypeStruct(row_blocks, BF16),
-        (expert_out[0],),
+        (zh_word, expert_out[0]),
         scratch=(
             pltpu.VMEM(expert_out.shape[1:3] + expert_out.shape[3:], BF16),
             pltpu.VMEM(row_blocks, BF16),
             pltpu.SemaphoreType.DMA((micros * local_experts,)),
-            pltpu.SemaphoreType.DMA((micros,)),
+            pltpu.SemaphoreType.DMA((micros * planes,)),
         ),
-        scalars=0,
         apart=1,
         apart_out=True,
     )
@@ -329,25 +340,29 @@
     table = lax.all_to_all(rows, ("x",) + expert_axes, split_axis=0, concat_axis=0, tiled=True)
     table = table.reshape(layers, experts * HALVES * capacity, half)
 
-    lower = jnp.where(zh == 0, kept, crossed)
-    upper = jnp.where(zh == 0, crossed, kept)
-    acts_part = jnp.stack([lower, upper], axis=2).reshape(micros, tokens * HALVES * part // 128, 128)
-    act_rows = acts_part.shape[1]
     route_part = routes_here.astype(BF16).reshape(micros, tokens * choices // 128, 128)
     route_rows = route_part.shape[1]
     route_part = jnp.pad(route_part, ((0, 0), (0, 8 - route_rows), (0, 0)))
+    act_rows = tokens * part // 128
+    held = jnp.concatenate([kept.reshape(micros, act_rows, 128), route_part], axis=1)
+    swapped = lax.ppermute(held, lines, [(planes + plane, planes + (plane ^ 1)) for plane in range(planes)])
+    held = jnp.where(zh == 0, held, swapped)
+    crossed = crossed.reshape(micros, act_rows, 128)
+    lower = jnp.where(zh == 0, held[:, :act_rows], crossed)
+    upper = jnp.where(zh == 0, crossed, held[:, :act_rows])
+    given = jnp.concatenate([lower, upper, held[:, act_rows:]], axis=1)
     gain_part = thirds(gain_here).reshape(3 * width // 128, 128)
     gain_rows = gain_part.shape[0]
     gain_part = jnp.pad(gain_part, ((0, -gain_rows % 8), (0, 0)))
     shared = jnp.concatenate([router_here, gain_part], axis=0)
-    packed = from_all(shared, jnp.concatenate([acts_part, route_part], axis=1), "x")
+    packed = from_all(shared, "x")
     w_all = packed[:, :width]
     gain_all = packed[:, width : width + gain_rows].reshape(layers, 3, width).astype(F32)
     gain_all = (gain_all[:, 0] + gain_all[:, 1] + gain_all[:, 2]).reshape(layers, HALVES, half)
-    at = shared.shape[0]
-    acts = packed[:, at : at + act_rows].reshape(layers, tokens, HALVES, part)
-    acts = acts.transpose(2, 1, 0, 3).reshape(HALVES, tokens, half)
-    at += act_rows
+    packed = from_all(given, "x", True)
+    acts = packed[:, : HALVES * act_rows].reshape(layers, HALVES, tokens, part)
+    acts = acts.transpose(1, 2, 0, 3).reshape(HALVES, tokens, half)
+    at = HALVES * act_rows
     routes = packed[:, at : at + route_rows].reshape(layers, tokens, choices).astype(F32).astype(jnp.int32)
 
     target = routes * (HALVES * capacity) + slot_numbers(routes)
@@ -355,7 +370,6 @@
     target = target.reshape(layers, HALVES * choices * tokens, 1)
     select = (target == jnp.arange(experts * HALVES * capacity)[None, None, :]).astype(BF16)
 
-    planes = lax.axis_size(plane_axis)
     groups = owners // planes
     piece = width // owners
     feature = jnp.arange(half)
@@ -380,7 +394,7 @@
         ),
         apart=2,
     )
-    arrived = lax.ppermute(sent, "zh", [(0, 1)])
+    arrived = lax.ppermute(sent, lines, there)
     normed, dlogits, sent = call(
         middle_kernel,
         (
@@ -393,7 +407,7 @@
         ),
         scratch=(pltpu.VMEM((layers,) + rows_shape, BF16), pltpu.VMEM((layers, tokens, 128), F32)),
     )
-    arrived = lax.ppermute(sent, "zh", [(1, 0)])
+    arrived = lax.ppermute(sent, lines, [(target, source) for source, target in there])
     normed = call(
         spread_kernel, shape((layers, groups, HALVES, tokens, 128), BF16), (normed, order), scalars=0
     )
@@ -408,9 +422,9 @@
     )
     dlogits = dlogits.reshape(layers * groups, tokens, experts)
     dlogits = lax.all_to_all(dlogits, ("x",) + flat_axes, split_axis=0, concat_axis=0, tiled=True)
-    term = call(grad_kernel, shape((planes, piece, experts), F32), (normed, dlogits), scalars=0)
+    term = call(grad_kernel, shape((planes, piece, experts), BF16), (normed, dlogits), scalars=0)
     term = lax.all_to_all(term, plane_axis, split_axis=0, concat_axis=0, tiled=True)
-    router_part = jnp.sum(term, axis=0)
+    router_part = jnp.sum(term.astype(F32), axis=0)
     at = lax.axis_index(expert_axes) * (width // owners)
     w_slab = lax.dynamic_slice_in_dim(router_w[0], at, width // owners, 0).astype(F32)
     gain_slab = lax.dynamic_slice_in_dim(norm_gain[0], at, width // owners, 0)

time: 281 us -> 280 us (level)
  waiting for transfers between devices: 155 us -> 140 us
  starting transfers between devices: 82.2 us -> 95 us
    ppermute x3 -> x6, waiting for transfers between devices: 21.5 us -> 9.47 us  [from_all(): lax.ppermute(block, axis, [(source, (source + shift) % count) for source...]
    ppermute x3 -> x6, starting transfers between devices: 8.22 us -> 18 us  [from_all(): lax.ppermute(block, axis, [(source, (source + shift) % count) for source...]
    ppermute x3 -> x4, waiting for transfers between devices: 78.9 us -> 70.4 us  [the longest x1 51.4 us: compute(): lax.ppermute(crossing, lines, there + [(planes + plane, plane) for plane...]
    all_to_all x1, waiting for transfers between devices: 43.5 us -> 48.9 us  [compute(): lax.all_to_all(rows, ('x',) + expert_axes, split_axis=0, concat_axis=0, t...]
    ppermute x3 -> x4, starting transfers between devices: 17.4 us -> 19.7 us  [the longest x1 10 us: compute(): lax.ppermute(crossing, lines, there + [(planes + plane, plane) for plane...]
  transfers between devices with their start and end apart: 9 -> 13, of which waited for: 8 -> 7; matrix products, arithmetic and copies ran while one was open for 2% -> 2% of each run, Pallas kernels for 0% -> 0%
where the time goes in v4:
time: 280 us; the launch traced here: 277 us
  waiting for transfers between devices  140 us (50%)
  starting transfers between devices  95 us (34%)
  blocking collectives  15.2 us (5%)
  Pallas kernels  13.2 us (5%)
  local copies, waits for them, and re-layouts  7.17 us (3%)
  other arithmetic  5.84 us (2%)
    ppermute x1, waiting for transfers between devices, compute(): lax.ppermute(crossing, lines, there + [(planes + plane, plane) for plane...  51.4 us
    all_to_all x1, waiting for transfers between devices, compute(): lax.all_to_all(rows, ('x',) + expert_axes, split_axis=0, concat_axis=0, t...  48.9 us
    all_to_all x1, starting transfers between devices, compute(): lax.all_to_all(term, plane_axis, split_axis=0, concat_axis=0, tiled=True)  26 us
    all_to_all x1, starting transfers between devices, compute(): lax.all_to_all(rows, ('x',) + expert_axes, split_axis=0, concat_axis=0, t...  23.2 us
    ppermute x6, starting transfers between devices, from_all(): lax.ppermute(block, axis, [(source, (source + shift) % count) for source...  18 us
    ppermute x1, waiting for transfers between devices, compute(): lax.ppermute(sent, lines, [(target, source) for source, target in there])  18 us
    all_to_all x1, blocking collectives, compute(): lax.all_to_all(dlogits, ('x',) + flat_axes, split_axis=0, concat_axis=0,...  15.2 us
    pallas_call x6, Pallas kernels, call(): pl.pallas_call(kernel, out_shape=outs, in_specs=smem + [free] * apart + [...  13.2 us
  transfers between devices with their start and end apart: 13, of which 7 were waited for; matrix products, arithmetic and copies ran while one was open for 2% of the time, Pallas kernels for 0%

profile of v4, /device:TPU:6, one launch (start us, length us, event | category | flops | bytes accessed | tf_op | source)
XLA Modules:
  0.0 277.2 jit_solution(7349776240673567039)
XLA Ops:
  0.6 3.9 %shard_map.86 = bf16[256,8,768]{2,1,0:T(8,128)(2,1)} custom-call(s32[1]{0:T(128)} %bitcast.zh_ref, bf16[4,2,64,2,1536]{4,3,2,1,0:T(2,128)(2,1)} %bitcast.33), custom_call_target="tpu_custom_call" | custom-call | tf_op jit(solution)/shard_map/pallas_call | solution.py:265
  4.6 0.0 copy-start.7
  4.6 0.0 copy-start.12
  4.6 0.0 copy-start.8
  4.6 0.0 copy-start.9
  4.6 23.2 %all-to-all-start = ((bf16[256,8,768]{2,1,0:T(8,128)(2,1)}), bf16[256,8,768]{2,1,0:T(8,128)(2,1)}, u32[]{:S(2)}, u32[]{:S(2)}) async-start(bf16[256,8,768]{2,1,0:T(8,128)(2,1)} %shard_map.86), calls=%async_computation | async-start | bytes 6291456 | tf_op jit(solution)/shard_map/all_to_all | solution.py:340
  27.9 0.1 fusion.25
  28.0 2.5 collective-permute-start.5
  30.5 3.8 %collective-permute-start.6 = (bf16[1576,128]{1,0:T(8,128)(2,1)S(1)}, bf16[1576,128]{1,0:T(8,128)(2,1)S(1)}, u32[]{:S(2)}, u32[]{:S(2)}) collective-permute-start(bf16[1576,128]{1,0:T(8,128)(2,1)S(1)} %get-tuple-element.35), channel_id=1, source_target_pairs={{0,128},{64,192},{128,0},{192,64},{1,129},{65,193},{129,1},{193,65... | collective-permute-start | bytes 1210376 | tf_op jit(solution)/shard_map/ppermute | solution.py:297
  34.3 0.1 copy.20
  34.4 0.1 reshape.146
  34.6 0.1 reshape.134
  34.8 0.7 collective-permute-start
  35.4 10.0 %collective-permute-start.1 = (bf16[4,32,192]{2,1,0:T(8,128)(2,1)S(1)}, bf16[4,32,192]{2,1,0:T(8,128)(2,1)S(1)}, u32[]{:S(2)}, u32[]{:S(2)}) collective-permute-start(bf16[4,32,192]{2,1,0:T(8,128)(2,1)S(1)} %get-tuple-element.36), channel_id=1, source_target_pairs={{0,264},{8,256},{16,280},{24,272},{32,296},{40,288},{48,312},{56,3... | collective-permute-start | bytes 147464 | tf_op jit(solution)/shard_map/ppermute | solution.py:321
  45.6 51.4 %collective-permute-done.1 = bf16[4,32,192]{2,1,0:T(8,128)(2,1)S(1)} collective-permute-done((bf16[4,32,192]{2,1,0:T(8,128)(2,1)S(1)}, bf16[4,32,192]{2,1,0:T(8,128)(2,1)S(1)}, u32[]{:S(2)}, u32[]{:S(2)}) %collective-permute-start.1) | collective-permute-done | bytes 49184 | tf_op jit(solution)/shard_map/ppermute | solution.py:321
  97.0 0.1 reshape.136
  97.3 2.3 collective-permute-start.4
  99.6 4.7 %collective-permute-start.2 = (bf16[104,128]{1,0:T(8,128)(2,1)S(1)}, bf16[104,128]{1,0:T(8,128)(2,1)S(1)}, u32[]{:S(2)}, u32[]{:S(2)}) collective-permute-start(bf16[104,128]{1,0:T(8,128)(2,1)S(1)} %get-tuple-element.45), channel_id=1, source_target_pairs={{0,64},{64,128},{128,192},{192,0},{1,65},{65,129},{129,193},{193,1... | collective-permute-start | bytes 79880 | tf_op jit(solution)/shard_map/ppermute | solution.py:297
  104.3 1.9 collective-permute-start.3
  106.3 0.1 add.177
  106.4 0.1 add.178
  106.5 2.8 collective-permute-start.7
  109.3 2.4 collective-permute-done.3
  111.8 0.1 reshape.138
  111.9 0.1 copy.23
  112.0 0.1 reshape.139.acts_ref
  112.2 0.5 broadcast.134
  112.7 0.7 fusion.26
  113.3 0.2 select_reduce_fusion
  113.6 0.1 reshape.137
  113.7 0.1 convert_element_type.53.routes_ref
  113.8 0.1 copy.22
  113.9 0.1 add.176
  114.0 1.2 fusion.1.chosen_ref
  115.3 7.0 %collective-permute-done.7 = bf16[1576,128]{1,0:T(8,128)(2,1)S(1)} collective-permute-done((bf16[1576,128]{1,0:T(8,128)(2,1)S(1)}, bf16[1576,128]{1,0:T(8,128)(2,1)S(1)}, u32[]{:S(2)}, u32[]{:S(2)}) %collective-permute-start.7) | collective-permute-done | bytes 403488 | tf_op jit(solution)/shard_map/ppermute | solution.py:297
  122.3 0.2 pad_maximum_fusion
  122.5 0.1 constant_dynamic-slice_fusion.4
  122.7 0.1 fusion.6
  122.8 0.2 pad_maximum_fusion.1
  123.0 0.1 slice.39.w_ref
  123.1 48.9 %all-to-all-done = bf16[256,8,768]{2,1,0:T(8,128)(2,1)} async-done(((bf16[256,8,768]{2,1,0:T(8,128)(2,1)}), bf16[256,8,768]{2,1,0:T(8,128)(2,1)}, u32[]{:S(2)}, u32[]{:S(2)}) %all-to-all-start) | async-done | bytes 3145760 | tf_op jit(solution)/shard_map/all_to_all | solution.py:340
  172.0 4.3 %shard_map.87 = (bf16[4,2,4,32,768]{4,3,2,1,0:T(8,128)(2,1)S(1)}, bf16[4,2,32,768]{3,2,1,0:T(8,128)(2,1)S(1)}, f32[4,32,128]{2,1,0:T(8,128)S(1)}, bf16[2,32,768]{2,1,0:T(8,128)(2,1)}) custom-call(s32[1]{0:T(128)} %bitcast.zh_ref, bf16[4,512,768]{2,1,0:T(8,128)(2,1)} %bitcast.4.rows_ref, bf16[4,256,512]{2,1,0:T(8,128)(2,1)} %fusion.1.chosen_ref, ...), custom_call_target="tpu_custom_call" | custom-call | tf_op jit(solution)/shard_map/pallas_call | solution.py:265
  176.3 0.7 copy-done.2
  177.1 7.7 %collective-permute-start.8 = (bf16[2,32,768]{2,1,0:T(8,128)(2,1)}, bf16[2,32,768]{2,1,0:T(8,128)(2,1)S(1)}, u32[]{:S(2)}, u32[]{:S(2)}) collective-permute-start(bf16[2,32,768]{2,1,0:T(8,128)(2,1)} %get-tuple-element.19), channel_id=1, source_target_pairs={{0,264},{8,256},{16,280},{24,272},{32,296},{40,288},{48,312},{56,3... | collective-permute-start | bytes 294920 | tf_op jit(solution)/shard_map/ppermute | solution.py:397
  184.8 1.5 fusion.order_ref
  186.3 1.0 collective-permute-done.8.arrived_ref
  187.3 1.0 copy-done.3
  188.3 0.2 shard_map.88
  188.5 0.6 copy-done.5
  189.1 0.6 copy-done
  189.7 0.6 shard_map.89
  190.3 0.8 copy-done.1
  191.1 8.1 %all-to-all-start.1 = ((bf16[32,2,32,128]{3,2,1,0:T(8,128)(2,1)}), bf16[32,2,32,128]{3,2,1,0:T(8,128)(2,1)}, u32[]{:S(2)}, u32[]{:S(2)}) async-start(bf16[32,2,32,128]{3,2,1,0:T(8,128)(2,1)} %bitcast.31), calls=%async_computation.1 | async-start | bytes 1048576 | tf_op jit(solution)/shard_map/all_to_all | solution.py:415
  199.3 1.3 collective-permute-start.9
  200.6 18.0 %collective-permute-done.9.arrived_ref = bf16[2,32,768]{2,1,0:T(8,128)(2,1)S(1)} collective-permute-done((bf16[2,32,768]{2,1,0:T(8,128)(2,1)S(1)}, bf16[2,32,768]{2,1,0:T(8,128)(2,1)S(1)}, u32[]{:S(2)}, u32[]{:S(2)}) %collective-permute-start.9) | collective-permute-done | bytes 98336 | tf_op jit(solution)/shard_map/ppermute | solution.py:410
  218.5 1.0 copy-done.4
  219.5 2.3 shard_map.90
  221.8 15.2 %all_to_all.20.dlogits_ref = bf16[32,32,128]{2,1,0:T(8,128)(2,1)S(1)} all-to-all(bf16[32,32,128]{2,1,0:T(8,128)(2,1)S(1)} %bitcast.32), channel_id=1, replica_groups=mesh['zh'=2,'x'=4,'z'=8,'yc'=8] {'x','yc'}, dimensions={0} | all-to-all | bytes 524288 | tf_op jit(solution)/shard_map/all_to_all | solution.py:424
  237.0 2.0 shard_map.91
  239.0 26.0 %all-to-all-start.3 = ((bf16[8,24,128]{2,1,0:T(8,128)(2,1)}), bf16[8,24,128]{2,1,0:T(8,128)(2,1)S(1)}, u32[]{:S(2)}, u32[]{:S(2)}) async-start(bf16[8,24,128]{2,1,0:T(8,128)(2,1)} %shard_map.91), calls=%async_computation.3 | async-start | bytes 98304 | tf_op jit(solution)/shard_map/all_to_all | solution.py:426
  265.0 10.8 %all-to-all-done.3 = bf16[8,24,128]{2,1,0:T(8,128)(2,1)S(1)} async-done(((bf16[8,24,128]{2,1,0:T(8,128)(2,1)}), bf16[8,24,128]{2,1,0:T(8,128)(2,1)S(1)}, u32[]{:S(2)}, u32[]{:S(2)}) %all-to-all-start.3) | async-done | bytes 49184 | tf_op jit(solution)/shard_map/all_to_all | solution.py:426
  275.8 0.0 copy-start.10
  275.8 0.8 fusion.7
  276.6 0.6 fusion.24
  (52 shorter events, 0.5 us)
Async XLA Ops:
  0.6 3.9 %copy-start.13 = (f32[1,1536]{1,0:T(1,128)S(1)}, f32[1,1536]{1,0:T(1,128)}, u32[]{:S(2)}) copy-start(f32[1,1536]{1,0:T(1,128)} %param.12) | copy-start | bytes 18436
  4.6 23.3 %copy-start.7 = (bf16[1,1536,128]{2,1,0:T(8,128)(2,1)S(1)}, bf16[1,1536,128]{2,1,0:T(8,128)(2,1)}, u32[]{:S(2)}) copy-start(bf16[1,1536,128]{2,1,0:T(8,128)(2,1)} %param.11) | copy-start | bytes 1179652
  4.6 29.7 %copy-start.12 = (s32[1,4,32,4]{2,3,1,0:T(4,128)S(1)}, s32[1,4,32,4]{2,3,1,0:T(4,128)}, u32[]{:S(2)}) copy-start(s32[1,4,32,4]{2,3,1,0:T(4,128)} %param.10) | copy-start | bytes 6148
  4.6 30.0 %copy-start.8 = (bf16[4,32,192]{2,1,0:T(8,128)(2,1)S(1)}, bf16[4,32,192]{2,1,0:T(8,128)(2,1)}, u32[]{:S(2)}) copy-start(bf16[4,32,192]{2,1,0:T(8,128)(2,1)} %param.8) | copy-start | bytes 147460
  4.6 30.0 %copy-start.9 = (bf16[4,32,192]{2,1,0:T(8,128)(2,1)S(1)}, bf16[4,32,192]{2,1,0:T(8,128)(2,1)}, u32[]{:S(2)}) copy-start(bf16[4,32,192]{2,1,0:T(8,128)(2,1)} %param.7) | copy-start | bytes 147460
  4.6 167.4 %all-to-all-start = ((bf16[256,8,768]{2,1,0:T(8,128)(2,1)}), bf16[256,8,768]{2,1,0:T(8,128)(2,1)}, u32[]{:S(2)}, u32[]{:S(2)}) async-start(bf16[256,8,768]{2,1,0:T(8,128)(2,1)} %shard_map.86), calls=%async_computation | async-start | bytes 6291456 | tf_op jit(solution)/shard_map/all_to_all | solution.py:340
  28.0 87.3 %collective-permute-start.5 = (bf16[1576,128]{1,0:T(8,128)(2,1)S(1)}, bf16[1576,128]{1,0:T(8,128)(2,1)S(1)}, u32[]{:S(2)}, u32[]{:S(2)}) collective-permute-start(bf16[1576,128]{1,0:T(8,128)(2,1)S(1)} %get-tuple-element.35), channel_id=1, source_target_pairs={{0,64},{64,128},{128,192},{192,0},{1,65},{65,129},{129,193},{193,1... | collective-permute-start | bytes 1210376 | tf_op jit(solution)/shard_map/ppermute | solution.py:297
  30.5 84.7 %collective-permute-start.6 = (bf16[1576,128]{1,0:T(8,128)(2,1)S(1)}, bf16[1576,128]{1,0:T(8,128)(2,1)S(1)}, u32[]{:S(2)}, u32[]{:S(2)}) collective-permute-start(bf16[1576,128]{1,0:T(8,128)(2,1)S(1)} %get-tuple-element.35), channel_id=1, source_target_pairs={{0,128},{64,192},{128,0},{192,64},{1,129},{65,193},{129,1},{193,65... | collective-permute-start | bytes 1210376 | tf_op jit(solution)/shard_map/ppermute | solution.py:297
  34.8 62.4 %collective-permute-start = (bf16[4,56,128]{2,1,0:T(8,128)(2,1)S(1)}, bf16[4,56,128]{2,1,0:T(8,128)(2,1)S(1)}, u32[]{:S(2)}, u32[]{:S(2)}) collective-permute-start(bf16[4,56,128]{2,1,0:T(8,128)(2,1)S(1)} %fusion.5), channel_id=1, source_target_pairs={{256,264},{264,256},{272,280},{280,272},{288,296},{296,288},{304,3... | collective-permute-start | bytes 172040 | tf_op jit(solution)/shard_map/ppermute | solution.py:348
  35.4 61.6 %collective-permute-start.1 = (bf16[4,32,192]{2,1,0:T(8,128)(2,1)S(1)}, bf16[4,32,192]{2,1,0:T(8,128)(2,1)S(1)}, u32[]{:S(2)}, u32[]{:S(2)}) collective-permute-start(bf16[4,32,192]{2,1,0:T(8,128)(2,1)S(1)} %get-tuple-element.36), channel_id=1, source_target_pairs={{0,264},{8,256},{16,280},{24,272},{32,296},{40,288},{48,312},{56,3... | collective-permute-start | bytes 147464 | tf_op jit(solution)/shard_map/ppermute | solution.py:321
  97.3 9.2 %collective-permute-start.4 = (bf16[104,128]{1,0:T(8,128)(2,1)S(1)}, bf16[104,128]{1,0:T(8,128)(2,1)S(1)}, u32[]{:S(2)}, u32[]{:S(2)}) collective-permute-start(bf16[104,128]{1,0:T(8,128)(2,1)S(1)} %get-tuple-element.43), channel_id=1, source_target_pairs={{0,192},{64,0},{128,64},{192,128},{1,193},{65,1},{129,65},{193,129... | collective-permute-start | bytes 79880 | tf_op jit(solution)/shard_map/ppermute | solution.py:297
  99.6 9.7 %collective-permute-start.2 = (bf16[104,128]{1,0:T(8,128)(2,1)S(1)}, bf16[104,128]{1,0:T(8,128)(2,1)S(1)}, u32[]{:S(2)}, u32[]{:S(2)}) collective-permute-start(bf16[104,128]{1,0:T(8,128)(2,1)S(1)} %get-tuple-element.45), channel_id=1, source_target_pairs={{0,64},{64,128},{128,192},{192,0},{1,65},{65,129},{129,193},{193,1... | collective-permute-start | bytes 79880 | tf_op jit(solution)/shard_map/ppermute | solution.py:297
  104.3 7.4 %collective-permute-start.3 = (bf16[104,128]{1,0:T(8,128)(2,1)S(1)}, bf16[104,128]{1,0:T(8,128)(2,1)S(1)}, u32[]{:S(2)}, u32[]{:S(2)}) collective-permute-start(bf16[104,128]{1,0:T(8,128)(2,1)S(1)} %get-tuple-element.44), channel_id=1, source_target_pairs={{0,128},{64,192},{128,0},{192,64},{1,129},{65,193},{129,1},{193,65... | collective-permute-start | bytes 79880 | tf_op jit(solution)/shard_map/ppermute | solution.py:297
  106.5 15.8 %collective-permute-start.7 = (bf16[1576,128]{1,0:T(8,128)(2,1)S(1)}, bf16[1576,128]{1,0:T(8,128)(2,1)S(1)}, u32[]{:S(2)}, u32[]{:S(2)}) collective-permute-start(bf16[1576,128]{1,0:T(8,128)(2,1)S(1)} %get-tuple-element.35), channel_id=1, source_target_pairs={{0,192},{64,0},{128,64},{192,128},{1,193},{65,1},{129,65},{193,129... | collective-permute-start | bytes 1210376 | tf_op jit(solution)/shard_map/ppermute | solution.py:297
  172.0 14.3 %copy-start.11 = (f32[1536]{0:T(1024)S(1)}, f32[1536]{0:T(1024)}, u32[]{:S(2)}) copy-start(f32[1536]{0:T(1024)} %param.13) | copy-start | bytes 18436
  176.3 0.8 copy-start.2
  177.1 10.2 %collective-permute-start.8 = (bf16[2,32,768]{2,1,0:T(8,128)(2,1)}, bf16[2,32,768]{2,1,0:T(8,128)(2,1)S(1)}, u32[]{:S(2)}, u32[]{:S(2)}) collective-permute-start(bf16[2,32,768]{2,1,0:T(8,128)(2,1)} %get-tuple-element.19), channel_id=1, source_target_pairs={{0,264},{8,256},{16,280},{24,272},{32,296},{40,288},{48,312},{56,3... | collective-permute-start | bytes 294920 | tf_op jit(solution)/shard_map/ppermute | solution.py:397
  187.3 1.0 copy-start.3
  188.3 1.4 copy-start
  188.5 0.6 copy-start.5
  189.7 9.5 %copy-start.6 = (bf16[2,32,768]{2,1,0:T(8,128)(2,1)S(1)}, bf16[2,32,768]{2,1,0:T(8,128)(2,1)}, u32[]{:S(2)}) copy-start(bf16[2,32,768]{2,1,0:T(8,128)(2,1)} %copy-done.5) | copy-start | bytes 294916
  190.3 0.8 copy-start.1
  191.1 27.4 %all-to-all-start.1 = ((bf16[32,2,32,128]{3,2,1,0:T(8,128)(2,1)}), bf16[32,2,32,128]{3,2,1,0:T(8,128)(2,1)}, u32[]{:S(2)}, u32[]{:S(2)}) async-start(bf16[32,2,32,128]{3,2,1,0:T(8,128)(2,1)} %bitcast.31), calls=%async_computation.1 | async-start | bytes 1048576 | tf_op jit(solution)/shard_map/all_to_all | solution.py:415
  199.3 19.3 %collective-permute-start.9 = (bf16[2,32,768]{2,1,0:T(8,128)(2,1)S(1)}, bf16[2,32,768]{2,1,0:T(8,128)(2,1)S(1)}, u32[]{:S(2)}, u32[]{:S(2)}) collective-permute-start(bf16[2,32,768]{2,1,0:T(8,128)(2,1)S(1)} %copy-done.6), channel_id=1, source_target_pairs={{264,0},{256,8},{280,16},{272,24},{296,32},{288,40},{312,48},{304,... | collective-permute-start | bytes 294920 | tf_op jit(solution)/shard_map/ppermute | solution.py:410
  218.5 1.0 copy-start.4
  239.0 36.8 %all-to-all-start.3 = ((bf16[8,24,128]{2,1,0:T(8,128)(2,1)}), bf16[8,24,128]{2,1,0:T(8,128)(2,1)S(1)}, u32[]{:S(2)}, u32[]{:S(2)}) async-start(bf16[8,24,128]{2,1,0:T(8,128)(2,1)} %shard_map.91), calls=%async_computation.3 | async-start | bytes 98304 | tf_op jit(solution)/shard_map/all_to_all | solution.py:426
  275.8 1.4 copy-start.10

commit v5 on v4

--- a/solution.py
+++ b/solution.py
@@ -313,12 +313,14 @@
     choices = route_ids.shape[3]
     zh_word = jnp.reshape(zh, (1,)).astype(jnp.int32)
 
-    kept = jnp.where(zh == 0, inputs, cotangent)
     crossing = jnp.where(zh == 0, cotangent, inputs)
     planes = lax.axis_size(plane_axis)
     lines = ("zh", plane_axis)
     there = [(plane, planes + (plane ^ 1)) for plane in range(planes)]
     crossed = lax.ppermute(crossing, lines, there + [(planes + plane, plane) for plane in range(planes)])
+    aside = [(planes + plane, planes + (plane ^ 1)) for plane in range(planes)]
+    swapped_rows = lax.ppermute(cotangent, lines, aside)
+    swapped_routes = lax.ppermute(route_ids[0], lines, aside)
 
     row_blocks = (micros * owners, local_experts * HALVES * capacity, half)
     rows = call(
@@ -334,9 +336,9 @@
         apart=1,
         apart_out=True,
     )
-    rows, router_here, gain_here, routes_here = lax.optimization_barrier(
-        (rows, router_w[0], norm_gain[0], route_ids[0])
-    )
+    rows, router_here, gain_here = lax.optimization_barrier((rows, router_w[0], norm_gain[0]))
+    kept = jnp.where(zh == 0, inputs, swapped_rows)
+    routes_here = jnp.where(zh == 0, route_ids[0], swapped_routes)
     table = lax.all_to_all(rows, ("x",) + expert_axes, split_axis=0, concat_axis=0, tiled=True)
     table = table.reshape(layers, experts * HALVES * capacity, half)
 
@@ -345,8 +347,6 @@
     route_part = jnp.pad(route_part, ((0, 0), (0, 8 - route_rows), (0, 0)))
     act_rows = tokens * part // 128
     held = jnp.concatenate([kept.reshape(micros, act_rows, 128), route_part], axis=1)
-    swapped = lax.ppermute(held, lines, [(planes + plane, planes + (plane ^ 1)) for plane in range(planes)])
-    held = jnp.where(zh == 0, held, swapped)
     crossed = crossed.reshape(micros, act_rows, 128)
     lower = jnp.where(zh == 0, held[:, :act_rows], crossed)
     upper = jnp.where(zh == 0, crossed, held[:, :act_rows])

time: 280 us -> 280 us (level)
  transfers between devices with their start and end apart: 13 -> 14, of which waited for: 7 -> 7; matrix products, arithmetic and copies ran while one was open for 2% -> 2% of each run, Pallas kernels for 0% -> 0%
where the time goes in v5:
time: 280 us; the launch traced here: 277 us
  waiting for transfers between devices  139 us (50%)
  starting transfers between devices  95.8 us (34%)
  blocking collectives  15.2 us (5%)
  Pallas kernels  13.2 us (5%)
  local copies, waits for them, and re-layouts  7.16 us (3%)
  other arithmetic  5.81 us (2%)
    ppermute x1, waiting for transfers between devices, compute(): lax.ppermute(crossing, lines, there + [(planes + plane, plane) for plane...  51.2 us
    all_to_all x1, waiting for transfers between devices, compute(): lax.all_to_all(rows, ('x',) + expert_axes, split_axis=0, concat_axis=0, t...  48.6 us
    all_to_all x1, starting transfers between devices, compute(): lax.all_to_all(term, plane_axis, split_axis=0, concat_axis=0, tiled=True)  26.1 us
    all_to_all x1, starting transfers between devices, compute(): lax.all_to_all(rows, ('x',) + expert_axes, split_axis=0, concat_axis=0, t...  23.2 us
    ppermute x6, starting transfers between devices, from_all(): lax.ppermute(block, axis, [(source, (source + shift) % count) for source...  18 us
    ppermute x1, waiting for transfers between devices, compute(): lax.ppermute(sent, lines, [(target, source) for source, target in there])  18 us
    all_to_all x1, blocking collectives, compute(): lax.all_to_all(dlogits, ('x',) + flat_axes, split_axis=0, concat_axis=0,...  15.2 us
    pallas_call x6, Pallas kernels, call(): pl.pallas_call(kernel, out_shape=outs, in_specs=smem + [free] * apart + [...  13.2 us
  transfers between devices with their start and end apart: 14, of which 7 were waited for; matrix products, arithmetic and copies ran while one was open for 2% of the time, Pallas kernels for 0%

profile of v5, /device:TPU:6, one launch (start us, length us, event | category | flops | bytes accessed | tf_op | source)
XLA Modules:
  0.0 277.4 jit_solution(1361773844558514676)
XLA Ops:
  0.6 3.9 %shard_map.86 = bf16[256,8,768]{2,1,0:T(8,128)(2,1)} custom-call(s32[1]{0:T(128)} %bitcast.zh_ref, bf16[4,2,64,2,1536]{4,3,2,1,0:T(2,128)(2,1)} %bitcast.34), custom_call_target="tpu_custom_call" | custom-call | tf_op jit(solution)/shard_map/pallas_call | solution.py:265
  4.6 0.0 copy-start.7
  4.6 0.0 copy-start.9
  4.6 0.0 copy-start.8
  4.6 0.0 copy-start.12
  4.6 23.2 %all-to-all-start = ((bf16[256,8,768]{2,1,0:T(8,128)(2,1)}), bf16[256,8,768]{2,1,0:T(8,128)(2,1)}, u32[]{:S(2)}, u32[]{:S(2)}) async-start(bf16[256,8,768]{2,1,0:T(8,128)(2,1)} %shard_map.86), calls=%async_computation | async-start | bytes 6291456 | tf_op jit(solution)/shard_map/all_to_all | solution.py:342
  27.9 0.1 fusion.25
  28.0 2.5 collective-permute-start.6
  30.5 3.8 %collective-permute-start.7 = (bf16[1576,128]{1,0:T(8,128)(2,1)S(1)}, bf16[1576,128]{1,0:T(8,128)(2,1)S(1)}, u32[]{:S(2)}, u32[]{:S(2)}) collective-permute-start(bf16[1576,128]{1,0:T(8,128)(2,1)S(1)} %get-tuple-element.33), channel_id=1, source_target_pairs={{0,128},{64,192},{128,0},{192,64},{1,129},{65,193},{129,1},{193,65... | collective-permute-start | bytes 1210376 | tf_op jit(solution)/shard_map/ppermute | solution.py:297
  34.3 0.7 collective-permute-start
  35.0 10.0 %collective-permute-start.1 = (bf16[4,32,192]{2,1,0:T(8,128)(2,1)S(1)}, bf16[4,32,192]{2,1,0:T(8,128)(2,1)S(1)}, u32[]{:S(2)}, u32[]{:S(2)}) collective-permute-start(bf16[4,32,192]{2,1,0:T(8,128)(2,1)S(1)} %broadcast_select_fusion.2), channel_id=1, source_target_pairs={{0,264},{8,256},{16,280},{24,272},{32,296},{40,288},{48,312},{56,3... | collective-permute-start | bytes 147464 | tf_op jit(solution)/shard_map/ppermute | solution.py:320
  45.1 0.7 collective-permute-start.2
  45.9 0.1 copy.19
  46.0 0.1 reshape.144
  46.1 51.2 %collective-permute-done.1 = bf16[4,32,192]{2,1,0:T(8,128)(2,1)S(1)} collective-permute-done((bf16[4,32,192]{2,1,0:T(8,128)(2,1)S(1)}, bf16[4,32,192]{2,1,0:T(8,128)(2,1)S(1)}, u32[]{:S(2)}, u32[]{:S(2)}) %collective-permute-start.1) | collective-permute-done | bytes 49184 | tf_op jit(solution)/shard_map/ppermute | solution.py:320
  97.3 0.1 select_n.150
  97.4 0.1 select_n.152
  97.6 2.3 collective-permute-start.5
  100.0 4.7 %collective-permute-start.3 = (bf16[104,128]{1,0:T(8,128)(2,1)S(1)}, bf16[104,128]{1,0:T(8,128)(2,1)S(1)}, u32[]{:S(2)}, u32[]{:S(2)}) collective-permute-start(bf16[104,128]{1,0:T(8,128)(2,1)S(1)} %get-tuple-element.43), channel_id=1, source_target_pairs={{0,64},{64,128},{128,192},{192,0},{1,65},{65,129},{129,193},{193,1... | collective-permute-start | bytes 79880 | tf_op jit(solution)/shard_map/ppermute | solution.py:297
  104.7 1.9 collective-permute-start.4
  106.7 0.1 add.177
  106.8 0.1 add.178
  106.8 2.8 collective-permute-start.8
  109.6 2.6 collective-permute-done.4
  112.3 0.1 reshape.136
  112.4 0.1 copy.22
  112.5 0.1 reshape.137.acts_ref
  112.7 0.5 broadcast.133
  113.2 0.7 fusion.26
  113.9 0.2 select_reduce_fusion
  114.1 0.1 reshape.135
  114.2 0.1 convert_element_type.53.routes_ref
  114.4 0.1 copy.21
  114.5 0.1 add.176
  114.6 1.2 fusion.1.chosen_ref
  115.8 6.8 %collective-permute-done.8 = bf16[1576,128]{1,0:T(8,128)(2,1)S(1)} collective-permute-done((bf16[1576,128]{1,0:T(8,128)(2,1)S(1)}, bf16[1576,128]{1,0:T(8,128)(2,1)S(1)}, u32[]{:S(2)}, u32[]{:S(2)}) %collective-permute-start.8) | collective-permute-done | bytes 403488 | tf_op jit(solution)/shard_map/ppermute | solution.py:297
  122.5 0.2 pad_maximum_fusion
  122.7 0.1 constant_dynamic-slice_fusion.4
  122.9 0.1 fusion.6
  123.1 0.2 pad_maximum_fusion.1
  123.3 0.1 slice.28.w_ref
  123.4 48.6 %all-to-all-done = bf16[256,8,768]{2,1,0:T(8,128)(2,1)} async-done(((bf16[256,8,768]{2,1,0:T(8,128)(2,1)}), bf16[256,8,768]{2,1,0:T(8,128)(2,1)}, u32[]{:S(2)}, u32[]{:S(2)}) %all-to-all-start) | async-done | bytes 3145760 | tf_op jit(solution)/shard_map/all_to_all | solution.py:342
  172.0 4.3 %shard_map.87 = (bf16[4,2,4,32,768]{4,3,2,1,0:T(8,128)(2,1)S(1)}, bf16[4,2,32,768]{3,2,1,0:T(8,128)(2,1)S(1)}, f32[4,32,128]{2,1,0:T(8,128)S(1)}, bf16[2,32,768]{2,1,0:T(8,128)(2,1)}) custom-call(s32[1]{0:T(128)} %bitcast.zh_ref, bf16[4,512,768]{2,1,0:T(8,128)(2,1)} %bitcast.3.rows_ref, bf16[4,256,512]{2,1,0:T(8,128)(2,1)} %fusion.1.chosen_ref, ...), custom_call_target="tpu_custom_call" | custom-call | tf_op jit(solution)/shard_map/pallas_call | solution.py:265
  176.3 0.7 copy-done.2
  177.1 7.7 %collective-permute-start.9 = (bf16[2,32,768]{2,1,0:T(8,128)(2,1)}, bf16[2,32,768]{2,1,0:T(8,128)(2,1)S(1)}, u32[]{:S(2)}, u32[]{:S(2)}) collective-permute-start(bf16[2,32,768]{2,1,0:T(8,128)(2,1)} %get-tuple-element.17), channel_id=1, source_target_pairs={{0,264},{8,256},{16,280},{24,272},{32,296},{40,288},{48,312},{56,3... | collective-permute-start | bytes 294920 | tf_op jit(solution)/shard_map/ppermute | solution.py:397
  184.8 1.5 fusion.order_ref
  186.3 1.0 collective-permute-done.9.arrived_ref
  187.3 1.0 copy-done.3
  188.3 0.2 shard_map.88
  188.5 0.6 copy-done.5
  189.1 0.6 copy-done
  189.7 0.6 shard_map.89
  190.3 0.8 copy-done.1
  191.1 8.1 %all-to-all-start.1 = ((bf16[32,2,32,128]{3,2,1,0:T(8,128)(2,1)}), bf16[32,2,32,128]{3,2,1,0:T(8,128)(2,1)}, u32[]{:S(2)}, u32[]{:S(2)}) async-start(bf16[32,2,32,128]{3,2,1,0:T(8,128)(2,1)} %bitcast.32), calls=%async_computation.1 | async-start | bytes 1048576 | tf_op jit(solution)/shard_map/all_to_all | solution.py:415
  199.3 1.3 collective-permute-start.10
  200.6 18.0 %collective-permute-done.10.arrived_ref = bf16[2,32,768]{2,1,0:T(8,128)(2,1)S(1)} collective-permute-done((bf16[2,32,768]{2,1,0:T(8,128)(2,1)S(1)}, bf16[2,32,768]{2,1,0:T(8,128)(2,1)S(1)}, u32[]{:S(2)}, u32[]{:S(2)}) %collective-permute-start.10) | collective-permute-done | bytes 98336 | tf_op jit(solution)/shard_map/ppermute | solution.py:410
  218.5 1.0 copy-done.4
  219.5 2.3 shard_map.90
  221.8 15.2 %all_to_all.20.dlogits_ref = bf16[32,32,128]{2,1,0:T(8,128)(2,1)S(1)} all-to-all(bf16[32,32,128]{2,1,0:T(8,128)(2,1)S(1)} %bitcast.33), channel_id=1, replica_groups=mesh['zh'=2,'x'=4,'z'=8,'yc'=8] {'x','yc'}, dimensions={0} | all-to-all | bytes 524288 | tf_op jit(solution)/shard_map/all_to_all | solution.py:424
  237.0 2.0 shard_map.91
  239.0 26.1 %all-to-all-start.3 = ((bf16[8,24,128]{2,1,0:T(8,128)(2,1)}), bf16[8,24,128]{2,1,0:T(8,128)(2,1)S(1)}, u32[]{:S(2)}, u32[]{:S(2)}) async-start(bf16[8,24,128]{2,1,0:T(8,128)(2,1)} %shard_map.91), calls=%async_computation.3 | async-start | bytes 98304 | tf_op jit(solution)/shard_map/all_to_all | solution.py:426
  265.2 10.8 %all-to-all-done.3 = bf16[8,24,128]{2,1,0:T(8,128)(2,1)S(1)} async-done(((bf16[8,24,128]{2,1,0:T(8,128)(2,1)}), bf16[8,24,128]{2,1,0:T(8,128)(2,1)S(1)}, u32[]{:S(2)}, u32[]{:S(2)}) %all-to-all-start.3) | async-done | bytes 49184 | tf_op jit(solution)/shard_map/all_to_all | solution.py:426
  276.0 0.8 fusion.7
  276.8 0.6 fusion.24
  (51 shorter events, 0.4 us)
Async XLA Ops:
  0.6 3.9 %copy-start.13 = (f32[1,1536]{1,0:T(1,128)S(1)}, f32[1,1536]{1,0:T(1,128)}, u32[]{:S(2)}) copy-start(f32[1,1536]{1,0:T(1,128)} %param.12) | copy-start | bytes 18436
  4.6 23.3 %copy-start.7 = (bf16[1,1536,128]{2,1,0:T(8,128)(2,1)S(1)}, bf16[1,1536,128]{2,1,0:T(8,128)(2,1)}, u32[]{:S(2)}) copy-start(bf16[1,1536,128]{2,1,0:T(8,128)(2,1)} %param.11) | copy-start | bytes 1179652
  4.6 29.7 %copy-start.9 = (bf16[4,32,192]{2,1,0:T(8,128)(2,1)S(1)}, bf16[4,32,192]{2,1,0:T(8,128)(2,1)}, u32[]{:S(2)}) copy-start(bf16[4,32,192]{2,1,0:T(8,128)(2,1)} %param.8) | copy-start | bytes 147460
  4.6 30.4 %copy-start.8 = (bf16[4,32,192]{2,1,0:T(8,128)(2,1)S(1)}, bf16[4,32,192]{2,1,0:T(8,128)(2,1)}, u32[]{:S(2)}) copy-start(bf16[4,32,192]{2,1,0:T(8,128)(2,1)} %param.7) | copy-start | bytes 147460
  4.6 40.4 %copy-start.12 = (s32[1,4,32,4]{2,3,1,0:T(4,128)S(1)}, s32[1,4,32,4]{2,3,1,0:T(4,128)}, u32[]{:S(2)}) copy-start(s32[1,4,32,4]{2,3,1,0:T(4,128)} %param.10) | copy-start | bytes 6148
  4.6 167.4 %all-to-all-start = ((bf16[256,8,768]{2,1,0:T(8,128)(2,1)}), bf16[256,8,768]{2,1,0:T(8,128)(2,1)}, u32[]{:S(2)}, u32[]{:S(2)}) async-start(bf16[256,8,768]{2,1,0:T(8,128)(2,1)} %shard_map.86), calls=%async_computation | async-start | bytes 6291456 | tf_op jit(solution)/shard_map/all_to_all | solution.py:342
  28.0 87.8 %collective-permute-start.6 = (bf16[1576,128]{1,0:T(8,128)(2,1)S(1)}, bf16[1576,128]{1,0:T(8,128)(2,1)S(1)}, u32[]{:S(2)}, u32[]{:S(2)}) collective-permute-start(bf16[1576,128]{1,0:T(8,128)(2,1)S(1)} %get-tuple-element.33), channel_id=1, source_target_pairs={{0,64},{64,128},{128,192},{192,0},{1,65},{65,129},{129,193},{193,1... | collective-permute-start | bytes 1210376 | tf_op jit(solution)/shard_map/ppermute | solution.py:297
  30.5 85.3 %collective-permute-start.7 = (bf16[1576,128]{1,0:T(8,128)(2,1)S(1)}, bf16[1576,128]{1,0:T(8,128)(2,1)S(1)}, u32[]{:S(2)}, u32[]{:S(2)}) collective-permute-start(bf16[1576,128]{1,0:T(8,128)(2,1)S(1)} %get-tuple-element.33), channel_id=1, source_target_pairs={{0,128},{64,192},{128,0},{192,64},{1,129},{65,193},{129,1},{193,65... | collective-permute-start | bytes 1210376 | tf_op jit(solution)/shard_map/ppermute | solution.py:297
  34.3 63.0 %collective-permute-start = (bf16[4,32,192]{2,1,0:T(8,128)(2,1)S(1)}, bf16[4,32,192]{2,1,0:T(8,128)(2,1)S(1)}, u32[]{:S(2)}, u32[]{:S(2)}) collective-permute-start(bf16[4,32,192]{2,1,0:T(8,128)(2,1)S(1)} %copy-done.9), channel_id=1, source_target_pairs={{256,264},{264,256},{272,280},{280,272},{288,296},{296,288},{304,3... | collective-permute-start | bytes 147464 | tf_op jit(solution)/shard_map/ppermute | solution.py:322
  35.0 62.3 %collective-permute-start.1 = (bf16[4,32,192]{2,1,0:T(8,128)(2,1)S(1)}, bf16[4,32,192]{2,1,0:T(8,128)(2,1)S(1)}, u32[]{:S(2)}, u32[]{:S(2)}) collective-permute-start(bf16[4,32,192]{2,1,0:T(8,128)(2,1)S(1)} %broadcast_select_fusion.2), channel_id=1, source_target_pairs={{0,264},{8,256},{16,280},{24,272},{32,296},{40,288},{48,312},{56,3... | collective-permute-start | bytes 147464 | tf_op jit(solution)/shard_map/ppermute | solution.py:320
  45.1 0.8 collective-permute-start.2
  97.6 9.2 %collective-permute-start.5 = (bf16[104,128]{1,0:T(8,128)(2,1)S(1)}, bf16[104,128]{1,0:T(8,128)(2,1)S(1)}, u32[]{:S(2)}, u32[]{:S(2)}) collective-permute-start(bf16[104,128]{1,0:T(8,128)(2,1)S(1)} %get-tuple-element.41), channel_id=1, source_target_pairs={{0,192},{64,0},{128,64},{192,128},{1,193},{65,1},{129,65},{193,129... | collective-permute-start | bytes 79880 | tf_op jit(solution)/shard_map/ppermute | solution.py:297
  100.0 9.7 %collective-permute-start.3 = (bf16[104,128]{1,0:T(8,128)(2,1)S(1)}, bf16[104,128]{1,0:T(8,128)(2,1)S(1)}, u32[]{:S(2)}, u32[]{:S(2)}) collective-permute-start(bf16[104,128]{1,0:T(8,128)(2,1)S(1)} %get-tuple-element.43), channel_id=1, source_target_pairs={{0,64},{64,128},{128,192},{192,0},{1,65},{65,129},{129,193},{193,1... | collective-permute-start | bytes 79880 | tf_op jit(solution)/shard_map/ppermute | solution.py:297
  104.7 7.6 %collective-permute-start.4 = (bf16[104,128]{1,0:T(8,128)(2,1)S(1)}, bf16[104,128]{1,0:T(8,128)(2,1)S(1)}, u32[]{:S(2)}, u32[]{:S(2)}) collective-permute-start(bf16[104,128]{1,0:T(8,128)(2,1)S(1)} %get-tuple-element.42), channel_id=1, source_target_pairs={{0,128},{64,192},{128,0},{192,64},{1,129},{65,193},{129,1},{193,65... | collective-permute-start | bytes 79880 | tf_op jit(solution)/shard_map/ppermute | solution.py:297
  106.8 15.7 %collective-permute-start.8 = (bf16[1576,128]{1,0:T(8,128)(2,1)S(1)}, bf16[1576,128]{1,0:T(8,128)(2,1)S(1)}, u32[]{:S(2)}, u32[]{:S(2)}) collective-permute-start(bf16[1576,128]{1,0:T(8,128)(2,1)S(1)} %get-tuple-element.33), channel_id=1, source_target_pairs={{0,192},{64,0},{128,64},{192,128},{1,193},{65,1},{129,65},{193,129... | collective-permute-start | bytes 1210376 | tf_op jit(solution)/shard_map/ppermute | solution.py:297
  172.0 14.3 %copy-start.11 = (f32[1536]{0:T(1024)S(1)}, f32[1536]{0:T(1024)}, u32[]{:S(2)}) copy-start(f32[1536]{0:T(1024)} %param.13) | copy-start | bytes 18436
  176.3 0.8 copy-start.2
  177.1 10.2 %collective-permute-start.9 = (bf16[2,32,768]{2,1,0:T(8,128)(2,1)}, bf16[2,32,768]{2,1,0:T(8,128)(2,1)S(1)}, u32[]{:S(2)}, u32[]{:S(2)}) collective-permute-start(bf16[2,32,768]{2,1,0:T(8,128)(2,1)} %get-tuple-element.17), channel_id=1, source_target_pairs={{0,264},{8,256},{16,280},{24,272},{32,296},{40,288},{48,312},{56,3... | collective-permute-start | bytes 294920 | tf_op jit(solution)/shard_map/ppermute | solution.py:397
  187.3 1.0 copy-start.3
  188.3 1.4 copy-start
  188.5 0.6 copy-start.5
  189.7 9.5 %copy-start.6 = (bf16[2,32,768]{2,1,0:T(8,128)(2,1)S(1)}, bf16[2,32,768]{2,1,0:T(8,128)(2,1)}, u32[]{:S(2)}) copy-start(bf16[2,32,768]{2,1,0:T(8,128)(2,1)} %copy-done.5) | copy-start | bytes 294916
  190.3 0.8 copy-start.1
  191.1 27.4 %all-to-all-start.1 = ((bf16[32,2,32,128]{3,2,1,0:T(8,128)(2,1)}), bf16[32,2,32,128]{3,2,1,0:T(8,128)(2,1)}, u32[]{:S(2)}, u32[]{:S(2)}) async-start(bf16[32,2,32,128]{3,2,1,0:T(8,128)(2,1)} %bitcast.32), calls=%async_computation.1 | async-start | bytes 1048576 | tf_op jit(solution)/shard_map/all_to_all | solution.py:415
  199.3 19.3 %collective-permute-start.10 = (bf16[2,32,768]{2,1,0:T(8,128)(2,1)S(1)}, bf16[2,32,768]{2,1,0:T(8,128)(2,1)S(1)}, u32[]{:S(2)}, u32[]{:S(2)}) collective-permute-start(bf16[2,32,768]{2,1,0:T(8,128)(2,1)S(1)} %copy-done.6), channel_id=1, source_target_pairs={{264,0},{256,8},{280,16},{272,24},{296,32},{288,40},{312,48},{304,... | collective-permute-start | bytes 294920 | tf_op jit(solution)/shard_map/ppermute | solution.py:410
  218.5 1.0 copy-start.4
  239.0 36.9 %all-to-all-start.3 = ((bf16[8,24,128]{2,1,0:T(8,128)(2,1)}), bf16[8,24,128]{2,1,0:T(8,128)(2,1)S(1)}, u32[]{:S(2)}, u32[]{:S(2)}) async-start(bf16[8,24,128]{2,1,0:T(8,128)(2,1)} %shard_map.91), calls=%async_computation.3 | async-start | bytes 98304 | tf_op jit(solution)/shard_map/all_to_all | solution.py:426
  276.0 1.4 copy-start.10

commit v6 on v3

--- a/solution.py
+++ b/solution.py
@@ -128,7 +128,7 @@
 
 
 def first_kernel(
-    zh_ref, rows_ref, chosen_ref, routes_ref, w_ref, gain_ref, acts_ref,
+    zh_ref, rows_ref, chosen_ref, routes_ref, w_ref, gain_ref, kept_ref, crossed_ref,
     picks_ref, states_ref, stats_ref, out_ref, table_ref, select_ref, sems,
 ):
     layers = table_ref.shape[0]
@@ -151,7 +151,7 @@
     @pl.when(zh_ref[0] == 0)
     def _():
         refs = (picks_ref, routes_ref, w_ref, gain_ref)
-        state = [acts_ref[h] for h in range(HALVES)]
+        state = [kept_ref[...], crossed_ref[...]]
         for layer in range(layers):
             pick_layer(layer, copies, table_ref, select_ref, picks_ref)
             for h in range(HALVES):
@@ -162,12 +162,12 @@
 
 
 def middle_kernel(
-    zh_ref, arrived_ref, acts_ref, final_ref, picks_ref, routes_ref, w_ref, gain_ref, given_states_ref, given_stats_ref,
+    zh_ref, arrived_ref, kept_ref, crossed_ref, final_ref, picks_ref, routes_ref, w_ref, gain_ref, given_states_ref, given_stats_ref,
     normed_ref, dlogits_ref, out_ref, states_ref, stats_ref,
 ):
     layers = picks_ref.shape[0]
     choices = routes_ref.shape[2]
-    half = acts_ref.shape[2]
+    half = kept_ref.shape[1]
 
     @pl.when(zh_ref[0] == 0)
     def _():
@@ -189,7 +189,8 @@
         total = sum(jnp.sum(part * part, axis=-1, keepdims=True) for part in floats)
         rscale = lax.rsqrt(total / (HALVES * half) + EPSILON)
         normal = [part * rscale for part in floats]
-        varied = [acts_ref[h].astype(F32) * final_ref[h : h + 1, :] for h in range(HALVES)]
+        cotangents = (crossed_ref, kept_ref)
+        varied = [cotangents[h][...].astype(F32) * final_ref[h : h + 1, :] for h in range(HALVES)]
         mean = sum(jnp.sum(v * s, axis=-1, keepdims=True) for v, s in zip(varied, normal)) / (HALVES * half)
         back = [(rscale * (v - s * mean)).astype(BF16) for v, s in zip(varied, normal)]
         for layer in reversed(range(layers)):
@@ -243,7 +244,7 @@
         normed = normed_ref[:, h].reshape(sources * tokens, lanes)
         term = lax.dot_general(normed, dlogits, (((0,), (0,)), ((), ())), preferred_element_type=F32)
         for plane in range(per_half):
-            out_ref[h * per_half + plane] = term[plane * rows : (plane + 1) * rows]
+            out_ref[h * per_half + plane] = term[plane * rows : (plane + 1) * rows].astype(BF16)
 
 
 def call(kernel, outs, args, scratch=(), scalars=1, apart=0, apart_out=False, limit=16):
@@ -278,12 +279,11 @@
     return jnp.stack([high, middle, values - high - middle]).astype(BF16)
 
 
-def from_all(shared, given, axis):
+def from_all(rows, axis, addressed=False):
     count, here = lax.axis_size(axis), lax.axis_index(axis)
     slots = []
     for shift in range(count):
-        mine = lax.dynamic_index_in_dim(given, (here + shift) % count, 0, keepdims=False)
-        block = jnp.concatenate([shared, mine], axis=0)
+        block = lax.dynamic_index_in_dim(rows, (here + shift) % count, 0, keepdims=False) if addressed else rows
         if shift:
             block = lax.ppermute(block, axis, [(source, (source + shift) % count) for source in range(count)])
         slots.append(block)
@@ -303,10 +303,6 @@
     experts = router_w.shape[2]
     choices = route_ids.shape[3]
     zh_word = jnp.reshape(zh, (1,)).astype(jnp.int32)
-
-    kept = jnp.where(zh == 0, inputs, cotangent)
-    crossing = jnp.where(zh == 0, cotangent, inputs)
-    crossed = lax.ppermute(crossing, "zh", [(0, 1), (1, 0)])
 
     row_blocks = (micros * owners, local_experts * HALVES * capacity, half)
     rows = call(
@@ -323,32 +319,33 @@
         apart=1,
         apart_out=True,
     )
-    rows, router_here, gain_here, routes_here = lax.optimization_barrier(
-        (rows, router_w[0], norm_gain[0], route_ids[0])
+    rows, router_here, gain_here, routes_here, inputs, cotangent = lax.optimization_barrier(
+        (rows, router_w[0], norm_gain[0], route_ids[0], inputs, cotangent)
     )
     table = lax.all_to_all(rows, ("x",) + expert_axes, split_axis=0, concat_axis=0, tiled=True)
     table = table.reshape(layers, experts * HALVES * capacity, half)
 
-    lower = jnp.where(zh == 0, kept, crossed)
-    upper = jnp.where(zh == 0, crossed, kept)
-    acts_part = jnp.stack([lower, upper], axis=2).reshape(micros, tokens * HALVES * part // 128, 128)
-    act_rows = acts_part.shape[1]
     route_part = routes_here.astype(BF16).reshape(micros, tokens * choices // 128, 128)
     route_rows = route_part.shape[1]
     route_part = jnp.pad(route_part, ((0, 0), (0, 8 - route_rows), (0, 0)))
+    act_rows = tokens * part // 128
+    pair = jnp.stack([inputs, cotangent], axis=1).reshape(micros, HALVES * act_rows, 128)
+    given = jnp.concatenate([pair, route_part], axis=1)
     gain_part = thirds(gain_here).reshape(3 * width // 128, 128)
     gain_rows = gain_part.shape[0]
     gain_part = jnp.pad(gain_part, ((0, -gain_rows % 8), (0, 0)))
     shared = jnp.concatenate([router_here, gain_part], axis=0)
-    packed = from_all(shared, jnp.concatenate([acts_part, route_part], axis=1), "x")
+    packed = from_all(given, "x", True)
+    pair = packed[:, : HALVES * act_rows].reshape(layers, HALVES, tokens, part)
+    pair = pair.transpose(1, 2, 0, 3).reshape(HALVES, tokens, half)
+    kept = jnp.where(zh == 0, pair[0], pair[1])
+    crossed = lax.ppermute(jnp.where(zh == 0, pair[1], pair[0]), "zh", [(0, 1), (1, 0)])
+    at = HALVES * act_rows
+    routes = packed[:, at : at + route_rows].reshape(layers, tokens, choices).astype(F32).astype(jnp.int32)
+    packed = from_all(shared, "x")
     w_all = packed[:, :width]
     gain_all = packed[:, width : width + gain_rows].reshape(layers, 3, width).astype(F32)
     gain_all = (gain_all[:, 0] + gain_all[:, 1] + gain_all[:, 2]).reshape(layers, HALVES, half)
-    at = shared.shape[0]
-    acts = packed[:, at : at + act_rows].reshape(layers, tokens, HALVES, part)
-    acts = acts.transpose(2, 1, 0, 3).reshape(HALVES, tokens, half)
-    at += act_rows
-    routes = packed[:, at : at + route_rows].reshape(layers, tokens, choices).astype(F32).astype(jnp.int32)
 
     target = routes * (HALVES * capacity) + slot_numbers(routes)
     target = target.transpose(0, 2, 1)[:, None] + (jnp.arange(HALVES) * capacity)[None, :, None, None]
@@ -372,7 +369,7 @@
             shape((layers, tokens, 128), F32),
             shape(rows_shape, BF16),
         ),
-        (zh_word, table, select, routes, w_all, gain_all, acts),
+        (zh_word, table, select, routes, w_all, gain_all, kept, crossed),
         scratch=(
             pltpu.VMEM(table.shape, BF16),
             pltpu.VMEM(select.shape, BF16),
@@ -389,7 +386,7 @@
             shape(rows_shape, BF16),
         ),
         (
-            zh_word, arrived, acts, final_gain.reshape(HALVES, half), picks, routes, w_all, gain_all, states, stats,
+            zh_word, arrived, kept, crossed, final_gain.reshape(HALVES, half), picks, routes, w_all, gain_all, states, stats,
         ),
         scratch=(pltpu.VMEM((layers,) + rows_shape, BF16), pltpu.VMEM((layers, tokens, 128), F32)),
     )
@@ -408,9 +405,9 @@
     )
     dlogits = dlogits.reshape(layers * groups, tokens, experts)
     dlogits = lax.all_to_all(dlogits, ("x",) + flat_axes, split_axis=0, concat_axis=0, tiled=True)
-    term = call(grad_kernel, shape((planes, piece, experts), F32), (normed, dlogits), scalars=0)
+    term = call(grad_kernel, shape((planes, piece, experts), BF16), (normed, dlogits), scalars=0)
     term = lax.all_to_all(term, plane_axis, split_axis=0, concat_axis=0, tiled=True)
-    router_part = jnp.sum(term, axis=0)
+    router_part = jnp.sum(term.astype(F32), axis=0)
     at = lax.axis_index(expert_axes) * (width // owners)
     w_slab = lax.dynamic_slice_in_dim(router_w[0], at, width // owners, 0).astype(F32)
     gain_slab = lax.dynamic_slice_in_dim(norm_gain[0], at, width // owners, 0)

time: 281 us -> 264 us (0.940)
  waiting for transfers between devices: 155 us -> 129 us
  starting transfers between devices: 82.2 us -> 88.6 us
    ppermute x1, waiting for transfers between devices: 57.7 us -> 14.3 us  [compute(): lax.ppermute(jnp.where(zh == 0, pair[1], pair[0]), 'zh', [(0, 1), (1, 0)])]
    all_to_all x1, waiting for transfers between devices: 43.5 us -> 77.9 us  [compute(): lax.all_to_all(rows, ('x',) + expert_axes, split_axis=0, concat_axis=0, t...]
    ppermute x3 -> x6, starting transfers between devices: 8.22 us -> 28.7 us  [from_all(): lax.ppermute(block, axis, [(source, (source + shift) % count) for source...]
    ppermute x3 -> x6, waiting for transfers between devices: 21.5 us -> 7.24 us  [from_all(): lax.ppermute(block, axis, [(source, (source + shift) % count) for source...]
    all_to_all x1, starting transfers between devices: 26.1 us -> 12.2 us  [compute(): lax.all_to_all(term, plane_axis, split_axis=0, concat_axis=0, tiled=True)]
  transfers between devices with their start and end apart: 9 -> 12, of which waited for: 8 -> 7; matrix products, arithmetic and copies ran while one was open for 2% -> 3% of each run, Pallas kernels for 0% -> 0%
where the time goes in v6:
time: 264 us; the launch traced here: 261 us
  waiting for transfers between devices  129 us (49%)
  starting transfers between devices  88.6 us (34%)
  blocking collectives  14.1 us (5%)
  Pallas kernels  13.2 us (5%)
  local copies, waits for them, and re-layouts  7.93 us (3%)
  other arithmetic  6.83 us (3%)
    all_to_all x1, waiting for transfers between devices, compute(): lax.all_to_all(rows, ('x',) + expert_axes, split_axis=0, concat_axis=0, t...  77.9 us
    ppermute x6, starting transfers between devices, from_all(): lax.ppermute(block, axis, [(source, (source + shift) % count) for source...  28.7 us
    all_to_all x1, starting transfers between devices, compute(): lax.all_to_all(rows, ('x',) + expert_axes, split_axis=0, concat_axis=0, t...  23.2 us
    ppermute x1, waiting for transfers between devices, compute(): arrived = lax.ppermute(sent, 'zh', [(1, 0)])  18 us
    ppermute x1, waiting for transfers between devices, compute(): lax.ppermute(jnp.where(zh == 0, pair[1], pair[0]), 'zh', [(0, 1), (1, 0)])  14.3 us
    all_to_all x1, blocking collectives, compute(): lax.all_to_all(dlogits, ('x',) + flat_axes, split_axis=0, concat_axis=0,...  14.1 us
    pallas_call x6, Pallas kernels, call(): pl.pallas_call(kernel, out_shape=outs, in_specs=smem + [free] * apart + [...  13.2 us
    all_to_all x1, starting transfers between devices, compute(): lax.all_to_all(term, plane_axis, split_axis=0, concat_axis=0, tiled=True)  12.2 us
  transfers between devices with their start and end apart: 12, of which 7 were waited for; matrix products, arithmetic and copies ran while one was open for 3% of the time, Pallas kernels for 0%

profile of v6, /device:TPU:6, one launch (start us, length us, event | category | flops | bytes accessed | tf_op | source)
XLA Modules:
  0.0 261.1 jit_solution(7050844127651724551)
XLA Ops:
  0.6 3.6 %shard_map.86 = bf16[256,8,768]{2,1,0:T(8,128)(2,1)} custom-call(bf16[4,2,64,2,1536]{4,3,2,1,0:T(2,128)(2,1)} %bitcast.37), custom_call_target="tpu_custom_call" | custom-call | tf_op jit(solution)/shard_map/pallas_call | solution.py:256
  4.3 0.0 copy-start.8
  4.3 0.0 copy-start.9
  4.3 0.0 copy-start.10
  4.4 23.2 %all-to-all-start = ((bf16[256,8,768]{2,1,0:T(8,128)(2,1)}), bf16[256,8,768]{2,1,0:T(8,128)(2,1)}, u32[]{:S(2)}, u32[]{:S(2)}) async-start(bf16[256,8,768]{2,1,0:T(8,128)(2,1)} %shard_map.86), calls=%async_computation | async-start | bytes 6291456 | tf_op jit(solution)/shard_map/all_to_all | solution.py:325
  27.5 0.0 copy-start.13
  27.7 0.1 fusion.25
  27.7 2.5 collective-permute-start.3
  30.3 3.8 %collective-permute-start.4 = (bf16[1576,128]{1,0:T(8,128)(2,1)S(1)}, bf16[1576,128]{1,0:T(8,128)(2,1)S(1)}, u32[]{:S(2)}, u32[]{:S(2)}) collective-permute-start(bf16[1576,128]{1,0:T(8,128)(2,1)S(1)} %get-tuple-element.39), channel_id=1, source_target_pairs={{0,128},{64,192},{128,0},{192,64},{1,129},{65,193},{129,1},{193,65... | collective-permute-start | bytes 1210376 | tf_op jit(solution)/shard_map/ppermute | solution.py:288
  34.2 0.2 reshape.137
  34.4 0.1 copy.20
  34.5 0.1 reshape.146
  34.7 3.6 %collective-permute-start.1 = (bf16[104,128]{1,0:T(8,128)(2,1)S(1)}, bf16[104,128]{1,0:T(8,128)(2,1)S(1)}, u32[]{:S(2)}, u32[]{:S(2)}) collective-permute-start(bf16[104,128]{1,0:T(8,128)(2,1)S(1)} %get-tuple-element.48), channel_id=1, source_target_pairs={{0,128},{64,192},{128,0},{192,64},{1,129},{65,193},{129,1},{193,65... | collective-permute-start | bytes 79880 | tf_op jit(solution)/shard_map/ppermute | solution.py:288
  38.3 3.3 %collective-permute-start.2 = (bf16[104,128]{1,0:T(8,128)(2,1)S(1)}, bf16[104,128]{1,0:T(8,128)(2,1)S(1)}, u32[]{:S(2)}, u32[]{:S(2)}) collective-permute-start(bf16[104,128]{1,0:T(8,128)(2,1)S(1)} %get-tuple-element.47), channel_id=1, source_target_pairs={{0,192},{64,0},{128,64},{192,128},{1,193},{65,1},{129,65},{193,129... | collective-permute-start | bytes 79880 | tf_op jit(solution)/shard_map/ppermute | solution.py:288
  41.6 3.8 %collective-permute-start = (bf16[104,128]{1,0:T(8,128)(2,1)S(1)}, bf16[104,128]{1,0:T(8,128)(2,1)S(1)}, u32[]{:S(2)}, u32[]{:S(2)}) collective-permute-start(bf16[104,128]{1,0:T(8,128)(2,1)S(1)} %get-tuple-element.49), channel_id=1, source_target_pairs={{0,64},{64,128},{128,192},{192,0},{1,65},{65,129},{129,193},{193,1... | collective-permute-start | bytes 79880 | tf_op jit(solution)/shard_map/ppermute | solution.py:288
  45.5 0.1 add.177
  45.5 0.1 add.178
  45.6 5.0 %collective-permute-done.1 = bf16[104,128]{1,0:T(8,128)(2,1)S(1)} collective-permute-done((bf16[104,128]{1,0:T(8,128)(2,1)S(1)}, bf16[104,128]{1,0:T(8,128)(2,1)S(1)}, u32[]{:S(2)}, u32[]{:S(2)}) %collective-permute-start.1) | collective-permute-done | bytes 26656 | tf_op jit(solution)/shard_map/ppermute | solution.py:288
  50.6 11.8 %collective-permute-start.5 = (bf16[1576,128]{1,0:T(8,128)(2,1)S(1)}, bf16[1576,128]{1,0:T(8,128)(2,1)S(1)}, u32[]{:S(2)}, u32[]{:S(2)}) collective-permute-start(bf16[1576,128]{1,0:T(8,128)(2,1)S(1)} %get-tuple-element.39), channel_id=1, source_target_pairs={{0,192},{64,0},{128,64},{192,128},{1,193},{65,1},{129,65},{193,129... | collective-permute-start | bytes 1210376 | tf_op jit(solution)/shard_map/ppermute | solution.py:288
  62.5 0.1 reshape.140
  62.6 0.1 copy.24
  62.7 0.1 select_n.146
  62.8 8.2 %collective-permute-start.6 = (bf16[32,768]{1,0:T(8,128)(2,1)S(1)}, bf16[32,768]{1,0:T(8,128)(2,1)S(1)}, u32[]{:S(2)}, u32[]{:S(2)}) collective-permute-start(bf16[32,768]{1,0:T(8,128)(2,1)S(1)} %select_n.146), channel_id=1, source_target_pairs={{0,256},{256,0},{1,257},{257,1},{2,258},{258,2},{3,259},{259,3},{4... | collective-permute-start | bytes 147464 | tf_op jit(solution)/shard_map/ppermute | solution.py:342
  71.0 0.1 copy.23
  71.1 0.1 select_n.144.kept_ref
  71.2 0.5 broadcast.133
  71.7 0.7 fusion.26
  72.4 0.2 select_reduce_fusion
  72.6 0.1 reshape.139
  72.7 0.1 convert_element_type.53.routes_ref
  72.9 0.1 copy.22
  73.0 0.1 add.176
  73.1 1.2 fusion.1.chosen_ref
  74.3 2.3 collective-permute-done.5
  76.6 0.2 pad_maximum_fusion
  76.8 0.1 constant_dynamic-slice_fusion.4
  76.9 0.8 copy-done.7
  77.7 1.2 pad_maximum_fusion.1
  78.9 0.1 fusion.6
  79.0 0.1 slice.40.w_ref
  79.2 14.3 %collective-permute-done.6.crossed_ref = bf16[32,768]{1,0:T(8,128)(2,1)S(1)} collective-permute-done((bf16[32,768]{1,0:T(8,128)(2,1)S(1)}, bf16[32,768]{1,0:T(8,128)(2,1)S(1)}, u32[]{:S(2)}, u32[]{:S(2)}) %collective-permute-start.6) | collective-permute-done | bytes 49184 | tf_op jit(solution)/shard_map/ppermute | solution.py:342
  93.4 77.9 %all-to-all-done = bf16[256,8,768]{2,1,0:T(8,128)(2,1)} async-done(((bf16[256,8,768]{2,1,0:T(8,128)(2,1)}), bf16[256,8,768]{2,1,0:T(8,128)(2,1)}, u32[]{:S(2)}, u32[]{:S(2)}) %all-to-all-start) | async-done | bytes 3145760 | tf_op jit(solution)/shard_map/all_to_all | solution.py:325
  171.3 4.5 %shard_map.87 = (bf16[4,2,4,32,768]{4,3,2,1,0:T(8,128)(2,1)S(1)}, bf16[4,2,32,768]{3,2,1,0:T(8,128)(2,1)S(1)}, f32[4,32,128]{2,1,0:T(8,128)S(1)}, bf16[2,32,768]{2,1,0:T(8,128)(2,1)}) custom-call(s32[1]{0:T(128)} %bitcast.zh_ref, bf16[4,512,768]{2,1,0:T(8,128)(2,1)} %bitcast.4.rows_ref, bf16[4,256,512]{2,1,0:T(8,128)(2,1)} %fusion.1.chosen_ref, ...), custom_call_target="tpu_custom_call" | custom-call | tf_op jit(solution)/shard_map/pallas_call | solution.py:256
  175.8 0.8 copy-done.2
  176.6 7.6 %collective-permute-start.7 = (bf16[2,32,768]{2,1,0:T(8,128)(2,1)}, bf16[2,32,768]{2,1,0:T(8,128)(2,1)S(1)}, u32[]{:S(2)}, u32[]{:S(2)}) collective-permute-start(bf16[2,32,768]{2,1,0:T(8,128)(2,1)} %get-tuple-element.23), channel_id=1, source_target_pairs={{0,256},{1,257},{2,258},{3,259},{4,260},{5,261},{6,262},{7,263},{8... | collective-permute-start | bytes 294920 | tf_op jit(solution)/shard_map/ppermute | solution.py:380
  184.2 1.5 fusion.order_ref
  185.7 1.0 collective-permute-done.7.arrived_ref
  186.7 1.0 copy-done.3
  187.7 0.2 shard_map.88
  187.9 0.6 copy-done.5
  188.5 0.6 copy-done
  189.1 0.6 shard_map.89
  189.7 0.8 copy-done.1
  190.5 7.4 %all-to-all-start.1 = ((bf16[32,2,32,128]{3,2,1,0:T(8,128)(2,1)}), bf16[32,2,32,128]{3,2,1,0:T(8,128)(2,1)}, u32[]{:S(2)}, u32[]{:S(2)}) async-start(bf16[32,2,32,128]{3,2,1,0:T(8,128)(2,1)} %bitcast.35), calls=%async_computation.1 | async-start | bytes 1048576 | tf_op jit(solution)/shard_map/all_to_all | solution.py:398
  197.9 1.3 collective-permute-start.8
  199.2 18.0 %collective-permute-done.8.arrived_ref = bf16[2,32,768]{2,1,0:T(8,128)(2,1)S(1)} collective-permute-done((bf16[2,32,768]{2,1,0:T(8,128)(2,1)S(1)}, bf16[2,32,768]{2,1,0:T(8,128)(2,1)S(1)}, u32[]{:S(2)}, u32[]{:S(2)}) %collective-permute-start.8) | collective-permute-done | bytes 98336 | tf_op jit(solution)/shard_map/ppermute | solution.py:393
  217.2 1.0 copy-done.4
  218.2 2.3 shard_map.90
  220.5 14.1 %all_to_all.20.dlogits_ref = bf16[32,32,128]{2,1,0:T(8,128)(2,1)S(1)} all-to-all(bf16[32,32,128]{2,1,0:T(8,128)(2,1)S(1)} %bitcast.36), channel_id=1, replica_groups=mesh['zh'=2,'x'=4,'z'=8,'yc'=8] {'x','yc'}, dimensions={0} | all-to-all | bytes 524288 | tf_op jit(solution)/shard_map/all_to_all | solution.py:407
  234.7 2.0 shard_map.91
  236.7 12.2 %all-to-all-start.3 = ((bf16[8,24,128]{2,1,0:T(8,128)(2,1)}), bf16[8,24,128]{2,1,0:T(8,128)(2,1)S(1)}, u32[]{:S(2)}, u32[]{:S(2)}) async-start(bf16[8,24,128]{2,1,0:T(8,128)(2,1)} %shard_map.91), calls=%async_computation.3 | async-start | bytes 98304 | tf_op jit(solution)/shard_map/all_to_all | solution.py:409
  248.9 10.8 %all-to-all-done.3 = bf16[8,24,128]{2,1,0:T(8,128)(2,1)S(1)} async-done(((bf16[8,24,128]{2,1,0:T(8,128)(2,1)}), bf16[8,24,128]{2,1,0:T(8,128)(2,1)S(1)}, u32[]{:S(2)}, u32[]{:S(2)}) %all-to-all-start.3) | async-done | bytes 49184 | tf_op jit(solution)/shard_map/all_to_all | solution.py:409
  259.7 0.8 fusion.7
  260.5 0.6 fusion.24
  (51 shorter events, 0.5 us)
Async XLA Ops:
  0.6 3.7 %copy-start.14 = (f32[1,1536]{1,0:T(1,128)S(1)}, f32[1,1536]{1,0:T(1,128)}, u32[]{:S(2)}) copy-start(f32[1,1536]{1,0:T(1,128)} %param.12) | copy-start | bytes 18436
  4.3 23.3 %copy-start.8 = (bf16[1,1536,128]{2,1,0:T(8,128)(2,1)S(1)}, bf16[1,1536,128]{2,1,0:T(8,128)(2,1)}, u32[]{:S(2)}) copy-start(bf16[1,1536,128]{2,1,0:T(8,128)(2,1)} %param.11) | copy-start | bytes 1179652
  4.3 29.8 %copy-start.9 = (bf16[4,32,192]{2,1,0:T(8,128)(2,1)S(1)}, bf16[4,32,192]{2,1,0:T(8,128)(2,1)}, u32[]{:S(2)}) copy-start(bf16[4,32,192]{2,1,0:T(8,128)(2,1)} %param.8) | copy-start | bytes 147460
  4.3 29.8 %copy-start.10 = (bf16[4,32,192]{2,1,0:T(8,128)(2,1)S(1)}, bf16[4,32,192]{2,1,0:T(8,128)(2,1)}, u32[]{:S(2)}) copy-start(bf16[4,32,192]{2,1,0:T(8,128)(2,1)} %param.7) | copy-start | bytes 147460
  4.4 167.0 %all-to-all-start = ((bf16[256,8,768]{2,1,0:T(8,128)(2,1)}), bf16[256,8,768]{2,1,0:T(8,128)(2,1)}, u32[]{:S(2)}, u32[]{:S(2)}) async-start(bf16[256,8,768]{2,1,0:T(8,128)(2,1)} %shard_map.86), calls=%async_computation | async-start | bytes 6291456 | tf_op jit(solution)/shard_map/all_to_all | solution.py:325
  27.5 6.8 %copy-start.13 = (s32[1,4,32,4]{2,3,1,0:T(4,128)S(1)}, s32[1,4,32,4]{2,3,1,0:T(4,128)}, u32[]{:S(2)}) copy-start(s32[1,4,32,4]{2,3,1,0:T(4,128)} %param.10) | copy-start | bytes 6148
  27.7 46.6 %collective-permute-start.3 = (bf16[1576,128]{1,0:T(8,128)(2,1)S(1)}, bf16[1576,128]{1,0:T(8,128)(2,1)S(1)}, u32[]{:S(2)}, u32[]{:S(2)}) collective-permute-start(bf16[1576,128]{1,0:T(8,128)(2,1)S(1)} %get-tuple-element.39), channel_id=1, source_target_pairs={{0,64},{64,128},{128,192},{192,0},{1,65},{65,129},{129,193},{193,1... | collective-permute-start | bytes 1210376 | tf_op jit(solution)/shard_map/ppermute | solution.py:288
  30.3 44.0 %collective-permute-start.4 = (bf16[1576,128]{1,0:T(8,128)(2,1)S(1)}, bf16[1576,128]{1,0:T(8,128)(2,1)S(1)}, u32[]{:S(2)}, u32[]{:S(2)}) collective-permute-start(bf16[1576,128]{1,0:T(8,128)(2,1)S(1)} %get-tuple-element.39), channel_id=1, source_target_pairs={{0,128},{64,192},{128,0},{192,64},{1,129},{65,193},{129,1},{193,65... | collective-permute-start | bytes 1210376 | tf_op jit(solution)/shard_map/ppermute | solution.py:288
  34.7 15.9 %collective-permute-start.1 = (bf16[104,128]{1,0:T(8,128)(2,1)S(1)}, bf16[104,128]{1,0:T(8,128)(2,1)S(1)}, u32[]{:S(2)}, u32[]{:S(2)}) collective-permute-start(bf16[104,128]{1,0:T(8,128)(2,1)S(1)} %get-tuple-element.48), channel_id=1, source_target_pairs={{0,128},{64,192},{128,0},{192,64},{1,129},{65,193},{129,1},{193,65... | collective-permute-start | bytes 79880 | tf_op jit(solution)/shard_map/ppermute | solution.py:288
  38.3 24.1 %collective-permute-start.2 = (bf16[104,128]{1,0:T(8,128)(2,1)S(1)}, bf16[104,128]{1,0:T(8,128)(2,1)S(1)}, u32[]{:S(2)}, u32[]{:S(2)}) collective-permute-start(bf16[104,128]{1,0:T(8,128)(2,1)S(1)} %get-tuple-element.47), channel_id=1, source_target_pairs={{0,192},{64,0},{128,64},{192,128},{1,193},{65,1},{129,65},{193,129... | collective-permute-start | bytes 79880 | tf_op jit(solution)/shard_map/ppermute | solution.py:288
  41.6 20.8 %collective-permute-start = (bf16[104,128]{1,0:T(8,128)(2,1)S(1)}, bf16[104,128]{1,0:T(8,128)(2,1)S(1)}, u32[]{:S(2)}, u32[]{:S(2)}) collective-permute-start(bf16[104,128]{1,0:T(8,128)(2,1)S(1)} %get-tuple-element.49), channel_id=1, source_target_pairs={{0,64},{64,128},{128,192},{192,0},{1,65},{65,129},{129,193},{193,1... | collective-permute-start | bytes 79880 | tf_op jit(solution)/shard_map/ppermute | solution.py:288
  50.6 26.0 %collective-permute-start.5 = (bf16[1576,128]{1,0:T(8,128)(2,1)S(1)}, bf16[1576,128]{1,0:T(8,128)(2,1)S(1)}, u32[]{:S(2)}, u32[]{:S(2)}) collective-permute-start(bf16[1576,128]{1,0:T(8,128)(2,1)S(1)} %get-tuple-element.39), channel_id=1, source_target_pairs={{0,192},{64,0},{128,64},{192,128},{1,193},{65,1},{129,65},{193,129... | collective-permute-start | bytes 1210376 | tf_op jit(solution)/shard_map/ppermute | solution.py:288
  62.8 30.6 %collective-permute-start.6 = (bf16[32,768]{1,0:T(8,128)(2,1)S(1)}, bf16[32,768]{1,0:T(8,128)(2,1)S(1)}, u32[]{:S(2)}, u32[]{:S(2)}) collective-permute-start(bf16[32,768]{1,0:T(8,128)(2,1)S(1)} %select_n.146), channel_id=1, source_target_pairs={{0,256},{256,0},{1,257},{257,1},{2,258},{258,2},{3,259},{259,3},{4... | collective-permute-start | bytes 147464 | tf_op jit(solution)/shard_map/ppermute | solution.py:342
  76.9 0.8 copy-start.7
  171.3 14.3 %copy-start.12 = (f32[1536]{0:T(1024)S(1)}, f32[1536]{0:T(1024)}, u32[]{:S(2)}) copy-start(f32[1536]{0:T(1024)} %param.13) | copy-start | bytes 18436
  175.8 0.8 copy-start.2
  176.6 10.1 %collective-permute-start.7 = (bf16[2,32,768]{2,1,0:T(8,128)(2,1)}, bf16[2,32,768]{2,1,0:T(8,128)(2,1)S(1)}, u32[]{:S(2)}, u32[]{:S(2)}) collective-permute-start(bf16[2,32,768]{2,1,0:T(8,128)(2,1)} %get-tuple-element.23), channel_id=1, source_target_pairs={{0,256},{1,257},{2,258},{3,259},{4,260},{5,261},{6,262},{7,263},{8... | collective-permute-start | bytes 294920 | tf_op jit(solution)/shard_map/ppermute | solution.py:380
  186.7 1.0 copy-start.3
  187.7 1.4 copy-start
  187.8 0.6 copy-start.5
  189.1 8.7 %copy-start.6 = (bf16[2,32,768]{2,1,0:T(8,128)(2,1)S(1)}, bf16[2,32,768]{2,1,0:T(8,128)(2,1)}, u32[]{:S(2)}) copy-start(bf16[2,32,768]{2,1,0:T(8,128)(2,1)} %copy-done.5) | copy-start | bytes 294916
  189.7 0.8 copy-start.1
  190.5 26.7 %all-to-all-start.1 = ((bf16[32,2,32,128]{3,2,1,0:T(8,128)(2,1)}), bf16[32,2,32,128]{3,2,1,0:T(8,128)(2,1)}, u32[]{:S(2)}, u32[]{:S(2)}) async-start(bf16[32,2,32,128]{3,2,1,0:T(8,128)(2,1)} %bitcast.35), calls=%async_computation.1 | async-start | bytes 1048576 | tf_op jit(solution)/shard_map/all_to_all | solution.py:398
  197.9 19.3 %collective-permute-start.8 = (bf16[2,32,768]{2,1,0:T(8,128)(2,1)S(1)}, bf16[2,32,768]{2,1,0:T(8,128)(2,1)S(1)}, u32[]{:S(2)}, u32[]{:S(2)}) collective-permute-start(bf16[2,32,768]{2,1,0:T(8,128)(2,1)S(1)} %copy-done.6), channel_id=1, source_target_pairs={{256,0},{257,1},{258,2},{259,3},{260,4},{261,5},{262,6},{263,7},{2... | collective-permute-start | bytes 294920 | tf_op jit(solution)/shard_map/ppermute | solution.py:393
  217.2 1.0 copy-start.4
  236.7 23.0 %all-to-all-start.3 = ((bf16[8,24,128]{2,1,0:T(8,128)(2,1)}), bf16[8,24,128]{2,1,0:T(8,128)(2,1)S(1)}, u32[]{:S(2)}, u32[]{:S(2)}) async-start(bf16[8,24,128]{2,1,0:T(8,128)(2,1)} %shard_map.91), calls=%async_computation.3 | async-start | bytes 98304 | tf_op jit(solution)/shard_map/all_to_all | solution.py:409
  259.7 1.4 copy-start.11

commit v7 on v6

--- a/solution.py
+++ b/solution.py
@@ -129,7 +129,7 @@
 
 def first_kernel(
     zh_ref, rows_ref, chosen_ref, routes_ref, w_ref, gain_ref, kept_ref, crossed_ref,
-    picks_ref, states_ref, stats_ref, out_ref, table_ref, select_ref, sems,
+    picks_ref, kept_states_ref, stats_ref, out_ref, table_ref, select_ref, states_ref, sems, state_sems,
 ):
     layers = table_ref.shape[0]
     copies = [
@@ -152,18 +152,25 @@
     def _():
         refs = (picks_ref, routes_ref, w_ref, gain_ref)
         state = [kept_ref[...], crossed_ref[...]]
+        leaving = []
         for layer in range(layers):
             pick_layer(layer, copies, table_ref, select_ref, picks_ref)
             for h in range(HALVES):
                 states_ref[layer, h] = state[h]
+            leaving.append(
+                pltpu.make_async_copy(states_ref.at[layer], kept_states_ref.at[layer], state_sems.at[layer])
+            )
+            leaving[-1].start()
             state = forward_layer(layer, state, refs, stats_ref)
         for h in range(HALVES):
             out_ref[h] = state[h]
+        for copy in leaving:
+            copy.wait()
 
 
 def middle_kernel(
-    zh_ref, arrived_ref, kept_ref, crossed_ref, final_ref, picks_ref, routes_ref, w_ref, gain_ref, given_states_ref, given_stats_ref,
-    normed_ref, dlogits_ref, out_ref, states_ref, stats_ref,
+    zh_ref, given_states_ref, arrived_ref, kept_ref, crossed_ref, final_ref, picks_ref, routes_ref, w_ref, gain_ref,
+    given_stats_ref, normed_ref, dlogits_ref, out_ref, states_ref, stats_ref, sem,
 ):
     layers = picks_ref.shape[0]
     choices = routes_ref.shape[2]
@@ -171,10 +178,13 @@
 
     @pl.when(zh_ref[0] == 0)
     def _():
+        copy = pltpu.make_async_copy(given_states_ref, states_ref, sem)
+        copy.start()
+        copy.wait()
         for layer in range(layers):
             rscale = given_stats_ref[layer][:, choices : choices + 1]
             for h in range(HALVES):
-                floats = given_states_ref[layer, h].astype(F32)
+                floats = states_ref[layer, h].astype(F32)
                 normed_ref[layer, h] = (floats * rscale * gain_ref[layer, h : h + 1, :]).astype(BF16)
 
     @pl.when(zh_ref[0] != 0)
@@ -201,8 +211,8 @@
 
 
 def last_kernel(
-    zh_ref, arrived_ref, states_ref, stats_ref, picks_ref, routes_ref, w_ref, gain_ref, given_ref,
-    copies_ref, dlogits_ref,
+    zh_ref, kept_states_ref, arrived_ref, stats_ref, picks_ref, routes_ref, w_ref, gain_ref, given_ref,
+    copies_ref, dlogits_ref, states_ref, sems,
 ):
     layers = picks_ref.shape[0]
 
@@ -214,7 +224,14 @@
     def _():
         refs = (picks_ref, routes_ref, w_ref, gain_ref)
         back = [arrived_ref[h] for h in range(HALVES)]
+        arriving = [
+            pltpu.make_async_copy(kept_states_ref.at[layer], states_ref.at[layer], sems.at[layer])
+            for layer in range(layers)
+        ]
+        for copy in reversed(arriving):
+            copy.start()
         for layer in reversed(range(layers)):
+            arriving[layer].wait()
             state = [states_ref[layer, h] for h in range(HALVES)]
             back = backward_layer(layer, back, state, refs, stats_ref, dlogits_ref)
 
@@ -247,20 +264,23 @@
             out_ref[h * per_half + plane] = term[plane * rows : (plane + 1) * rows].astype(BF16)
 
 
-def call(kernel, outs, args, scratch=(), scalars=1, apart=0, apart_out=False, limit=16):
+def call(kernel, outs, args, scratch=(), scalars=1, apart=0, apart_out=(), limit=16):
     smem = [pl.BlockSpec(memory_space=pltpu.SMEM)] * scalars
     free = pl.BlockSpec(memory_space=pltpu.HBM)
     vmem = pl.BlockSpec(memory_space=pltpu.VMEM)
     far = [pltpu.with_memory_space_constraint(arg, pltpu.HBM) for arg in args[scalars : scalars + apart]]
     args = (*args[:scalars], *far, *args[scalars + apart :])
-    return pl.pallas_call(
+    single = not isinstance(outs, tuple)
+    outs = (outs,) if single else outs
+    results = pl.pallas_call(
         kernel,
-        out_shape=outs,
+        out_shape=[pltpu.HBM(out.shape, out.dtype) if index in apart_out else out for index, out in enumerate(outs)],
         in_specs=smem + [free] * apart + [vmem] * (len(args) - scalars - apart),
-        out_specs=jax.tree.map(lambda _: free if apart_out else vmem, outs),
+        out_specs=[free if index in apart_out else vmem for index in range(len(outs))],
         scratch_shapes=list(scratch),
         compiler_params=pltpu.CompilerParams(vmem_limit_bytes=limit * 2**20),
     )(*args)
+    return results[0] if single else results
 
 
 def slot_numbers(routes):
@@ -317,7 +337,7 @@
         ),
         scalars=0,
         apart=1,
-        apart_out=True,
+        apart_out=(0,),
     )
     rows, router_here, gain_here, routes_here, inputs, cotangent = lax.optimization_barrier(
         (rows, router_w[0], norm_gain[0], route_ids[0], inputs, cotangent)
@@ -373,9 +393,12 @@
         scratch=(
             pltpu.VMEM(table.shape, BF16),
             pltpu.VMEM(select.shape, BF16),
+            pltpu.VMEM((layers,) + rows_shape, BF16),
             pltpu.SemaphoreType.DMA((2, layers)),
+            pltpu.SemaphoreType.DMA((layers,)),
         ),
         apart=2,
+        apart_out=(1,),
     )
     arrived = lax.ppermute(sent, "zh", [(0, 1)])
     normed, dlogits, sent = call(
@@ -386,9 +409,14 @@
             shape(rows_shape, BF16),
         ),
         (
-            zh_word, arrived, kept, crossed, final_gain.reshape(HALVES, half), picks, routes, w_all, gain_all, states, stats,
-        ),
-        scratch=(pltpu.VMEM((layers,) + rows_shape, BF16), pltpu.VMEM((layers, tokens, 128), F32)),
+            zh_word, states, arrived, kept, crossed, final_gain.reshape(HALVES, half), picks, routes, w_all, gain_all, stats,
+        ),
+        scratch=(
+            pltpu.VMEM((layers,) + rows_shape, BF16),
+            pltpu.VMEM((layers, tokens, 128), F32),
+            pltpu.SemaphoreType.DMA,
+        ),
+        apart=1,
     )
     arrived = lax.ppermute(sent, "zh", [(1, 0)])
     normed = call(
@@ -400,8 +428,13 @@
     dlogits = call(
         last_kernel,
         shape((layers, groups, tokens, experts), BF16),
-        (zh_word, arrived, states, stats, picks, routes, w_all, gain_all, dlogits),
-        scratch=(pltpu.VMEM((layers, tokens, experts), BF16),),
+        (zh_word, states, arrived, stats, picks, routes, w_all, gain_all, dlogits),
+        scratch=(
+            pltpu.VMEM((layers, tokens, experts), BF16),
+            pltpu.VMEM((layers,) + rows_shape, BF16),
+            pltpu.SemaphoreType.DMA((layers,)),
+        ),
+        apart=1,
     )
     dlogits = dlogits.reshape(layers * groups, tokens, experts)
     dlogits = lax.all_to_all(dlogits, ("x",) + flat_axes, split_axis=0, concat_axis=0, tiled=True)

time: 264 us -> 262 us (level)
  local copies, waits for them, and re-layouts: 7.93 us -> 4.56 us
    unnamed x30 -> x24, local copies, waits for them, and re-layouts: 5.59 us -> 2.23 us
where the time goes in v7:
time: 262 us; the launch traced here: 259 us
  waiting for transfers between devices  129 us (49%)
  starting transfers between devices  88.2 us (34%)
  Pallas kernels  15.7 us (6%)
  blocking collectives  14.1 us (5%)
  other arithmetic  6.83 us (3%)
  local copies, waits for them, and re-layouts  4.56 us (2%)
    all_to_all x1, waiting for transfers between devices, compute(): lax.all_to_all(rows, ('x',) + expert_axes, split_axis=0, concat_axis=0, t...  77.9 us
    ppermute x6, starting transfers between devices, from_all(): lax.ppermute(block, axis, [(source, (source + shift) % count) for source...  28.7 us
    all_to_all x1, starting transfers between devices, compute(): lax.all_to_all(rows, ('x',) + expert_axes, split_axis=0, concat_axis=0, t...  23.2 us
    ppermute x1, waiting for transfers between devices, compute(): arrived = lax.ppermute(sent, 'zh', [(1, 0)])  17.6 us
    pallas_call x6, Pallas kernels, call(): pl.pallas_call(kernel, out_shape=[pltpu.HBM(out.shape, out.dtype) if inde...  15.7 us
    ppermute x1, waiting for transfers between devices, compute(): lax.ppermute(jnp.where(zh == 0, pair[1], pair[0]), 'zh', [(0, 1), (1, 0)])  14.3 us
    all_to_all x1, blocking collectives, compute(): lax.all_to_all(dlogits, ('x',) + flat_axes, split_axis=0, concat_axis=0,...  14.1 us
    all_to_all x1, starting transfers between devices, compute(): lax.all_to_all(term, plane_axis, split_axis=0, concat_axis=0, tiled=True)  12.2 us
  transfers between devices with their start and end apart: 12, of which 7 were waited for; matrix products, arithmetic and copies ran while one was open for 3% of the time, Pallas kernels for 0%

profile of v7, /device:TPU:6, one launch (start us, length us, event | category | flops | bytes accessed | tf_op | source)
XLA Modules:
  0.0 259.4 jit_solution(5413241794782444572)
XLA Ops:
  0.6 3.7 %shard_map.86 = bf16[256,8,768]{2,1,0:T(8,128)(2,1)} custom-call(bf16[4,2,64,2,1536]{4,3,2,1,0:T(2,128)(2,1)} %bitcast.37), custom_call_target="tpu_custom_call" | custom-call | tf_op jit(solution)/shard_map/pallas_call | solution.py:275
  4.3 0.0 copy-start.5
  4.4 0.0 copy-start.6
  4.4 0.0 copy-start.7
  4.4 23.2 %all-to-all-start = ((bf16[256,8,768]{2,1,0:T(8,128)(2,1)}), bf16[256,8,768]{2,1,0:T(8,128)(2,1)}, u32[]{:S(2)}, u32[]{:S(2)}) async-start(bf16[256,8,768]{2,1,0:T(8,128)(2,1)} %shard_map.86), calls=%async_computation | async-start | bytes 6291456 | tf_op jit(solution)/shard_map/all_to_all | solution.py:345
  27.5 0.0 copy-start.10
  27.7 0.1 fusion.25
  27.7 2.5 collective-permute-start.3
  30.3 3.8 %collective-permute-start.4 = (bf16[1576,128]{1,0:T(8,128)(2,1)S(1)}, bf16[1576,128]{1,0:T(8,128)(2,1)S(1)}, u32[]{:S(2)}, u32[]{:S(2)}) collective-permute-start(bf16[1576,128]{1,0:T(8,128)(2,1)S(1)} %get-tuple-element.39), channel_id=1, source_target_pairs={{0,128},{64,192},{128,0},{192,64},{1,129},{65,193},{129,1},{193,65... | collective-permute-start | bytes 1210376 | tf_op jit(solution)/shard_map/ppermute | solution.py:308
  34.2 0.2 reshape.137
  34.4 0.1 copy.20
  34.5 0.1 reshape.146
  34.7 3.6 %collective-permute-start.1 = (bf16[104,128]{1,0:T(8,128)(2,1)S(1)}, bf16[104,128]{1,0:T(8,128)(2,1)S(1)}, u32[]{:S(2)}, u32[]{:S(2)}) collective-permute-start(bf16[104,128]{1,0:T(8,128)(2,1)S(1)} %get-tuple-element.48), channel_id=1, source_target_pairs={{0,128},{64,192},{128,0},{192,64},{1,129},{65,193},{129,1},{193,65... | collective-permute-start | bytes 79880 | tf_op jit(solution)/shard_map/ppermute | solution.py:308
  38.3 3.3 %collective-permute-start.2 = (bf16[104,128]{1,0:T(8,128)(2,1)S(1)}, bf16[104,128]{1,0:T(8,128)(2,1)S(1)}, u32[]{:S(2)}, u32[]{:S(2)}) collective-permute-start(bf16[104,128]{1,0:T(8,128)(2,1)S(1)} %get-tuple-element.47), channel_id=1, source_target_pairs={{0,192},{64,0},{128,64},{192,128},{1,193},{65,1},{129,65},{193,129... | collective-permute-start | bytes 79880 | tf_op jit(solution)/shard_map/ppermute | solution.py:308
  41.6 3.8 %collective-permute-start = (bf16[104,128]{1,0:T(8,128)(2,1)S(1)}, bf16[104,128]{1,0:T(8,128)(2,1)S(1)}, u32[]{:S(2)}, u32[]{:S(2)}) collective-permute-start(bf16[104,128]{1,0:T(8,128)(2,1)S(1)} %get-tuple-element.49), channel_id=1, source_target_pairs={{0,64},{64,128},{128,192},{192,0},{1,65},{65,129},{129,193},{193,1... | collective-permute-start | bytes 79880 | tf_op jit(solution)/shard_map/ppermute | solution.py:308
  45.5 0.1 add.177
  45.6 0.1 add.178
  45.6 5.0 %collective-permute-done.1 = bf16[104,128]{1,0:T(8,128)(2,1)S(1)} collective-permute-done((bf16[104,128]{1,0:T(8,128)(2,1)S(1)}, bf16[104,128]{1,0:T(8,128)(2,1)S(1)}, u32[]{:S(2)}, u32[]{:S(2)}) %collective-permute-start.1) | collective-permute-done | bytes 26656 | tf_op jit(solution)/shard_map/ppermute | solution.py:308
  50.6 11.8 %collective-permute-start.5 = (bf16[1576,128]{1,0:T(8,128)(2,1)S(1)}, bf16[1576,128]{1,0:T(8,128)(2,1)S(1)}, u32[]{:S(2)}, u32[]{:S(2)}) collective-permute-start(bf16[1576,128]{1,0:T(8,128)(2,1)S(1)} %get-tuple-element.39), channel_id=1, source_target_pairs={{0,192},{64,0},{128,64},{192,128},{1,193},{65,1},{129,65},{193,129... | collective-permute-start | bytes 1210376 | tf_op jit(solution)/shard_map/ppermute | solution.py:308
  62.4 0.0 collective-permute-done.2
  62.4 0.0 collective-permute-done
  62.5 0.1 reshape.140
  62.6 0.1 copy.24
  62.7 0.1 select_n.146
  62.8 8.2 %collective-permute-start.6 = (bf16[32,768]{1,0:T(8,128)(2,1)S(1)}, bf16[32,768]{1,0:T(8,128)(2,1)S(1)}, u32[]{:S(2)}, u32[]{:S(2)}) collective-permute-start(bf16[32,768]{1,0:T(8,128)(2,1)S(1)} %select_n.146), channel_id=1, source_target_pairs={{0,256},{256,0},{1,257},{257,1},{2,258},{258,2},{3,259},{259,3},{4... | collective-permute-start | bytes 147464 | tf_op jit(solution)/shard_map/ppermute | solution.py:362
  71.0 0.1 copy.23
  71.1 0.1 select_n.144.kept_ref
  71.2 0.5 broadcast.133
  71.7 0.7 fusion.26
  72.4 0.2 select_reduce_fusion
  72.6 0.1 reshape.139
  72.8 0.1 convert_element_type.53.routes_ref
  72.9 0.1 copy.22
  73.0 0.1 add.176
  73.1 1.2 fusion.1.chosen_ref
  74.3 2.3 collective-permute-done.5
  76.6 0.2 pad_maximum_fusion
  76.8 0.1 constant_dynamic-slice_fusion.4
  76.9 0.8 copy-done.4
  77.7 1.2 pad_maximum_fusion.1
  78.9 0.1 fusion.6
  79.1 0.1 slice.40.w_ref
  79.2 14.3 %collective-permute-done.6.crossed_ref = bf16[32,768]{1,0:T(8,128)(2,1)S(1)} collective-permute-done((bf16[32,768]{1,0:T(8,128)(2,1)S(1)}, bf16[32,768]{1,0:T(8,128)(2,1)S(1)}, u32[]{:S(2)}, u32[]{:S(2)}) %collective-permute-start.6) | collective-permute-done | bytes 49184 | tf_op jit(solution)/shard_map/ppermute | solution.py:362
  93.4 77.9 %all-to-all-done = bf16[256,8,768]{2,1,0:T(8,128)(2,1)} async-done(((bf16[256,8,768]{2,1,0:T(8,128)(2,1)}), bf16[256,8,768]{2,1,0:T(8,128)(2,1)}, u32[]{:S(2)}, u32[]{:S(2)}) %all-to-all-start) | async-done | bytes 3145760 | tf_op jit(solution)/shard_map/all_to_all | solution.py:345
  171.3 4.9 %shard_map.87 = (bf16[4,2,4,32,768]{4,3,2,1,0:T(8,128)(2,1)S(1)}, bf16[4,2,32,768]{3,2,1,0:T(8,128)(2,1)}, f32[4,32,128]{2,1,0:T(8,128)S(1)}, bf16[2,32,768]{2,1,0:T(8,128)(2,1)}) custom-call(s32[1]{0:T(128)} %bitcast.zh_ref, bf16[4,512,768]{2,1,0:T(8,128)(2,1)} %bitcast.4.rows_ref, bf16[4,256,512]{2,1,0:T(8,128)(2,1)} %fusion.1.chosen_ref, ...), custom_call_target="tpu_custom_call" | custom-call | tf_op jit(solution)/shard_map/pallas_call | solution.py:275
  176.3 7.2 %collective-permute-start.7 = (bf16[2,32,768]{2,1,0:T(8,128)(2,1)}, bf16[2,32,768]{2,1,0:T(8,128)(2,1)S(1)}, u32[]{:S(2)}, u32[]{:S(2)}) collective-permute-start(bf16[2,32,768]{2,1,0:T(8,128)(2,1)} %get-tuple-element.24), channel_id=1, source_target_pairs={{0,256},{1,257},{2,258},{3,259},{4,260},{5,261},{6,262},{7,263},{8... | collective-permute-start | bytes 294920 | tf_op jit(solution)/shard_map/ppermute | solution.py:403
  183.5 1.5 fusion.order_ref
  185.0 1.0 collective-permute-done.7.arrived_ref
  186.0 1.3 shard_map.88
  187.3 0.6 copy-done.2
  187.9 0.6 shard_map.89
  188.5 0.8 copy-done.1
  189.3 7.4 %all-to-all-start.1 = ((bf16[32,2,32,128]{3,2,1,0:T(8,128)(2,1)}), bf16[32,2,32,128]{3,2,1,0:T(8,128)(2,1)}, u32[]{:S(2)}, u32[]{:S(2)}) async-start(bf16[32,2,32,128]{3,2,1,0:T(8,128)(2,1)} %bitcast.35), calls=%async_computation.1 | async-start | bytes 1048576 | tf_op jit(solution)/shard_map/all_to_all | solution.py:426
  196.7 1.3 collective-permute-start.8
  198.0 17.6 %collective-permute-done.8.arrived_ref = bf16[2,32,768]{2,1,0:T(8,128)(2,1)S(1)} collective-permute-done((bf16[2,32,768]{2,1,0:T(8,128)(2,1)S(1)}, bf16[2,32,768]{2,1,0:T(8,128)(2,1)S(1)}, u32[]{:S(2)}, u32[]{:S(2)}) %collective-permute-start.8) | collective-permute-done | bytes 98336 | tf_op jit(solution)/shard_map/ppermute | solution.py:421
  215.6 0.0 all-to-all-done.1.normed_ref
  215.6 3.3 %shard_map.90 = bf16[4,8,32,128]{3,2,1,0:T(8,128)(2,1)S(1)} custom-call(s32[1]{0:T(128)} %bitcast.zh_ref, bf16[4,2,32,768]{3,2,1,0:T(8,128)(2,1)} %get-tuple-element.23.given_states_ref.kept_states_ref, bf16[2,32,768]{2,1,0:T(8,128)(2,1)S(1)} %collective-permute-done.8.arrived_ref, f32[4,32,128]{2,1,0:T(8,128)S(1)} %get-tuple-element.26.given_stats_ref.stats_ref, ...), custom_call_target="tpu_custom_call" | custom-call | tf_op jit(solution)/shard_map/pallas_call | solution.py:275
  218.8 14.1 %all_to_all.20.dlogits_ref = bf16[32,32,128]{2,1,0:T(8,128)(2,1)S(1)} all-to-all(bf16[32,32,128]{2,1,0:T(8,128)(2,1)S(1)} %bitcast.36), channel_id=1, replica_groups=mesh['zh'=2,'x'=4,'z'=8,'yc'=8] {'x','yc'}, dimensions={0} | all-to-all | bytes 524288 | tf_op jit(solution)/shard_map/all_to_all | solution.py:440
  233.0 2.0 shard_map.91
  235.0 12.2 %all-to-all-start.3 = ((bf16[8,24,128]{2,1,0:T(8,128)(2,1)}), bf16[8,24,128]{2,1,0:T(8,128)(2,1)S(1)}, u32[]{:S(2)}, u32[]{:S(2)}) async-start(bf16[8,24,128]{2,1,0:T(8,128)(2,1)} %shard_map.91), calls=%async_computation.3 | async-start | bytes 98304 | tf_op jit(solution)/shard_map/all_to_all | solution.py:442
  247.2 10.8 %all-to-all-done.3 = bf16[8,24,128]{2,1,0:T(8,128)(2,1)S(1)} async-done(((bf16[8,24,128]{2,1,0:T(8,128)(2,1)}), bf16[8,24,128]{2,1,0:T(8,128)(2,1)S(1)}, u32[]{:S(2)}, u32[]{:S(2)}) %all-to-all-start.3) | async-done | bytes 49184 | tf_op jit(solution)/shard_map/all_to_all | solution.py:442
  258.0 0.0 copy-start.8
  258.0 0.8 fusion.7
  258.8 0.6 fusion.24
  (45 shorter events, 0.4 us)
Async XLA Ops:
  0.6 3.7 %copy-start.11 = (f32[1,1536]{1,0:T(1,128)S(1)}, f32[1,1536]{1,0:T(1,128)}, u32[]{:S(2)}) copy-start(f32[1,1536]{1,0:T(1,128)} %param.12) | copy-start | bytes 18436
  4.3 23.3 %copy-start.5 = (bf16[1,1536,128]{2,1,0:T(8,128)(2,1)S(1)}, bf16[1,1536,128]{2,1,0:T(8,128)(2,1)}, u32[]{:S(2)}) copy-start(bf16[1,1536,128]{2,1,0:T(8,128)(2,1)} %param.11) | copy-start | bytes 1179652
  4.4 29.8 %copy-start.6 = (bf16[4,32,192]{2,1,0:T(8,128)(2,1)S(1)}, bf16[4,32,192]{2,1,0:T(8,128)(2,1)}, u32[]{:S(2)}) copy-start(bf16[4,32,192]{2,1,0:T(8,128)(2,1)} %param.8) | copy-start | bytes 147460
  4.4 29.8 %copy-start.7 = (bf16[4,32,192]{2,1,0:T(8,128)(2,1)S(1)}, bf16[4,32,192]{2,1,0:T(8,128)(2,1)}, u32[]{:S(2)}) copy-start(bf16[4,32,192]{2,1,0:T(8,128)(2,1)} %param.7) | copy-start | bytes 147460
  4.4 167.0 %all-to-all-start = ((bf16[256,8,768]{2,1,0:T(8,128)(2,1)}), bf16[256,8,768]{2,1,0:T(8,128)(2,1)}, u32[]{:S(2)}, u32[]{:S(2)}) async-start(bf16[256,8,768]{2,1,0:T(8,128)(2,1)} %shard_map.86), calls=%async_computation | async-start | bytes 6291456 | tf_op jit(solution)/shard_map/all_to_all | solution.py:345
  27.5 6.8 %copy-start.10 = (s32[1,4,32,4]{2,3,1,0:T(4,128)S(1)}, s32[1,4,32,4]{2,3,1,0:T(4,128)}, u32[]{:S(2)}) copy-start(s32[1,4,32,4]{2,3,1,0:T(4,128)} %param.10) | copy-start | bytes 6148
  27.7 46.6 %collective-permute-start.3 = (bf16[1576,128]{1,0:T(8,128)(2,1)S(1)}, bf16[1576,128]{1,0:T(8,128)(2,1)S(1)}, u32[]{:S(2)}, u32[]{:S(2)}) collective-permute-start(bf16[1576,128]{1,0:T(8,128)(2,1)S(1)} %get-tuple-element.39), channel_id=1, source_target_pairs={{0,64},{64,128},{128,192},{192,0},{1,65},{65,129},{129,193},{193,1... | collective-permute-start | bytes 1210376 | tf_op jit(solution)/shard_map/ppermute | solution.py:308
  30.3 44.0 %collective-permute-start.4 = (bf16[1576,128]{1,0:T(8,128)(2,1)S(1)}, bf16[1576,128]{1,0:T(8,128)(2,1)S(1)}, u32[]{:S(2)}, u32[]{:S(2)}) collective-permute-start(bf16[1576,128]{1,0:T(8,128)(2,1)S(1)} %get-tuple-element.39), channel_id=1, source_target_pairs={{0,128},{64,192},{128,0},{192,64},{1,129},{65,193},{129,1},{193,65... | collective-permute-start | bytes 1210376 | tf_op jit(solution)/shard_map/ppermute | solution.py:308
  34.7 15.9 %collective-permute-start.1 = (bf16[104,128]{1,0:T(8,128)(2,1)S(1)}, bf16[104,128]{1,0:T(8,128)(2,1)S(1)}, u32[]{:S(2)}, u32[]{:S(2)}) collective-permute-start(bf16[104,128]{1,0:T(8,128)(2,1)S(1)} %get-tuple-element.48), channel_id=1, source_target_pairs={{0,128},{64,192},{128,0},{192,64},{1,129},{65,193},{129,1},{193,65... | collective-permute-start | bytes 79880 | tf_op jit(solution)/shard_map/ppermute | solution.py:308
  38.3 24.1 %collective-permute-start.2 = (bf16[104,128]{1,0:T(8,128)(2,1)S(1)}, bf16[104,128]{1,0:T(8,128)(2,1)S(1)}, u32[]{:S(2)}, u32[]{:S(2)}) collective-permute-start(bf16[104,128]{1,0:T(8,128)(2,1)S(1)} %get-tuple-element.47), channel_id=1, source_target_pairs={{0,192},{64,0},{128,64},{192,128},{1,193},{65,1},{129,65},{193,129... | collective-permute-start | bytes 79880 | tf_op jit(solution)/shard_map/ppermute | solution.py:308
  41.6 20.8 %collective-permute-start = (bf16[104,128]{1,0:T(8,128)(2,1)S(1)}, bf16[104,128]{1,0:T(8,128)(2,1)S(1)}, u32[]{:S(2)}, u32[]{:S(2)}) collective-permute-start(bf16[104,128]{1,0:T(8,128)(2,1)S(1)} %get-tuple-element.49), channel_id=1, source_target_pairs={{0,64},{64,128},{128,192},{192,0},{1,65},{65,129},{129,193},{193,1... | collective-permute-start | bytes 79880 | tf_op jit(solution)/shard_map/ppermute | solution.py:308
  50.6 26.0 %collective-permute-start.5 = (bf16[1576,128]{1,0:T(8,128)(2,1)S(1)}, bf16[1576,128]{1,0:T(8,128)(2,1)S(1)}, u32[]{:S(2)}, u32[]{:S(2)}) collective-permute-start(bf16[1576,128]{1,0:T(8,128)(2,1)S(1)} %get-tuple-element.39), channel_id=1, source_target_pairs={{0,192},{64,0},{128,64},{192,128},{1,193},{65,1},{129,65},{193,129... | collective-permute-start | bytes 1210376 | tf_op jit(solution)/shard_map/ppermute | solution.py:308
  62.8 30.6 %collective-permute-start.6 = (bf16[32,768]{1,0:T(8,128)(2,1)S(1)}, bf16[32,768]{1,0:T(8,128)(2,1)S(1)}, u32[]{:S(2)}, u32[]{:S(2)}) collective-permute-start(bf16[32,768]{1,0:T(8,128)(2,1)S(1)} %select_n.146), channel_id=1, source_target_pairs={{0,256},{256,0},{1,257},{257,1},{2,258},{258,2},{3,259},{259,3},{4... | collective-permute-start | bytes 147464 | tf_op jit(solution)/shard_map/ppermute | solution.py:362
  76.9 0.8 copy-start.4
  171.3 13.6 %copy-start.9 = (f32[1536]{0:T(1024)S(1)}, f32[1536]{0:T(1024)}, u32[]{:S(2)}) copy-start(f32[1536]{0:T(1024)} %param.13) | copy-start | bytes 18436
  176.3 9.7 %collective-permute-start.7 = (bf16[2,32,768]{2,1,0:T(8,128)(2,1)}, bf16[2,32,768]{2,1,0:T(8,128)(2,1)S(1)}, u32[]{:S(2)}, u32[]{:S(2)}) collective-permute-start(bf16[2,32,768]{2,1,0:T(8,128)(2,1)} %get-tuple-element.24), channel_id=1, source_target_pairs={{0,256},{1,257},{2,258},{3,259},{4,260},{5,261},{6,262},{7,263},{8... | collective-permute-start | bytes 294920 | tf_op jit(solution)/shard_map/ppermute | solution.py:403
  186.0 1.9 copy-start
  187.2 0.6 copy-start.2
  187.9 8.8 %copy-start.3 = (bf16[2,32,768]{2,1,0:T(8,128)(2,1)S(1)}, bf16[2,32,768]{2,1,0:T(8,128)(2,1)}, u32[]{:S(2)}) copy-start(bf16[2,32,768]{2,1,0:T(8,128)(2,1)} %copy-done.2) | copy-start | bytes 294916
  188.5 0.8 copy-start.1
  189.3 26.3 %all-to-all-start.1 = ((bf16[32,2,32,128]{3,2,1,0:T(8,128)(2,1)}), bf16[32,2,32,128]{3,2,1,0:T(8,128)(2,1)}, u32[]{:S(2)}, u32[]{:S(2)}) async-start(bf16[32,2,32,128]{3,2,1,0:T(8,128)(2,1)} %bitcast.35), calls=%async_computation.1 | async-start | bytes 1048576 | tf_op jit(solution)/shard_map/all_to_all | solution.py:426
  196.7 18.9 %collective-permute-start.8 = (bf16[2,32,768]{2,1,0:T(8,128)(2,1)S(1)}, bf16[2,32,768]{2,1,0:T(8,128)(2,1)S(1)}, u32[]{:S(2)}, u32[]{:S(2)}) collective-permute-start(bf16[2,32,768]{2,1,0:T(8,128)(2,1)S(1)} %copy-done.3), channel_id=1, source_target_pairs={{256,0},{257,1},{258,2},{259,3},{260,4},{261,5},{262,6},{263,7},{2... | collective-permute-start | bytes 294920 | tf_op jit(solution)/shard_map/ppermute | solution.py:421
  235.0 23.0 %all-to-all-start.3 = ((bf16[8,24,128]{2,1,0:T(8,128)(2,1)}), bf16[8,24,128]{2,1,0:T(8,128)(2,1)S(1)}, u32[]{:S(2)}, u32[]{:S(2)}) async-start(bf16[8,24,128]{2,1,0:T(8,128)(2,1)} %shard_map.91), calls=%async_computation.3 | async-start | bytes 98304 | tf_op jit(solution)/shard_map/all_to_all | solution.py:442
  258.0 1.4 copy-start.8
